TPU v7x, 32 devices: a whole 2x2x4 slice. The times are simulated.
32 devices in a mesh: dp: 16 (over z, y, x), seq: 2 (over core).
Axes of the slice: x: 2, y: 2, z: 4, core: 2. Of those that a mesh axis runs over, the one named last changes fastest.
Arguments:
- tokens: bfloat16 [16, 1024, 768], P('dp', 'seq'), may hold values from -6 to 6
- cotangent: bfloat16 [16, 1024, 768], P('dp', 'seq'), may hold values from -6 to 6
- page_boxes: int32 [4, 16, 1024], P(None, 'dp', 'seq'), may hold values from 0 to 1000
- page_lengths: int32 [16, 4], P('dp'), may hold values from 1 to 512, 1024 in all within a row
- padding: int32 [16, 1024], P('dp', 'seq'), may hold values 0 or 1
- buckets: int32 [16, 1024, 1024], P('dp', 'seq'), may hold values from 0 to 31
- master: float32 [7186560], P(('dp', 'seq')), may hold values from -4 to 4
- first_moment: float32 [7186560], P(('dp', 'seq')), may hold values from -1.5 to 1.5
- second_moment: float32 [7186560], P(('dp', 'seq')), may hold values from 0.005 to 0.1
Outputs:
- activations: bfloat16 [16, 1024, 768], P('dp', 'seq')
- input_grad: float32 [16, 1024, 768], P('dp', 'seq')
- param_step: float32 [7186560], P(('dp', 'seq'))
- new_first: float32 [7186560], P(('dp', 'seq'))
- new_second: float32 [7186560], P(('dp', 'seq'))
Inputs may be any that keep to these rules, and one draw needn't show every extreme that they name: `page_lengths`: each block's 4 page lengths sum to 1024; the longest page of each block has 512 tokens.
All inputs are finite; a program needn't handle non-finite values. No bound on the sum of `padding` on one device may be relied on, other than what follows from the above.
Results may differ from a plain program's by a relative error of at most 0.015.
The roundings to bfloat16 on the way count: a program that leaves them out, or rounds other values in their place, can miss the bound.
Values may be sent and summed in bfloat16 or wider, within the bound.
A program may use at most 192 MiB of HBM per device.

v0:
```python
from types import SimpleNamespace
from typing import Any, NamedTuple

import functools
import jax
import jax.numpy as jnp
from jax import lax
from jax.experimental import pallas as pl
from jax.experimental.pallas import tpu as pltpu
from jax.sharding import PartitionSpec as P

D = 768
H = 12
HD = 64
FF = 3072
BUCKETS = 32
FREQ = 16
LF = 128
LAYERS = 1
BLOCK = 1024
STEP = 10
ENTRY = 99456
LAYER_PARAMS = 7087104
RAW = 7186560


beta_one = 0.8
beta_two = 0.98
adam_eps = 1e-06
learn_rate = 0.0006
layer_decay = 0.8
weight_decay = 0.1
norm_eps = 1e-05
masked_score = -1000000000.0


class Params(NamedTuple):
    layout_weight: Any
    layout_bias: Any
    bias_table: Any
    query_weight: Any
    query_bias: Any
    key_weight: Any
    value_weight: Any
    value_bias: Any
    output_weight: Any
    output_bias: Any
    first_gain: Any
    first_shift: Any
    up_weight: Any
    up_bias: Any
    down_weight: Any
    down_bias: Any
    second_gain: Any
    second_shift: Any


SHAPES = (
    (LF, D), (D,), (BUCKETS, H),
    (D, D), (D,), (D, D), (D, D), (D,), (D, D), (D,), (D,), (D,),
    (D, FF), (FF,), (FF, D), (D,), (D,), (D,),
)


def unpack(flat_params):
    pieces, offset = [], 0
    for shape in SHAPES:
        amount = shape[0] * (shape[1] if len(shape) > 1 else 1)
        pieces.append(flat_params[offset : offset + amount].reshape(shape))
        offset = offset + amount
    return Params(*pieces)


def as_float(piece):
    return piece.astype(jnp.float32)


def matmul_low(left, right):
    return jnp.dot(left, right, preferred_element_type=jnp.float32)


def layer_norm(values, gain, shift):
    center = values - jnp.mean(values, axis=-1, keepdims=True)
    spread = jnp.mean(center * center, axis=-1, keepdims=True)
    return center * lax.rsqrt(spread + norm_eps) * gain + shift


def gelu_exact(values):
    return jax.nn.gelu(values, approximate=False)


def layout_features(page_boxes):
    rates_sin = jnp.power(10000.0, -jnp.arange(FREQ, dtype=jnp.float32) / FREQ)
    angles = page_boxes.astype(jnp.float32)[:, :, None] * rates_sin
    stacked = jnp.stack([jnp.sin(angles), jnp.cos(angles)], axis=1)
    return jnp.transpose(stacked, (2, 0, 1, 3)).reshape(page_boxes.shape[1], LF)


def attention_scores(query_low, key_all, score_bias, allowed, blocks_here, rows):
    query_heads = query_low.reshape(blocks_here, rows, H, HD)
    key_heads = key_all.reshape(blocks_here, BLOCK, H, HD)
    products = (
        jnp.einsum("cqhd,ckhd->chqk", query_heads, key_heads, preferred_element_type=jnp.float32)
        + score_bias
    )
    return jnp.where(allowed, products, masked_score)


def adam_update(master, first_moment, second_moment, gradient, global_index):
    exponent = jnp.where(
        global_index < ENTRY,
        LAYERS,
        jnp.maximum(LAYERS - 1 - (global_index - ENTRY) // LAYER_PARAMS, 0),
    )
    rate = jnp.where(
        global_index < RAW, learn_rate * jnp.power(layer_decay, exponent.astype(jnp.float32)), 0.0
    )
    moment_one = beta_one * first_moment + (1.0 - beta_one) * gradient
    moment_two = beta_two * second_moment + (1.0 - beta_two) * gradient * gradient
    fixed_one = moment_one / (1.0 - beta_one**STEP)
    fixed_two = moment_two / (1.0 - beta_two**STEP)
    param_step = -rate * (fixed_one / (jnp.sqrt(fixed_two) + adam_eps) + weight_decay * master)
    return (param_step, moment_one, moment_two)


def running_sum(lengths):
    total, sums = lengths[:, :1], [lengths[:, :1]]
    for i in range(1, lengths.shape[1]):
        total = total + lengths[:, i : i + 1]
        sums.append(total)
    return jnp.concatenate(sums, axis=1)


MESH = pl.DeviceIdType.MESH
SHARD = 224580
ROWS = 1760
TAIL, HEAD = 160, 176
WIN = 2176
SLOTS = 37
CHIP = 74
PARTS = ((0, 19), (19, 18))


def place():
    k = lax.axis_index("dp")
    return k, lax.axis_index("seq"), k // 4, (k // 2) % 2, k % 2


def shard_start(d):
    return d * 1754 + (d * 68) // 128, (d * 68) % 128


def early_vectors(k):
    return (k == 0) | (k == 4) | (k == 5)


def vector_row(k, other):
    at = other
    for chip, row in ((0, 768), (1, 5385), (4, 14607), (5, 19221), (10, 37671), (15, 56127)):
        at = jnp.where(k == chip, row, at)
    return at


def tile_start(w):
    at = w * 48
    for first, shift in ((16, 777 - 16 * 48), (112, 5391 - 112 * 48), (208, 9999 - 208 * 48), (304, 14613 - 304 * 48), (784, 37695 - 784 * 48)):
        at = jnp.where(w >= first, w * 48 + shift, at)
    wide = (w >= 400) & (w < 784)
    v = w - 400
    at = jnp.where(wide, 19239 + (v // 4) * 192 + (v % 4) * 6, at)
    return at, wide


def neighbours(k, c, z, y, x):
    t = k >= 0
    return [
        (t, (k, 1 - c)),
        (t, (z * 4 + y * 2 + 1 - x, c)),
        (t, (z * 4 + (1 - y) * 2 + x, c)),
        (z < 3, (jnp.minimum(k + 4, 15), c)),
        (z > 0, (jnp.maximum(k - 4, 0), c)),
        ((c == 1) & (k < 15), (jnp.minimum(k + 1, 15), 0)),
        ((c == 0) & (k > 0), (jnp.maximum(k - 1, 0), 1)),
    ]


def greet(k, c, z, y, x):
    bar = pltpu.get_barrier_semaphore()
    for cond, dev in neighbours(k, c, z, y, x):
        @pl.when(cond)
        def _():
            pl.semaphore_signal(bar, inc=1, device_id=dev, device_id_type=MESH)
    peers = 3
    for cond, _ in neighbours(k, c, z, y, x)[3:]:
        peers = peers + jnp.where(cond, 1, 0)
    pl.semaphore_wait(bar, peers)


def rcopy(src, dst, ssem, rsem, dev):
    return pltpu.make_async_remote_copy(src_ref=src, dst_ref=dst, send_sem=ssem, recv_sem=rsem, device_id=dev, device_id_type=MESH)


def gather_kernel(x_ref, g_ref, xv, tail, head, win, chunk, lsem, hsend, hrecv, own,
                  zs, zr, xas, xar, xbs, xbr, yas, yar, ybs, ybr, cs, cr):
    k, c, z, y, x = place()
    d = 2 * k + c
    greet(k, c, z, y, x)
    load = pltpu.make_async_copy(x_ref, xv, lsem)
    load.start()
    prev = (jnp.where(c == 1, k, jnp.maximum(k - 1, 0)), 1 - c)
    nxt = (jnp.where(c == 0, k, jnp.minimum(k + 1, 15)), 1 - c)
    to_next = rcopy(x_ref.at[pl.ds(ROWS - TAIL, TAIL)], tail, hsend.at[0], hrecv.at[0], nxt)
    to_prev = rcopy(x_ref.at[pl.ds(0, HEAD)], head, hsend.at[1], hrecv.at[1], prev)

    @pl.when(d < 31)
    def _():
        to_next.start()

    @pl.when(d > 0)
    def _():
        to_prev.start()

    win[...] = jnp.zeros_like(win)
    lanes = lax.broadcasted_iota(jnp.int32, (80, 128), 1)
    q, sh = shard_start(d)
    load.wait()

    @pl.loop(0, ROWS // 80)
    def _(i):
        r = pl.multiple_of(i * 80, 8)
        rolled = pltpu.roll(xv[pl.ds(r, 80), :], sh, 1)
        win[pl.ds(160 + r, 80), :] += jnp.where(lanes >= sh, rolled, 0.0)
        win[pl.ds(161 + r, 80), :] += jnp.where(lanes < sh, rolled, 0.0)

    @pl.when(d > 0)
    def _():
        to_next.wait_recv()
        qp, shp = shard_start(d - 1)
        lanes = lax.broadcasted_iota(jnp.int32, (TAIL, 128), 1)
        rolled = pltpu.roll(tail[...], shp, 1)
        at = 1760 - (q - qp)
        win[pl.ds(at, TAIL), :] += jnp.where(lanes >= shp, rolled, 0.0)
        win[pl.ds(at + 1, TAIL), :] += jnp.where(lanes < shp, rolled, 0.0)

    @pl.when(d < 31)
    def _():
        to_prev.wait_recv()
        qn, shn = shard_start(d + 1)
        lanes = lax.broadcasted_iota(jnp.int32, (HEAD, 128), 1)
        rolled = pltpu.roll(head[...], shn, 1)
        at = 160 + (qn - q)
        win[pl.ds(at, HEAD), :] += jnp.where(lanes >= shn, rolled, 0.0)
        win[pl.ds(at + 1, HEAD), :] += jnp.where(lanes < shn, rolled, 0.0)

    early = early_vectors(k)
    nw0 = jnp.where(early, 36, 37)
    vecs = early == (c == 0)
    first = jnp.where(c == 0, 73 * k, 73 * k + nw0)
    base = q - 160

    @pl.loop(0, SLOTS)
    def _(t):
        at, wide = tile_start(first + t)
        is_vec = vecs & (t == 36)
        at = jnp.where(is_vec, vector_row(k, q), at) - base
        wide = wide & jnp.logical_not(is_vec)

        @pl.when(wide)
        def _():
            parts = [win[pl.ds(at + j, 8, stride=24), :] for j in range(6)]
            chunk[t] = jnp.concatenate(parts, axis=1).astype(jnp.bfloat16)

        @pl.when(jnp.logical_not(wide))
        def _():
            parts = [win[pl.ds(at + j, 8, stride=6), :] for j in range(6)]
            chunk[t] = jnp.concatenate(parts, axis=1).astype(jnp.bfloat16)

    @pl.when(d < 31)
    def _():
        to_next.wait_send()

    @pl.when(d > 0)
    def _():
        to_prev.wait_send()

    xdev, ydev, cdev = (z * 4 + y * 2 + 1 - x, c), (z * 4 + (1 - y) * 2 + x, c), (k, 1 - c)
    zdev = {1: (jnp.minimum(k + 4, 15), c), -1: (jnp.maximum(k - 4, 0), c)}

    def gsl(chip, p):
        off, n = PARTS[p]
        return g_ref.at[chip, pl.ds(37 * c + off, n)]

    def src(chip, p, mine=False):
        off, n = PARTS[p]
        return chunk.at[pl.ds(off, n)] if mine else gsl(chip, p)

    def chip_of(zo, yo, xo):
        return zo * 4 + yo * 2 + xo

    def zcopy(zo, p, way, mine=False):
        chip = chip_of(zo, y, x)
        w = (way + 1) // 2
        return rcopy(src(chip, p, mine), gsl(chip, p), zs.at[w, zo, p], zr.at[zo, p], zdev[way])

    def xcopy(zo, yo, xo, p, mine=False):
        chip = chip_of(zo, yo, xo)
        s, r = (xas, xar) if p == 0 else (xbs, xbr)
        i = zo if p == 0 else zo * 2 + yo
        return rcopy(src(chip, p, mine), gsl(chip, p), s.at[i], r.at[i], xdev)

    def ycopy(zo, yo, xo, p, mine=False):
        chip = chip_of(zo, yo, xo)
        s, r = (ybs, ybr) if p == 1 else (yas, yar)
        i = zo if p == 1 else zo * 2 + xo
        return rcopy(src(chip, p, mine), gsl(chip, p), s.at[i], r.at[i], ydev)

    def ccopy(chip, p, mine=False):
        return rcopy(src(chip, p, mine), gsl(chip, p), cs.at[chip, p], cr.at[chip, p], cdev)

    for p in (0, 1):
        for way in (1, -1):
            @pl.when((z + way >= 0) & (z + way <= 3))
            def _():
                zcopy(z, p, way, True).start()
    xcopy(z, y, x, 0, True).start()
    ycopy(z, y, x, 1, True).start()
    ycopy(z, y, x, 0, True).start()
    xcopy(z, y, x, 1, True).start()
    mine = [pltpu.make_async_copy(chunk.at[pl.ds(*PARTS[p])], gsl(k, p), own.at[p]) for p in (0, 1)]
    for p in (0, 1):
        mine[p].start()
        ccopy(k, p, True).start()

    def column(zo, way):
        for p in (0, 1):
            zcopy(zo, p, way).wait_recv()

            @pl.when((zo + way * 0 + 0 >= 0) & (z + way >= 0) & (z + way <= 3))
            def _():
                zcopy(zo, p, way).start()
            if p == 0:
                xcopy(zo, y, x, 0).start()
                ycopy(zo, y, x, 0).start()
            else:
                ycopy(zo, y, x, 1).start()
                xcopy(zo, y, x, 1).start()
            ccopy(chip_of(zo, y, x), p).start()

    def beside(zo):
        xcopy(zo, y, 1 - x, 0).wait_recv()
        ycopy(zo, y, 1 - x, 0).start()
        ccopy(chip_of(zo, y, 1 - x), 0).start()
        ycopy(zo, 1 - y, x, 1).wait_recv()
        xcopy(zo, 1 - y, x, 1).start()
        ccopy(chip_of(zo, 1 - y, x), 1).start()

    def last(zo):
        ycopy(zo, 1 - y, x, 0).wait_recv()
        ccopy(chip_of(zo, 1 - y, x), 0).start()
        xcopy(zo, y, 1 - x, 1).wait_recv()
        ccopy(chip_of(zo, y, 1 - x), 1).start()
        ycopy(zo, 1 - y, 1 - x, 0).wait_recv()
        ccopy(chip_of(zo, 1 - y, 1 - x), 0).start()
        xcopy(zo, 1 - y, 1 - x, 1).wait_recv()
        ccopy(chip_of(zo, 1 - y, 1 - x), 1).start()

    def at_distance(s, f):
        for way in (1, -1):
            @pl.when((z - s * way >= 0) & (z - s * way <= 3))
            def _():
                f(z - s * way, way)

    at_distance(1, column)
    beside(z)
    at_distance(2, column)
    at_distance(1, lambda zo, way: beside(zo))
    at_distance(3, column)
    last(z)
    at_distance(2, lambda zo, way: beside(zo))
    at_distance(1, lambda zo, way: last(zo))
    at_distance(3, lambda zo, way: beside(zo))
    at_distance(2, lambda zo, way: last(zo))
    at_distance(3, lambda zo, way: last(zo))

    for p in (0, 1):
        mine[p].wait()
        for way in (1, -1):
            for zo in range(4):
                @pl.when(((z - zo) * way >= 0) & (z + way >= 0) & (z + way <= 3))
                def _():
                    zcopy(zo, p, way).wait_send()
    for zo in range(4):
        xcopy(zo, y, x, 0).wait_send()
        ycopy(zo, y, x, 1).wait_send()
        for o in range(2):
            ycopy(zo, y, o, 0).wait_send()
            xcopy(zo, o, x, 1).wait_send()
    for chip in range(16):
        for p in (0, 1):
            ccopy(chip, p).wait_send()
            off, n = PARTS[p]
            theirs = g_ref.at[chip, pl.ds(37 * (1 - c) + off, n)]
            rcopy(theirs, theirs, cs.at[chip, p], cr.at[chip, p], cdev).wait_recv()


def gather_weights(master):
    x = jnp.pad(master, (0, ROWS * 128 - SHARD)).reshape(ROWS, 128)
    sem = pltpu.SemaphoreType.DMA
    any_ = pl.BlockSpec(memory_space=pl.ANY)
    return pl.pallas_call(
        gather_kernel,
        out_shape=jax.ShapeDtypeStruct((16, CHIP, 8, 768), jnp.bfloat16),
        in_specs=[any_],
        out_specs=any_,
        scratch_shapes=[
            pltpu.VMEM((ROWS, 128), jnp.float32),
            pltpu.VMEM((TAIL, 128), jnp.float32),
            pltpu.VMEM((HEAD, 128), jnp.float32),
            pltpu.VMEM((WIN, 128), jnp.float32),
            pltpu.VMEM((SLOTS, 8, 768), jnp.bfloat16),
            sem, sem((2,)), sem((2,)), sem((2,)),
            sem((2, 4, 2)), sem((4, 2)),
            sem((4,)), sem((4,)), sem((8,)), sem((8,)),
            sem((8,)), sem((8,)), sem((4,)), sem((4,)),
            sem((16, 2)), sem((16, 2)),
        ],
        compiler_params=pltpu.CompilerParams(collective_id=0, has_side_effects=True, vmem_limit_bytes=40 << 20),
        name="gather_weights",
    )(x)


FRONT = 344
WIN2 = 2464
EDGE = 4
ENTRY_ROWS = 777


def reduce_kernel(g_ref, m_ref, one_ref, two_ref, step_ref, new1_ref, new2_ref,
                  acc, crecv, a1, b1, a2, b2, up, dn, total, ebuf, sq, sqr, win, mv, onev, twov,
                  lsem, asem, cs, cr, a1s, a1r, b1s, b1r, a2s, a2r, b2s, b2r, us, ur, ds_, dr, es, er, qs, qr):
    k, c, z, y, x = place()
    d = 2 * k + c
    xdev, ydev, cdev = (z * 4 + y * 2 + 1 - x, c), (z * 4 + (1 - y) * 2 + x, c), (k, 1 - c)
    zdev = {1: (jnp.minimum(k + 4, 15), c), -1: (jnp.maximum(k - 4, 0), c)}
    column_devs = [((z + s) % 4 * 4 + y * 2 + x, c) for s in (1, 2, 3)]
    prev = (jnp.where(c == 1, k, jnp.maximum(k - 1, 0)), 1 - c)
    nxt = (jnp.where(c == 0, k, jnp.minimum(k + 1, 15)), 1 - c)
    bar = pltpu.get_barrier_semaphore()
    far_next, far_prev = (c == 1) & (k < 15), (c == 0) & (k > 0)
    for dev in [xdev, ydev, cdev] + column_devs:
        pl.semaphore_signal(bar, inc=1, device_id=dev, device_id_type=MESH)

    @pl.when(far_next)
    def _():
        pl.semaphore_signal(bar, inc=1, device_id=nxt, device_id_type=MESH)

    @pl.when(far_prev)
    def _():
        pl.semaphore_signal(bar, inc=1, device_id=prev, device_id_type=MESH)

    pl.semaphore_wait(bar, 6 + jnp.where(far_next | far_prev, 1, 0))

    def chip_of(zo, yo, xo):
        return zo * 4 + yo * 2 + xo

    def load(chip):
        return pltpu.make_async_copy(g_ref.at[chip, pl.ds(37 * c, 37)], acc.at[chip], asem.at[chip])

    def ccopy(chip):
        return rcopy(g_ref.at[chip, pl.ds(37 * (1 - c), 37)], crecv.at[chip], cs.at[chip], cr.at[chip], cdev)

    def at_distance(s, f):
        if s == 0:
            f(z, 0)
            return
        for way in (1, -1):
            @pl.when((z + s * way >= 0) & (z + s * way <= 3))
            def _():
                f(z + s * way, way)

    def order(f):
        for s in (3, 2, 1, 0):
            at_distance(s, f)

    corners = ((1, 1), (1, 0), (0, 1), (0, 0))

    def flip(v, o):
        return 1 - v if o else v

    for oy, ox in corners:
        def go(zo, way):
            chip = chip_of(zo, flip(y, oy), flip(x, ox))
            load(chip).start()
            ccopy(chip).start()
        order(go)
    shards = [pltpu.make_async_copy(r, v, lsem.at[i]) for i, (r, v) in enumerate(((m_ref, mv), (one_ref, onev), (two_ref, twov)))]
    for s in shards:
        s.start()

    def psl(p):
        return pl.ds(*PARTS[p])

    def gain(dst, at, p, ref):
        off, n = PARTS[p]

        @pl.loop(0, n)
        def _(i):
            acc[at, off + i] = acc[at, off + i] + ref[i]

    def pair(chip):
        load(chip).wait()
        ccopy(chip).wait_recv()

        @pl.loop(0, 37)
        def _(i):
            acc[chip, i] = acc[chip, i] + crecv[chip, i]

    def a1copy(zo, xo):
        return rcopy(acc.at[chip_of(zo, 1 - y, xo), psl(0)], a1.at[zo * 2 + xo], a1s.at[zo * 2 + xo], a1r.at[zo * 2 + xo], ydev)

    def b1copy(zo, yo):
        return rcopy(acc.at[chip_of(zo, yo, 1 - x), psl(1)], b1.at[zo * 2 + yo], b1s.at[zo * 2 + yo], b1r.at[zo * 2 + yo], xdev)

    def a2copy(zo):
        return rcopy(acc.at[chip_of(zo, y, 1 - x), psl(0)], a2.at[zo], a2s.at[zo], a2r.at[zo], xdev)

    def b2copy(zo):
        return rcopy(acc.at[chip_of(zo, 1 - y, x), psl(1)], b2.at[zo], b2s.at[zo], b2r.at[zo], ydev)

    def zcopy(zo, way):
        buf, s, r = (up, us, ur) if way == 1 else (dn, ds_, dr)
        return rcopy(acc.at[chip_of(zo, y, x)], buf.at[zo], s.at[zo], r.at[zo], zdev[way])

    def first(oy, ox):
        def go(zo, way):
            yo, xo = flip(y, oy), flip(x, ox)
            pair(chip_of(zo, yo, xo))
            if oy:
                a1copy(zo, xo).start()
            if ox:
                b1copy(zo, yo).start()
        return go

    def second(zo, way):
        a1copy(zo, 1 - x).wait_recv()
        gain(acc, chip_of(zo, y, 1 - x), 0, a1.at[zo * 2 + 1 - x])
        a2copy(zo).start()
        b1copy(zo, 1 - y).wait_recv()
        gain(acc, chip_of(zo, 1 - y, x), 1, b1.at[zo * 2 + 1 - y])
        b2copy(zo).start()

    def third(zo, way):
        chip = chip_of(zo, y, x)
        a1copy(zo, x).wait_recv()
        gain(acc, chip, 0, a1.at[zo * 2 + x])
        b1copy(zo, y).wait_recv()
        gain(acc, chip, 1, b1.at[zo * 2 + y])
        a2copy(zo).wait_recv()
        gain(acc, chip, 0, a2.at[zo])
        b2copy(zo).wait_recv()
        gain(acc, chip, 1, b2.at[zo])
        if way:
            @pl.when((z - way >= 0) & (z - way <= 3))
            def _():
                zcopy(zo, way).wait_recv()
                buf = up if way == 1 else dn

                @pl.loop(0, 37)
                def _(i):
                    acc[chip, i] = acc[chip, i] + buf[zo, i]
            zcopy(zo, way).start()

    order(first(1, 1))
    order(first(1, 0))
    order(first(0, 1))
    order(second)
    order(first(0, 0))
    order(third)

    f32 = jnp.float32

    @pl.loop(0, 37)
    def _(i):
        total[i] = acc[k, i].astype(f32)

    for way in (1, -1):
        @pl.when((z - way >= 0) & (z - way <= 3))
        def _():
            zcopy(z, way).wait_recv()
            buf = up if way == 1 else dn

            @pl.loop(0, 37)
            def _(i):
                total[i] = total[i] + buf[z, i].astype(f32)

    early = early_vectors(k)
    nw0 = jnp.where(early, 36, 37)
    vecs = early == (c == 0)
    mine = jnp.where(vecs, 36, 37)
    to_next = rcopy(total.at[pl.ds(mine - EDGE, EDGE)], ebuf.at[0], es.at[0], er.at[0], nxt)
    to_prev = rcopy(total.at[pl.ds(0, EDGE)], ebuf.at[1], es.at[1], er.at[1], prev)

    @pl.when(d < 31)
    def _():
        to_next.start()

    @pl.when(d > 0)
    def _():
        to_prev.start()

    def square(i, run):
        t = total[i]
        t = t * t
        for j in range(6):
            run = run + t[:, 128 * j:128 * j + 128]
        return run

    sq[0] = lax.fori_loop(0, 37, square, jnp.zeros((8, 128), f32))
    for i, dev in enumerate((cdev, xdev, ydev)):
        step = rcopy(sq.at[i], sqr.at[i], qs.at[i], qr.at[i], dev)
        step.start()
        step.wait_recv()
        sq[i + 1] = sq[i] + sqr[i]
    hops = [rcopy(sq.at[3], sqr.at[3 + i], qs.at[3 + i], qr.at[3 + i], column_devs[i]) for i in range(3)]
    for h in hops:
        h.start()

    q, sh = shard_start(d)
    base = q - FRONT

    def flatten(ref, i, at, wide):
        @pl.when(wide)
        def _():
            t = ref[i]
            for j in range(6):
                win[pl.ds(at + j, 8, stride=24), :] = t[:, 128 * j:128 * j + 128]

        @pl.when(jnp.logical_not(wide))
        def _():
            t = ref[i]
            for j in range(6):
                win[pl.ds(at + j, 8, stride=6), :] = t[:, 128 * j:128 * j + 128]

    own_vectors = vecs & (vector_row(k, -1) >= 0)

    @pl.when(own_vectors)
    def _():
        flatten(total, 36, vector_row(k, q) - base, k < 0)

    w0 = jnp.where(c == 0, 73 * k, 73 * k + nw0)

    @pl.loop(0, mine)
    def _(t):
        at, wide = tile_start(w0 + t)
        flatten(total, t, at - base, wide)

    @pl.when(d > 0)
    def _():
        to_next.wait_recv()

        @pl.loop(0, EDGE)
        def _(t):
            at, wide = tile_start(w0 - EDGE + t)
            flatten(ebuf.at[0], t, at - base, wide)

    @pl.when(d < 31)
    def _():
        to_prev.wait_recv()

        @pl.loop(0, EDGE)
        def _(t):
            at, wide = tile_start(w0 + mine + t)
            flatten(ebuf.at[1], t, at - base, wide)

    for i, h in enumerate(hops):
        h.wait_recv()
    parts = [sqr[3], sqr[4], sqr[5]]
    rows = [sq[3]] + parts
    whole = (rows[0] + rows[2]) + (rows[1] + rows[3])
    square_sum = jnp.sum(jnp.sum(whole, axis=1, keepdims=True), axis=0, keepdims=True)
    factor = jnp.minimum(1.0, lax.rsqrt(square_sum / RAW + 1e-06))
    for s in shards:
        s.wait()
    lanes = lax.broadcasted_iota(jnp.int32, (80, 128), 1)
    rowi = lax.broadcasted_iota(jnp.int32, (80, 128), 0)
    back = (128 - sh) % 128

    @pl.loop(0, ROWS // 80)
    def _(i):
        r = pl.multiple_of(i * 80, 8)
        here = pltpu.roll(win[pl.ds(FRONT + r, 80), :], back, 1)
        there = pltpu.roll(win[pl.ds(FRONT + 1 + r, 80), :], back, 1)
        grad = jnp.where(lanes < 128 - sh, here, there) * factor
        entry = (d == 0) & (rowi + r < ENTRY_ROWS)
        rate = jnp.where(entry, learn_rate * layer_decay, learn_rate)
        one = beta_one * onev[pl.ds(r, 80), :] + (1.0 - beta_one) * grad
        two = beta_two * twov[pl.ds(r, 80), :] + (1.0 - beta_two) * grad * grad
        fixed_one = one / (1.0 - beta_one ** STEP)
        fixed_two = two / (1.0 - beta_two ** STEP)
        step_ref[pl.ds(r, 80), :] = -rate * (fixed_one / (jnp.sqrt(fixed_two) + adam_eps) + weight_decay * mv[pl.ds(r, 80), :])
        new1_ref[pl.ds(r, 80), :] = one
        new2_ref[pl.ds(r, 80), :] = two

    for i, dev in enumerate((cdev, xdev, ydev)):
        rcopy(sq.at[i], sqr.at[i], qs.at[i], qr.at[i], dev).wait_send()
    for h in hops:
        h.wait_send()

    @pl.when(d < 31)
    def _():
        to_next.wait_send()

    @pl.when(d > 0)
    def _():
        to_prev.wait_send()

    for chip in range(16):
        ccopy(chip).wait_send()
    for zo in range(4):
        a2copy(zo).wait_send()
        b2copy(zo).wait_send()
        for o in range(2):
            a1copy(zo, o).wait_send()
            b1copy(zo, o).wait_send()
        for way in (1, -1):
            @pl.when((zo - z) * way > 0)
            def _():
                zcopy(zo, way).wait_send()


def reduce_and_step(grads, master, first_moment, second_moment):
    def rows(v):
        return jnp.pad(v, (0, ROWS * 128 - SHARD)).reshape(ROWS, 128)

    sem = pltpu.SemaphoreType.DMA
    any_ = pl.BlockSpec(memory_space=pl.ANY)
    vm = pl.BlockSpec(memory_space=pltpu.VMEM)
    bf, f32 = jnp.bfloat16, jnp.float32
    tile = (8, 768)
    outs = pl.pallas_call(
        reduce_kernel,
        out_shape=[jax.ShapeDtypeStruct((ROWS, 128), f32)] * 3,
        in_specs=[any_] * 4,
        out_specs=[vm] * 3,
        scratch_shapes=[
            pltpu.VMEM((16, 37) + tile, bf), pltpu.VMEM((16, 37) + tile, bf),
            pltpu.VMEM((8, 19) + tile, bf), pltpu.VMEM((8, 18) + tile, bf),
            pltpu.VMEM((4, 19) + tile, bf), pltpu.VMEM((4, 18) + tile, bf),
            pltpu.VMEM((4, 37) + tile, bf), pltpu.VMEM((4, 37) + tile, bf),
            pltpu.VMEM((37,) + tile, f32), pltpu.VMEM((2, EDGE) + tile, f32),
            pltpu.VMEM((4, 8, 128), f32), pltpu.VMEM((6, 8, 128), f32),
            pltpu.VMEM((WIN2, 128), f32),
            pltpu.VMEM((ROWS, 128), f32), pltpu.VMEM((ROWS, 128), f32), pltpu.VMEM((ROWS, 128), f32),
            sem((3,)), sem((16,)), sem((16,)), sem((16,)),
            sem((8,)), sem((8,)), sem((8,)), sem((8,)), sem((4,)), sem((4,)), sem((4,)), sem((4,)),
            sem((4,)), sem((4,)), sem((4,)), sem((4,)), sem((2,)), sem((2,)), sem((6,)), sem((6,)),
        ],
        compiler_params=pltpu.CompilerParams(collective_id=1, has_side_effects=True, vmem_limit_bytes=56 << 20),
        name="reduce_and_step",
    )(grads, rows(master), rows(first_moment), rows(second_moment))
    return [o.reshape(-1)[:SHARD] for o in outs]


WEIGHTS = (
    (0, 0, 16),
    (3, 16, 96),
    (5, 112, 96),
    (6, 208, 96),
    (8, 304, 96),
    (12, 400, 384),
    (14, 784, 384),
)
VECTORS = (
    (1, 0, 0),
    (2, 0, 1),
    (4, 1, 0),
    (7, 4, 0),
    (9, 5, 0),
    (10, 5, 1),
    (11, 5, 2),
    (13, 10, 0),
    (15, 15, 0),
    (16, 15, 1),
    (17, 15, 2),
)


def vector_slot(chip):
    return 36 if chip in (0, 4, 5) else 73


def slots_of(first, count):
    runs = []
    for w in range(first, first + count):
        chip, at = divmod(w, 73)
        slot = chip * CHIP + at + (1 if at >= vector_slot(chip) else 0)
        if runs and runs[-1][0] + runs[-1][1] == slot:
            runs[-1][1] += 1
        else:
            runs.append([slot, 1])
    return runs


def unpack_gathered(gathered):
    tiles = gathered.reshape(16 * CHIP, 8, D)
    pieces = {}
    for name, first, count in WEIGHTS:
        got = jnp.concatenate([tiles[s : s + n] for s, n in slots_of(first, count)])
        if name == 12:
            got = got.reshape(96, 4, 8, D).transpose(0, 2, 1, 3).reshape(D, FF)
        pieces[name] = got.reshape(-1, FF if name == 12 else D)
    for name, chip, row in VECTORS:
        block = gathered[chip, vector_slot(chip)]
        if name == 13:
            pieces[name] = block[row : row + 4].reshape(FF)
        elif name == 2:
            pieces[name] = block[row, : BUCKETS * H].reshape(BUCKETS, H)
        else:
            pieces[name] = block[row]
    return Params(*[pieces[i] for i in range(18)])


def pack_gradients(pieces):
    by_name = [p.astype(jnp.bfloat16) for p in pieces]
    weights = []
    for name, first, count in WEIGHTS:
        got = by_name[name]
        if name == 12:
            got = got.reshape(96, 8, 4, D).transpose(0, 2, 1, 3)
        weights.append(got.reshape(count, 8, D))
    cuts = []
    for chip in range(16):
        held = [(r, by_name[n]) for n, c, r in VECTORS if c == chip]
        rows = [jnp.pad(v.reshape(-1), (0, -v.size % D)).reshape(-1, D) for _, v in held]
        block = jnp.concatenate(rows + [jnp.zeros((8 - sum(r.shape[0] for r in rows), D), jnp.bfloat16)])
        cuts.append((73 * chip + vector_slot(chip), block[None]))
    parts = []
    for (name, first, count), tiles in zip(WEIGHTS, weights):
        at = first
        for w, block in [c for c in cuts if first <= c[0] < first + count]:
            if w > at:
                parts.append(tiles[at - first : w - first])
            parts.append(block)
            at = w
        parts.append(tiles[at - first :])
    parts.extend(block for w, block in cuts if w == 1168)
    return jnp.concatenate(parts).reshape(16, CHIP, 8, D)


def per_device(
    custom,
    tokens,
    cotangent,
    page_boxes,
    page_lengths,
    padding,
    buckets,
    master,
    first_moment,
    second_moment,
):
    blocks_here = tokens.shape[0]
    rows = tokens.shape[1]
    count_rows = blocks_here * rows
    if custom:
        entry_part = unpack_gathered(gather_weights(master))
    else:
        shard_low = master.astype(jnp.bfloat16)
        flat_params = lax.all_gather(shard_low, ("dp", "seq"), axis=0, tiled=True)
        entry_part = unpack(flat_params)
    layers = [entry_part]
    places = lax.axis_index("seq") * rows + jnp.arange(rows, dtype=jnp.int32)
    page_ends = running_sum(page_lengths)
    page_of = jnp.sum((places[None, :, None] >= page_ends[:, None, :]).astype(jnp.int32), axis=2)
    own_tags = jnp.where(padding > 0, page_of + 1, 0).astype(jnp.bfloat16)
    query_tags = (page_of + 1).astype(jnp.float32)
    key_places = jnp.arange(BLOCK, dtype=jnp.int32)
    bucket_ids = jnp.arange(BUCKETS, dtype=jnp.int32)
    onehot = (buckets[:, None, :, :] == bucket_ids[None, :, None, None]).astype(jnp.bfloat16)
    score_bias = jnp.einsum(
        "bh,cbqk->chqk", entry_part.bias_table, onehot, preferred_element_type=jnp.float32
    )
    features_low = layout_features(page_boxes.reshape(4, count_rows)).astype(jnp.bfloat16)
    hidden = (
        tokens.reshape(count_rows, D).astype(jnp.float32)
        + matmul_low(features_low, entry_part.layout_weight)
        + as_float(entry_part.layout_bias)
    )
    saved = []
    for weights in layers:
        inputs_low = hidden.astype(jnp.bfloat16)
        query_low = (
            (matmul_low(inputs_low, weights.query_weight) + as_float(weights.query_bias))
            * 0.125
        ).astype(jnp.bfloat16)
        key_low = matmul_low(inputs_low, weights.key_weight).astype(jnp.bfloat16)
        value_low = (
            matmul_low(inputs_low, weights.value_weight) + as_float(weights.value_bias)
        ).astype(jnp.bfloat16)
        key_all, value_all, tags_all = (
            lax.all_gather(key_low.reshape(blocks_here, rows, D), "seq", axis=1, tiled=True),
            lax.all_gather(value_low.reshape(blocks_here, rows, D), "seq", axis=1, tiled=True),
            lax.all_gather(own_tags, "seq", axis=1, tiled=True),
        )
        allowed = (tags_all[:, None, :].astype(jnp.float32) == query_tags[:, :, None]) | (
            key_places[None, None, :] == places[None, :, None]
        )
        allowed = allowed[:, None, :, :]
        scores = attention_scores(query_low, key_all, score_bias, allowed, blocks_here, rows)
        top_score = jnp.max(scores, axis=-1, keepdims=True)
        expo_score = jnp.exp(scores - top_score)
        total_exp = jnp.sum(expo_score, axis=-1, keepdims=True)
        soft = expo_score / total_exp
        log_total = top_score + jnp.log(total_exp)
        value_heads = value_all.reshape(blocks_here, BLOCK, H, HD)
        context = jnp.einsum(
            "chqk,ckhd->cqhd",
            soft.astype(jnp.bfloat16),
            value_heads,
            preferred_element_type=jnp.float32,
        )
        context_low = context.reshape(count_rows, D).astype(jnp.bfloat16)
        first_in = (
            hidden
            + matmul_low(context_low, weights.output_weight)
            + as_float(weights.output_bias)
        )
        first_out = layer_norm(
            first_in, as_float(weights.first_gain), as_float(weights.first_shift)
        )
        first_low = first_out.astype(jnp.bfloat16)
        up_sum = matmul_low(first_low, weights.up_weight) + as_float(weights.up_bias)
        activated = gelu_exact(up_sum).astype(jnp.bfloat16)
        second_in = (
            first_out
            + matmul_low(activated, weights.down_weight)
            + as_float(weights.down_bias)
        )
        stash = SimpleNamespace(
            inputs_low=inputs_low,
            query_low=query_low,
            key_low=key_low,
            value_low=value_low,
            allowed=allowed,
            log_total=log_total,
            context_low=context_low,
            first_in=first_in,
            first_low=first_low,
            up_sum=up_sum,
            activated=activated,
            second_in=second_in,
        )
        stash.key_all = key_all
        stash.value_all = value_all
        saved.append(stash)
        hidden = layer_norm(
            second_in, as_float(weights.second_gain), as_float(weights.second_shift)
        )
    grad_out = cotangent.reshape(count_rows, D).astype(jnp.float32)
    table_grad = jnp.zeros((BUCKETS, H), jnp.float32)
    layer_grads = []
    for number in reversed(range(LAYERS)):
        weights = layers[number]
        stash = saved[number]
        norm_pair = jax.vjp(
            layer_norm,
            stash.second_in,
            as_float(weights.second_gain),
            as_float(weights.second_shift),
        )
        grad_second, grad_gain_two, grad_shift_two = norm_pair[1](grad_out)
        grad_down_bias = jnp.sum(grad_second, axis=0)
        down_back = grad_second.astype(jnp.bfloat16)
        grad_down_weight = jnp.einsum(
            "nf,nd->fd", stash.activated, down_back, preferred_element_type=jnp.float32
        )
        grad_activated = jnp.einsum(
            "nd,fd->nf", down_back, weights.down_weight, preferred_element_type=jnp.float32
        )
        gelu_pair = jax.vjp(gelu_exact, stash.up_sum)
        grad_up = gelu_pair[1](grad_activated)[0]
        grad_up_bias = jnp.sum(grad_up, axis=0)
        up_back = grad_up.astype(jnp.bfloat16)
        grad_up_weight = jnp.einsum(
            "nd,nf->df", stash.first_low, up_back, preferred_element_type=jnp.float32
        )
        grad_first = grad_second + jnp.einsum(
            "nf,df->nd", up_back, weights.up_weight, preferred_element_type=jnp.float32
        )
        first_pair = jax.vjp(
            layer_norm,
            stash.first_in,
            as_float(weights.first_gain),
            as_float(weights.first_shift),
        )
        grad_first_in, grad_gain_one, grad_shift_one = first_pair[1](grad_first)
        grad_output_bias = jnp.sum(grad_first_in, axis=0)
        attend_back = grad_first_in.astype(jnp.bfloat16)
        grad_output_weight = jnp.einsum(
            "nd,ne->de", stash.context_low, attend_back, preferred_element_type=jnp.float32
        )
        grad_context = jnp.einsum(
            "ne,de->nd", attend_back, weights.output_weight, preferred_element_type=jnp.float32
        ).astype(jnp.bfloat16)
        grad_context = grad_context.reshape(blocks_here, rows, H, HD)
        key_all = stash.key_all
        value_all = stash.value_all
        scores = attention_scores(
            stash.query_low, key_all, score_bias, stash.allowed, blocks_here, rows
        )
        soft = jnp.exp(scores - stash.log_total)
        key_heads = key_all.reshape(blocks_here, BLOCK, H, HD)
        value_heads = value_all.reshape(blocks_here, BLOCK, H, HD)
        grad_soft = jnp.einsum(
            "cqhd,ckhd->chqk", grad_context, value_heads, preferred_element_type=jnp.float32
        )
        inner_sum = jnp.sum(soft * grad_soft, axis=-1, keepdims=True)
        grad_scores = (soft * (grad_soft - inner_sum)).astype(jnp.bfloat16)
        table_grad = jnp.einsum(
            "chqk,cbqk->bh", grad_scores, onehot, preferred_element_type=jnp.float32
        )
        query_heads = stash.query_low.reshape(blocks_here, rows, H, HD)
        grad_query = (
            jnp.einsum(
                "chqk,ckhd->cqhd", grad_scores, key_heads, preferred_element_type=jnp.float32
            ).reshape(count_rows, D)
            * 0.125
        )
        grad_key_all = jnp.einsum(
            "chqk,cqhd->ckhd", grad_scores, query_heads, preferred_element_type=jnp.float32
        ).reshape(blocks_here, BLOCK, D)
        grad_value_all = jnp.einsum(
            "chqk,cqhd->ckhd",
            soft.astype(jnp.bfloat16),
            grad_context,
            preferred_element_type=jnp.float32,
        ).reshape(blocks_here, BLOCK, D)
        grad_key, grad_value = (
            lax.psum_scatter(
                grad_key_all.astype(jnp.bfloat16), "seq", scatter_dimension=1, tiled=True
            ).astype(jnp.float32),
            lax.psum_scatter(
                grad_value_all.astype(jnp.bfloat16), "seq", scatter_dimension=1, tiled=True
            ).astype(jnp.float32),
        )
        grad_key = grad_key.reshape(count_rows, D)
        grad_value = grad_value.reshape(count_rows, D)
        grad_query_bias = jnp.sum(grad_query, axis=0)
        grad_value_bias = jnp.sum(grad_value, axis=0)
        query_back = grad_query.astype(jnp.bfloat16)
        key_back = grad_key.astype(jnp.bfloat16)
        value_back = grad_value.astype(jnp.bfloat16)
        grad_query_weight = jnp.einsum(
            "nd,ne->de", stash.inputs_low, query_back, preferred_element_type=jnp.float32
        )
        grad_key_weight = jnp.einsum(
            "nd,ne->de", stash.inputs_low, key_back, preferred_element_type=jnp.float32
        )
        grad_value_weight = jnp.einsum(
            "nd,ne->de", stash.inputs_low, value_back, preferred_element_type=jnp.float32
        )
        grad_out = grad_first_in + jnp.einsum(
            "ne,de->nd", query_back, weights.query_weight, preferred_element_type=jnp.float32
        )
        grad_out = grad_out + jnp.einsum(
            "ne,de->nd", key_back, weights.key_weight, preferred_element_type=jnp.float32
        )
        grad_out = grad_out + jnp.einsum(
            "ne,de->nd", value_back, weights.value_weight, preferred_element_type=jnp.float32
        )
        layer_grads.insert(
            0,
            [
                grad_query_weight,
                grad_query_bias,
                grad_key_weight,
                grad_value_weight,
                grad_value_bias,
                grad_output_weight,
                grad_output_bias,
                grad_gain_one,
                grad_shift_one,
                grad_up_weight,
                grad_up_bias,
                grad_down_weight,
                grad_down_bias,
                grad_gain_two,
                grad_shift_two,
            ],
        )
    embed_back = grad_out.astype(jnp.bfloat16)
    grad_layout_weight = jnp.einsum(
        "nf,nd->fd", features_low, embed_back, preferred_element_type=jnp.float32
    )
    grad_layout_bias = jnp.sum(grad_out, axis=0)
    all_pieces = [grad_layout_weight, grad_layout_bias, table_grad]
    layer_list = layer_grads[0]
    all_pieces = all_pieces + layer_list
    if custom:
        param_step, new_first, new_second = reduce_and_step(
            pack_gradients(all_pieces), master, first_moment, second_moment
        )
    else:
        flat_grad = jnp.concatenate([piece.reshape(-1) for piece in all_pieces])
        grad_shard = lax.psum_scatter(flat_grad, ("dp", "seq"), scatter_dimension=0, tiled=True)
        square = lax.psum(jnp.sum(grad_shard * grad_shard), ("dp", "seq"))
        factor = jnp.minimum(1.0, lax.rsqrt(square / RAW + 1e-06))
        shard_size = master.shape[0]
        global_index = lax.axis_index(("dp", "seq")) * shard_size + jnp.arange(
            shard_size, dtype=jnp.int32
        )
        param_step, new_first, new_second = adam_update(
            master, first_moment, second_moment, grad_shard * factor, global_index
        )
    activations = hidden.reshape(blocks_here, rows, D).astype(jnp.bfloat16)
    input_grad = grad_out.reshape(blocks_here, rows, D)
    return (activations, input_grad, param_step, new_first, new_second)


def solution(mesh):
    in_specs = (
        P("dp", "seq", None),
        P("dp", "seq", None),
        P(None, "dp", "seq"),
        P("dp", None),
        P("dp", "seq"),
        P("dp", "seq", None),
        P(("dp", "seq")),
        P(("dp", "seq")),
        P(("dp", "seq")),
    )
    out_specs = (
        P("dp", "seq", None),
        P("dp", "seq", None),
        P(("dp", "seq")),
        P(("dp", "seq")),
        P(("dp", "seq")),
    )
    custom = dict(mesh.shape) == {"dp": 16, "seq": 2}
    return jax.shard_map(
        functools.partial(per_device, custom), mesh=mesh, in_specs=in_specs, out_specs=out_specs, check_vma=False
    )
```

profile of v0, /device:TPU:0, one launch (start us, length us, event | category | flops | bytes accessed | tf_op | source)
XLA Modules:
  0.0 554.7 jit_solution(13396492844274003)
XLA Ops:
  8.5 72.8 %gather_weights.1 = bf16[16,74,8,768]{3,2,1,0:T(8,128)(2,1)} custom-call(f32[1760,128]{1,0:T(8,128)S(1)} %pad_bitcast_fusion.2.x_ref.m_ref), custom_call_target="tpu_custom_call" | custom-call | tf_op jit(solution)/shard_map/gather_weights/pallas_call | solution.py:410
  130.5 16.2 %fusion.1 = f32[512,1024,12]{0,2,1:T(8,128)} fusion(s32[512,1024]{0,1:T(8,128)S(1)} %copy.40, bf16[32,12]{1,0:T(8,128)(2,1)S(1)} %reshape_squeeze.3), kind=kOutput, calls=%fused_computation.2 | convolution fusion | flops 419430400 | bytes 27263744 | tf_op jit(solution)/shard_map/bh,cbqk->chqk/dot_general | solution.py:880
  146.7 30.4 %copy.43 = f32[512,1024,12]{1,0,2:T(8,128)} copy(f32[512,1024,12]{0,2,1:T(8,128)} %fusion.1) | data formatting | bytes 50331648 | tf_op jit(solution)/shard_map/bh,cbqk->chqk/dot_general | solution.py:880
  181.3 16.0 %fusion.98 = (f32[12,512]{1,0:T(8,128)S(1)}, f32[1,12,512,1024]{3,2,1,0:T(8,128)}) fusion(f32[512,1024,12]{1,0,2:T(8,128)} %copy.43, bf16[512,12,64]{0,2,1:T(8,128)(2,1)S(1)} %bitcast.297, bf16[1024,12,64]{0,2,1:T(8,128)(2,1)S(1)} %bitcast.295, pred[512,1024]{1,0:T(8,128)(4,1)S(1)} %fusion.28), kind=kOutput, calls=%fused_computation.227 | convolution fusion | flops 824174592 | bytes 53239808 | tf_op jit(solution)/shard_map/cqhd,ckhd->chqk/dot_general | solution.py:103
  197.3 10.9 %fusion.7 = f32[12,512]{1,0:T(8,128)S(1)} fusion(f32[1,12,512,1024]{3,2,1,0:T(8,128)} %get-tuple-element.52, f32[12,512]{1,0:T(8,128)S(1)} %get-tuple-element.51), kind=kLoop, calls=%fused_computation.14 | loop fusion | flops 12576768 | bytes 25214976 | tf_op jit(solution)/shard_map/reduce_sum | solution.py:912
  210.1 11.3 %fusion.45 = bf16[12,64,512]{2,1,0:T(8,128)(2,1)S(1)} fusion(bf16[1024,12,64]{0,2,1:T(8,128)(2,1)S(1)} %bitcast.302, f32[12,512]{1,0:T(8,128)S(1)} %fusion.7, f32[1,12,512,1024]{3,2,1,0:T(8,128)} %get-tuple-element.52, f32[12,512]{1,0:T(8,128)S(1)} %get-tuple-element.51), kind=kOutput, calls=%fused_computation.83 | convolution fusion | flops 824573952 | bytes 27574272 | tf_op jit(solution)/shard_map/chqk,ckhd->cqhd/dot_general | solution.py:916
  222.7 19.5 %multiply_convert_fusion = (bf16[512,3072]{1,0:T(8,128)(2,1)S(1)}, f32[512,3072]{1,0:T(8,128)S(1)}, f32[512,3072]{1,0:T(8,128)}) fusion(f32[3072]{0:T(1024)S(1)} %reshape.702, bf16[768,3072]{1,0:T(8,128)(2,1)} %bitcast.28, f32[512,768]{1,0:T(8,128)S(1)} %get-tuple-element.54, f32[768]{0:T(1024)S(1)} %get-tuple-element.14, f32[768]{0:T(1024)S(1)} %get-tuple-element.15, ...), kind=kOutput, calls=%fused_computation.25 | convolution fusion | flops 2521694208 | bytes 22042624 | tf_op jit(solution)/shard_map/dot_general | solution.py:79
  242.2 6.3 %fusion.100 = (f32[512]{0:T(512)S(1)}, f32[512,768]{1,0:T(8,128)S(1)}) fusion(f32[768]{0:T(1024)S(1)} %get-tuple-element.13, bf16[512,3072]{1,0:T(8,128)(2,1)S(1)} %get-tuple-element.29, bf16[384,8,768]{2,1,0:T(8,128)(2,1)} %get-tuple-element.31, f32[768]{0:T(1024)S(1)} %get-tuple-element.14, f32[768]{0:T(1024)S(1)} %get-tuple-element.15, ...), kind=kOutput, calls=%fused_computation.229 | convolution fusion | flops 2418671104 | bytes 11025408 | tf_op jit(solution)/shard_map/dot_general | solution.py:79
  251.2 8.4 %fusion.102 = (bf16[3072]{0:T(1024)(128)(2,1)S(1)}, bf16[512,3072]{1,0:T(8,128)(2,1)S(1)}) fusion(f32[512,3072]{1,0:T(8,128)S(1)} %get-tuple-element.30, bf16[384,8,768]{2,1,0:T(8,128)(2,1)} %get-tuple-element.31, f32[512,768]{1,0:T(8,128)S(1)} %get-tuple-element.28, f32[512]{0:T(512)S(1)} %negate_multiply_fusion.2, f32[512,3072]{1,0:T(8,128)} %get-tuple-element.55, ...), kind=kOutput, calls=%fused_computation.231 | convolution fusion | flops 2441868288 | bytes 22040576 | tf_op jit(solution)/shard_map/nd,fd->nf/dot_general | solution.py:977
  259.6 6.6 %multiply_reduce_fusion = (bf16[768]{0:T(1024)(128)(2,1)S(1)}, f32[512]{0:T(512)S(1)}, bf16[768]{0:T(1024)(128)(2,1)S(1)}, f32[512,768]{1,0:T(8,128)S(1)}) fusion(f32[512,768]{1,0:T(8,128)S(1)} %get-tuple-element.54, f32[512]{0:T(512)S(1)} %fusion.78, f32[512]{0:T(512)S(1)} %broadcast_multiply_fusion.1, f32[768]{0:T(1024)S(1)} %get-tuple-element.15, ...), kind=kOutput, calls=%fused_computation.61 | convolution fusion | flops 2419849216 | bytes 12597248 | tf_op jit(solution)/shard_map/nf,df->nd/dot_general | solution.py:987
  270.0 18.1 %fusion.6 = (f32[12,512]{1,0:T(8,128)S(1)}, f32[12,512,1024]{2,1,0:T(8,128)}) fusion(f32[1,12,512,1024]{3,2,1,0:T(8,128)} %get-tuple-element.52, f32[12,512]{1,0:T(8,128)S(1)} %log_add_fusion, bf16[512,12,64]{0,2,1:T(8,128)(2,1)S(1)} %bitcast.300, bf16[1024,12,64]{0,2,1:T(8,128)(2,1)} %bitcast.303), kind=kOutput, calls=%fused_computation.10 | convolution fusion | flops 824174592 | bytes 52740096 | tf_op jit(solution)/shard_map/cqhd,ckhd->chqk/dot_general | solution.py:1014
  288.1 16.6 %fusion.12 = bf16[12,512,1024]{2,1,0:T(8,128)(2,1)S(1)} fusion(f32[12,512,1024]{2,1,0:T(8,128)} %get-tuple-element.60, f32[1,12,512,1024]{3,2,1,0:T(8,128)} %get-tuple-element.52, f32[12,512]{1,0:T(8,128)S(1)} %get-tuple-element.59, f32[12,512]{1,0:T(8,128)S(1)} %log_add_fusion), kind=kLoop, calls=%fused_computation.18 | loop fusion | flops 25165824 | bytes 62963712 | tf_op jit(solution)/shard_map/reshape.51
  304.8 4.0 convolution_convert_fusion.2
  313.4 23.3 %copy.45 = bf16[12,512,1024]{1,0,2:T(8,128)(2,1)} copy(bf16[12,512,1024]{2,1,0:T(8,128)(2,1)} %copy-done.1) | data formatting | bytes 25165824 | tf_op jit(solution)/shard_map/reshape.51
  336.7 11.7 %fusion.31 = bf16[12,64,1024]{2,1,0:T(8,128)(2,1)} fusion(bf16[512,12,64]{0,2,1:T(8,128)(2,1)S(1)} %bitcast.301, f32[1,12,512,1024]{3,2,1,0:T(8,128)} %get-tuple-element.52, f32[12,512]{1,0:T(8,128)S(1)} %log_add_fusion), kind=kOutput, calls=%fused_computation.54 | convolution fusion | flops 818675712 | bytes 27549696 | tf_op jit(solution)/shard_map/chqk,cqhd->ckhd/dot_general | solution.py:1032
  348.5 12.8 %fusion.52 = bf16[32,12]{0,1:T(8,128)(2,1)S(1)} fusion(bf16[12,512,1024]{1,0,2:T(8,128)(2,1)} %copy.45, s32[512,1024]{0,1:T(8,128)S(1)} %copy-done.5), kind=kOutput, calls=%fused_computation.99 | convolution fusion | flops 419430784 | bytes 14680832 | tf_op jit(solution)/shard_map/chqk,cbqk->bh/dot_general | solution.py:1019
  361.3 10.2 %fusion.95 = (bf16[12,64,512]{2,1,0:T(8,128)(2,1)}, bf16[1,512,12,64]{1,3,2,0:T(8,128)(2,1)}, f32[12,64,512]{2,1,0:T(8,128)}) fusion(bf16[1024,12,64]{0,2,1:T(8,128)(2,1)S(1)} %bitcast.296, bf16[12,512,1024]{2,1,0:T(8,128)(2,1)} %copy-done.1), kind=kOutput, calls=%fused_computation.224 | convolution fusion | flops 806486016 | bytes 17301504 | tf_op jit(solution)/shard_map/chqk,ckhd->cqhd/dot_general | solution.py:1024
  378.4 3.2 fusion.69
  381.6 3.1 convolution_convert_fusion.6
  386.8 4.7 convolution_convert_fusion
  391.5 4.9 convolution_convert_fusion.1
  396.4 3.1 fusion.65
  399.6 3.6 fusion.101
  441.7 99.6 %reduce_and_step.1 = (f32[1760,128]{1,0:T(8,128)}, f32[1760,128]{1,0:T(8,128)}, f32[1760,128]{1,0:T(8,128)}) custom-call(bf16[16,74,8,768]{3,2,1,0:T(8,128)(2,1)} %bitcast.87.g_ref, f32[1760,128]{1,0:T(8,128)} %copy-done, f32[1760,128]{1,0:T(8,128)} %get-tuple-element.67.one_ref, f32[1760,128]{1,0:T(8,128)} %get-tuple-element.66.two_ref), custom_call_target="tpu_custom_call" | custom-call | tf_op jit(solution)/shard_map/reduce_and_step/pallas_call | solution.py:740
  (260 shorter events, 119.9 us)
Async XLA Ops:
  7.2 172.4 %all-gather.7.cloned.1.call-start = ((), (), s32[]{:S(2)}) async-start(), calls=%async_computation.5 | async-start | bytes 2359296 | tf_op jit(solution)/shard_map/all_gather | solution.py:901
  8.5 72.9 %copy-start = (f32[1760,128]{1,0:T(8,128)}, f32[1760,128]{1,0:T(8,128)S(1)}, u32[]{:S(2)}) copy-start(f32[1760,128]{1,0:T(8,128)S(1)} %pad_bitcast_fusion.2.x_ref.m_ref) | copy-start | bytes 2703364
  8.5 76.9 %copy-start.45 = (s32[4,1,512]{2,1,0:T(1,128)S(1)}, s32[4,1,512]{2,1,0:T(1,128)}, u32[]{:S(2)}) copy-start(s32[4,1,512]{2,1,0:T(1,128)} %param.11) | copy-start | bytes 24580
  8.5 78.1 %copy-start.26 = (bf16[1,512,768]{2,1,0:T(8,128)(2,1)S(1)}, bf16[1,512,768]{2,1,0:T(8,128)(2,1)}, u32[]{:S(2)}) copy-start(bf16[1,512,768]{2,1,0:T(8,128)(2,1)} %param.9) | copy-start | bytes 2359300
  89.1 32.3 %copy-start.27 = (bf16[512,768]{1,0:T(8,128)(2,1)}, bf16[512,768]{1,0:T(8,128)(2,1)S(1)}, u32[]{:S(2)}) copy-start(bf16[512,768]{1,0:T(8,128)(2,1)S(1)} %get-tuple-element.49) | copy-start | bytes 2359300
  90.8 117.5 %all-gather.5.cloned.1.call-start = ((), (), s32[]{:S(2)}) async-start(), calls=%async_computation.4 | async-start | bytes 2359296 | tf_op jit(solution)/shard_map/all_gather | solution.py:902
  99.1 12.4 %copy-start.31 = (bf16[12,8,768]{2,1,0:T(8,128)(2,1)}, bf16[12,8,768]{2,1,0:T(8,128)(2,1)S(1)}, u32[]{:S(2)}) copy-start(bf16[12,8,768]{2,1,0:T(8,128)(2,1)S(1)} %slice.342) | copy-start | bytes 442372
  100.1 11.4 %copy-start.33 = (bf16[11,8,768]{2,1,0:T(8,128)(2,1)}, bf16[11,8,768]{2,1,0:T(8,128)(2,1)S(1)}, u32[]{:S(2)}) copy-start(bf16[11,8,768]{2,1,0:T(8,128)(2,1)S(1)} %slice.340) | copy-start | bytes 405508
  114.1 282.3 %reduce-scatter.3.cloned.1.call-start = ((), (), s32[]{:S(2)}) async-start(), calls=%async_computation.2 | async-start | bytes 2359296 | tf_op jit(solution)/shard_map/reduce_scatter | solution.py:1039
  116.8 11.6 %copy-start.36 = (bf16[20,8,768]{2,1,0:T(8,128)(2,1)}, bf16[20,8,768]{2,1,0:T(8,128)(2,1)S(1)}, u32[]{:S(2)}) copy-start(bf16[20,8,768]{2,1,0:T(8,128)(2,1)S(1)} %slice.343) | copy-start | bytes 737284
  122.5 58.8 %copy-start.6 = (bf16[512,768]{0,1:T(8,128)(2,1)}, bf16[512,768]{0,1:T(8,128)(2,1)S(1)}, u32[]{:S(2)}) copy-start(bf16[512,768]{0,1:T(8,128)(2,1)S(1)} %copy.38) | copy-start | bytes 2359300
  130.5 16.2 %copy-start.4 = (s32[512,1024]{0,1:T(8,128)}, s32[512,1024]{0,1:T(8,128)S(1)}, u32[]{:S(2)}) copy-start(s32[512,1024]{0,1:T(8,128)S(1)} %copy.40) | copy-start | bytes 6291460
  181.3 16.0 %copy-start.2 = (bf16[1024,768]{0,1:T(8,128)(2,1)}, bf16[1024,768]{0,1:T(8,128)(2,1)S(1)}, u32[]{:S(2)}) copy-start(bf16[1024,768]{0,1:T(8,128)(2,1)S(1)} %copy.39) | copy-start | bytes 4718596
  210.0 11.4 %copy-start.9 = (bf16[1024,768]{0,1:T(8,128)(2,1)}, bf16[1024,768]{0,1:T(8,128)(2,1)S(1)}, u32[]{:S(2)}) copy-start(bf16[1024,768]{0,1:T(8,128)(2,1)S(1)} %copy.37) | copy-start | bytes 4718596
  210.0 11.4 %copy-start.17 = (f32[512,768]{1,0:T(8,128)S(1)}, f32[512,768]{1,0:T(8,128)}, u32[]{:S(2)}) copy-start(f32[512,768]{1,0:T(8,128)} %get-tuple-element.50) | copy-start | bytes 4718596
  210.1 11.4 %copy-start.24 = (bf16[72,8,768]{2,1,0:T(8,128)(2,1)S(1)}, bf16[72,8,768]{2,1,0:T(8,128)(2,1)}, u32[]{:S(2)}) copy-start(bf16[72,8,768]{2,1,0:T(8,128)(2,1)} %slice.349) | copy-start | bytes 2654212
  221.4 20.8 %copy-start.50 = (bf16[12,64,512]{2,1,0:T(8,128)(2,1)}, bf16[12,64,512]{2,1,0:T(8,128)(2,1)S(1)}, u32[]{:S(2)}) copy-start(bf16[12,64,512]{2,1,0:T(8,128)(2,1)S(1)} %fusion.45) | copy-start | bytes 2359300
  222.4 43.9 %copy-start.11 = (f32[512,768]{1,0:T(8,128)}, f32[512,768]{1,0:T(8,128)S(1)}, u32[]{:S(2)}) copy-start(f32[512,768]{1,0:T(8,128)S(1)} %get-tuple-element.54) | copy-start | bytes 4718596
  288.1 16.6 %copy-start.7 = (bf16[512,768]{0,1:T(8,128)(2,1)S(1)}, bf16[512,768]{0,1:T(8,128)(2,1)}, u32[]{:S(2)}) copy-start(bf16[512,768]{0,1:T(8,128)(2,1)} %copy-done.6) | copy-start | bytes 2359300
  309.7 89.8 %reduce-scatter.5.cloned.1.call-start = ((), (), s32[]{:S(2)}) async-start(), calls=%async_computation.3 | async-start | bytes 2359296 | tf_op jit(solution)/shard_map/reduce_scatter | solution.py:1042
  336.7 11.7 %copy-start.5 = (s32[512,1024]{0,1:T(8,128)S(1)}, s32[512,1024]{0,1:T(8,128)}, u32[]{:S(2)}) copy-start(s32[512,1024]{0,1:T(8,128)} %copy-done.4) | copy-start | bytes 6291460
  348.5 12.9 %copy-start.3 = (bf16[1024,768]{0,1:T(8,128)(2,1)S(1)}, bf16[1024,768]{0,1:T(8,128)(2,1)}, u32[]{:S(2)}) copy-start(bf16[1024,768]{0,1:T(8,128)(2,1)} %copy-done.2) | copy-start | bytes 4718596
  411.9 20.4 %slice-start = ((s8[4718592]{0:T(1024)(128)(4,1)}), s8[524288]{0:T(1024)(128)(4,1)S(1)}, s32[]{:S(2)}) async-start(s8[4718592]{0:T(1024)(128)(4,1)} %bitcast.306), calls=%async_computation.6 | async-start | bytes 1048576
  418.6 13.6 %slice-start.1 = ((s8[4718592]{0:T(1024)(128)(4,1)}), s8[4194304]{0:T(1024)(128)(4,1)S(1)}, s32[]{:S(2)}) async-start(s8[4718592]{0:T(1024)(128)(4,1)} %bitcast.306), calls=%async_computation.7 | async-start | bytes 8388608
  (38 other events, 238.2 us)
Sparse Core Ops, SparseCore 0:
  90.9 9.6 all-gather.6
  114.2 9.6 all-gather.4
  309.9 8.7 reduce-scatter.2
  361.4 8.9 reduce-scatter.4
where the time goes:
time: 562 us; the launch traced here: 555 us
  matrix products  178 us (32%)
  Pallas kernels  172 us (31%)
  local copies, waits for them, and re-layouts  144 us (26%)
  other arithmetic  41.1 us (7%)
  between operations  17.4 us (3%)
    pallas_call x1, Pallas kernels, reduce_and_step(): pl.pallas_call(reduce_kernel, out_shape=[jax.ShapeDtypeStruct((ROWS, 128)...  99.6 us
    pallas_call x1, Pallas kernels, gather_weights(): pl.pallas_call(gather_kernel, out_shape=jax.ShapeDtypeStruct((16, CHIP, 8...  72.8 us
    unnamed x161, local copies, waits for them, and re-layouts  58.3 us
    dot_general x7, matrix products, matmul_low(): return jnp.dot(left, right, preferred_element_type=jnp.float32)  33.3 us
    dot_general x1, local copies, waits for them, and re-layouts, per_device(): jnp.einsum('bh,cbqk->chqk', entry_part.bias_table, onehot, preferred_elem...  30.4 us
    another operation x2, local copies, waits for them, and re-layouts  23.3 us
    dot_general x1, matrix products, per_device(): jnp.einsum('cqhd,ckhd->chqk', grad_context, value_heads, preferred_elemen...  18.1 us
    another operation x1, other arithmetic  16.6 us
  transfers between devices with their start and end apart: 4, of which 0 were waited for; matrix products, arithmetic and copies ran while one was open for 36% of the time, Pallas kernels for 0%

commit v1 on v0

--- a/solution.py
+++ b/solution.py
@@ -1,7 +1,5 @@
-from types import SimpleNamespace
-from typing import Any, NamedTuple
-
 import functools
+
 import jax
 import jax.numpy as jnp
 from jax import lax
@@ -34,27 +32,6 @@
 masked_score = -1000000000.0
 
 
-class Params(NamedTuple):
-    layout_weight: Any
-    layout_bias: Any
-    bias_table: Any
-    query_weight: Any
-    query_bias: Any
-    key_weight: Any
-    value_weight: Any
-    value_bias: Any
-    output_weight: Any
-    output_bias: Any
-    first_gain: Any
-    first_shift: Any
-    up_weight: Any
-    up_bias: Any
-    down_weight: Any
-    down_bias: Any
-    second_gain: Any
-    second_shift: Any
-
-
 SHAPES = (
     (LF, D), (D,), (BUCKETS, H),
     (D, D), (D,), (D, D), (D, D), (D,), (D, D), (D,), (D,), (D,),
@@ -68,42 +45,7 @@
         amount = shape[0] * (shape[1] if len(shape) > 1 else 1)
         pieces.append(flat_params[offset : offset + amount].reshape(shape))
         offset = offset + amount
-    return Params(*pieces)
-
-
-def as_float(piece):
-    return piece.astype(jnp.float32)
-
-
-def matmul_low(left, right):
-    return jnp.dot(left, right, preferred_element_type=jnp.float32)
-
-
-def layer_norm(values, gain, shift):
-    center = values - jnp.mean(values, axis=-1, keepdims=True)
-    spread = jnp.mean(center * center, axis=-1, keepdims=True)
-    return center * lax.rsqrt(spread + norm_eps) * gain + shift
-
-
-def gelu_exact(values):
-    return jax.nn.gelu(values, approximate=False)
-
-
-def layout_features(page_boxes):
-    rates_sin = jnp.power(10000.0, -jnp.arange(FREQ, dtype=jnp.float32) / FREQ)
-    angles = page_boxes.astype(jnp.float32)[:, :, None] * rates_sin
-    stacked = jnp.stack([jnp.sin(angles), jnp.cos(angles)], axis=1)
-    return jnp.transpose(stacked, (2, 0, 1, 3)).reshape(page_boxes.shape[1], LF)
-
-
-def attention_scores(query_low, key_all, score_bias, allowed, blocks_here, rows):
-    query_heads = query_low.reshape(blocks_here, rows, H, HD)
-    key_heads = key_all.reshape(blocks_here, BLOCK, H, HD)
-    products = (
-        jnp.einsum("cqhd,ckhd->chqk", query_heads, key_heads, preferred_element_type=jnp.float32)
-        + score_bias
-    )
-    return jnp.where(allowed, products, masked_score)
+    return pieces
 
 
 def adam_update(master, first_moment, second_moment, gradient, global_index):
@@ -123,12 +65,11 @@
     return (param_step, moment_one, moment_two)
 
 
-def running_sum(lengths):
-    total, sums = lengths[:, :1], [lengths[:, :1]]
-    for i in range(1, lengths.shape[1]):
-        total = total + lengths[:, i : i + 1]
-        sums.append(total)
-    return jnp.concatenate(sums, axis=1)
+def layout_features(page_boxes):
+    rates_sin = jnp.power(10000.0, -jnp.arange(FREQ, dtype=jnp.float32) / FREQ)
+    angles = page_boxes.astype(jnp.float32)[:, :, None] * rates_sin
+    stacked = jnp.stack([jnp.sin(angles), jnp.cos(angles)], axis=1)
+    return jnp.transpose(stacked, (2, 0, 1, 3)).reshape(page_boxes.shape[1], LF)
 
 
 MESH = pl.DeviceIdType.MESH
@@ -785,43 +726,563 @@
 )
 
 
-def vector_slot(chip):
-    return 36 if chip in (0, 4, 5) else 73
-
-
 def slots_of(first, count):
     runs = []
     for w in range(first, first + count):
         chip, at = divmod(w, 73)
         slot = chip * CHIP + at + (1 if at >= vector_slot(chip) else 0)
-        if runs and runs[-1][0] + runs[-1][1] == slot:
-            runs[-1][1] += 1
+        if runs and runs[-1][0] + runs[-1][2] == slot:
+            runs[-1][2] += 1
         else:
-            runs.append([slot, 1])
+            runs.append([slot, w - first, 1])
     return runs
 
 
-def unpack_gathered(gathered):
-    tiles = gathered.reshape(16 * CHIP, 8, D)
-    pieces = {}
+def vector_slot(chip):
+    return 36 if chip in (0, 4, 5) else 73
+
+
+def vector_at(chip):
+    return chip * CHIP + vector_slot(chip)
+
+
+def pieces(tiles, held, first, count, sems, base, out=False):
+    made = []
+    for i, (slot, at, n) in enumerate(slots_of(first, count)):
+        a, b = tiles.at[pl.ds(slot, n)], held.at[pl.ds(at, n)]
+        a, b = (b, a) if out else (a, b)
+        made.append(pltpu.make_async_copy(a, b, sems.at[base + i]))
+    return made
+
+
+def matrix(tile_rows):
+    return tile_rows.reshape(-1, D)
+
+
+def col_sum(v):
+    return jnp.sum(v.reshape(-1, 8, v.shape[-1]), axis=0)
+
+
+def norm_stats(v):
+    mean = jnp.mean(v, axis=-1, keepdims=True)
+    center = v - mean
+    spread = jnp.mean(center * center, axis=-1, keepdims=True)
+    inv = lax.rsqrt(spread + norm_eps)
+    return center * inv, inv
+
+
+def norm_back(grad, gain, hat, inv):
+    g = grad * gain
+    return inv * (g - jnp.mean(g, axis=-1, keepdims=True) - hat * jnp.mean(g * hat, axis=-1, keepdims=True))
+
+
+ROOT_HALF = 0.7071067811865476
+ROOT_TAU = 0.3989422804014327
+
+
+def middle_kernel(tiles, ctx, hidden, cot, act_out, gfi_out, gctx_out, grads,
+                  wo, wup, wdn, vecs, vf, act, slope, low1, hat1, inv1, hat2, inv2, a, sums, dwo, dwup, dwdn, vgrads, lsem, ssem):
+    f32, bf = jnp.float32, jnp.bfloat16
+    rows = ctx.shape[0]
+    R = 64
+    steps = rows // R
+    loads_o = pieces(tiles, wo, 304, 96, lsem, 0)
+    loads_u = pieces(tiles, wup, 400, 384, lsem, 4)
+    loads_d = pieces(tiles, wdn, 784, 384, lsem, 12)
+    loads_v = [pltpu.make_async_copy(tiles.at[vector_at(c)], vecs.at[i], lsem.at[20 + i]) for i, c in enumerate((5, 10, 15))]
+    for c in loads_v + loads_o + loads_u + loads_d:
+        c.start()
+    up4 = wup.reshape(96, 4, 8, D)
+    dup4 = dwup.reshape(96, 4, 8, D)
+
+    def vec(i, r):
+        return vf[i, pl.ds(r, 1), :]
+
+    def each(f):
+        @pl.loop(0, steps)
+        def _(i):
+            f(pl.ds(pl.multiple_of(i * R, R), R))
+
+    for c in loads_v + loads_o:
+        c.wait()
+    vf[...] = vecs[...].astype(f32)
+    a[...] = jnp.dot(ctx[...], matrix(wo[...]), preferred_element_type=f32)
+
+    def first(sl):
+        hat, inv = norm_stats(hidden[sl, :] + a[sl, :] + vec(0, 0))
+        hat1[sl, :] = hat
+        inv1[sl, :] = inv
+        out = hat * vec(0, 1) + vec(0, 2)
+        a[sl, :] = out
+        low1[sl, :] = out.astype(bf)
+
+    each(first)
+    for c in loads_u + loads_d:
+        c.wait()
+
+    def up(j, _):
+        for half in range(2):
+            sl = pl.ds(half * (rows // 2), rows // 2)
+            u = jnp.dot(low1[sl, :], matrix(up4[:, j]), preferred_element_type=f32) + vec(1, j)
+            share = 0.5 * (1.0 + lax.erf(u * ROOT_HALF))
+            act[j, sl, :] = (u * share).astype(bf)
+            slope[j, sl, :] = share + u * jnp.exp(-0.5 * u * u) * ROOT_TAU
+        return 0
+
+    lax.fori_loop(0, 4, up, 0)
+
+    def down(j, _):
+        a[...] += jnp.dot(act[j], matrix(wdn[pl.ds(96 * j, 96)]), preferred_element_type=f32)
+        return 0
+
+    lax.fori_loop(0, 4, down, 0)
+    sums[...] = jnp.zeros_like(sums)
+
+    def second(sl):
+        hat, inv = norm_stats(a[sl, :] + vec(2, 0))
+        act_out[sl, :] = (hat * vec(2, 1) + vec(2, 2)).astype(bf)
+        g = cot[sl, :].astype(f32)
+        sums[6] += col_sum(g * hat)
+        sums[7] += col_sum(g)
+        back = norm_back(g, vec(2, 1), hat, inv)
+        sums[5] += col_sum(back)
+        a[sl, :] = back
+        hat2[sl, :] = back.astype(bf)
+
+    each(second)
+    down_back = hat2
+
+    def back(j, _):
+        for half in range(2):
+            sl = pl.ds(half * (rows // 2), rows // 2)
+            g = lax.dot_general(down_back[sl, :], matrix(wdn[pl.ds(96 * j, 96)]), NT, preferred_element_type=f32) * slope[j, sl, :]
+            sums[8 + j] += col_sum(g)
+            act_back[sl, :] = g.astype(bf)
+        dwdn[pl.ds(96 * j, 96)] = lax.dot_general(act[j], down_back[...], TN, preferred_element_type=f32).astype(bf).reshape(96, 8, D)
+        dup4[:, j] = lax.dot_general(low1[...], act_back[...], TN, preferred_element_type=f32).astype(bf).reshape(96, 8, D)
+        a[...] += lax.dot_general(act_back[...], matrix(up4[:, j]), NT, preferred_element_type=f32)
+        return 0
+
+    act_back = inv2
+    lax.fori_loop(0, 4, back, 0)
+    stores = pieces(grads, dwup, 400, 384, ssem, 4, True) + pieces(grads, dwdn, 784, 384, ssem, 12, True)
+    for c in stores:
+        c.start()
+
+    def third(sl):
+        g = a[sl, :]
+        sums[3] += col_sum(g * hat1[sl, :])
+        sums[4] += col_sum(g)
+        back = norm_back(g, vec(0, 1), hat1[sl, :], inv1[sl, :])
+        sums[2] += col_sum(back)
+        gfi_out[sl, :] = back
+        hat2[sl, :] = back.astype(bf)
+
+    each(third)
+    gctx_out[...] = lax.dot_general(hat2[...], matrix(wo[...]), NT, preferred_element_type=f32).astype(bf)
+    dwo[...] = lax.dot_general(ctx[...], hat2[...], TN, preferred_element_type=f32).astype(bf).reshape(96, 8, D)
+    for i, held in enumerate(((2, 3, 4), (8, 9, 10, 11), (5, 6, 7))):
+        lines = [jnp.sum(sums[s], axis=0, keepdims=True) for s in held]
+        lines.append(jnp.zeros((8 - len(held), D), f32))
+        vgrads[i] = jnp.concatenate(lines).astype(bf)
+    last = pieces(grads, dwo, 304, 96, ssem, 0, True)
+    last += [pltpu.make_async_copy(vgrads.at[i], grads.at[vector_at(c)], ssem.at[20 + i]) for i, c in enumerate((5, 10, 15))]
+    for c in last:
+        c.start()
+    for c in stores + last:
+        c.wait()
+
+
+def middle(tiles, ctx, hidden, cot):
+    rows = ctx.shape[0]
+    f32, bf = jnp.float32, jnp.bfloat16
+    vm, any_ = pl.BlockSpec(memory_space=pltpu.VMEM), pl.BlockSpec(memory_space=pl.ANY)
+    S = jax.ShapeDtypeStruct
+    return pl.pallas_call(
+        middle_kernel,
+        out_shape=[S((rows, D), bf), S((rows, D), f32), S((rows, D), bf), S((16 * CHIP, 8, D), bf)],
+        in_specs=[any_, vm, vm, vm],
+        out_specs=[vm, vm, vm, any_],
+        scratch_shapes=[
+            pltpu.VMEM((96, 8, D), bf), pltpu.VMEM((384, 8, D), bf), pltpu.VMEM((384, 8, D), bf), pltpu.VMEM((3, 8, D), bf), pltpu.VMEM((3, 8, D), f32),
+            pltpu.VMEM((4, rows, D), bf), pltpu.VMEM((4, rows, D), f32), pltpu.VMEM((rows, D), bf),
+            pltpu.VMEM((rows, D), f32), pltpu.VMEM((rows, 1), f32), pltpu.VMEM((rows, D), bf), pltpu.VMEM((rows, D), bf),
+            pltpu.VMEM((rows, D), f32), pltpu.VMEM((12, 8, D), f32),
+            pltpu.VMEM((96, 8, D), bf), pltpu.VMEM((384, 8, D), bf), pltpu.VMEM((384, 8, D), bf), pltpu.VMEM((3, 8, D), bf),
+            pltpu.SemaphoreType.DMA((24,)), pltpu.SemaphoreType.DMA((24,)),
+        ],
+        compiler_params=pltpu.CompilerParams(vmem_limit_bytes=58 << 20),
+        name="middle",
+    )(tiles, ctx, hidden, cot)
+
+
+NT = (((1,), (1,)), ((), ()))
+TN = (((0,), (0,)), ((), ()))
+
+
+def half(ref_value, hh):
+    lanes = lax.broadcasted_iota(jnp.int32, ref_value.shape, 1)
+    keep = lanes < 64 if hh == 0 else lanes >= 64
+    return jnp.where(keep, ref_value, jnp.zeros_like(ref_value))
+
+
+def page_of(at, lengths):
+    end, page = 0, jnp.zeros(at.shape, jnp.int32)
+    for i in range(4):
+        end = end + lengths[0, i]
+        page = page + jnp.where(at >= end, 1, 0)
+    return page
+
+
+def attend_kernel(lengths, q_ref, k_ref, v_ref, buckets, pads, lines, ctx_ref, p_ref, code_ref, s_scr, tab_ref):
+    pair = pl.program_id(0)
+    keys, rows = s_scr.shape
+    f32, bf = jnp.float32, jnp.bfloat16
+
+    @pl.when(pair == 0)
+    def _():
+        own = lax.axis_index("seq") * rows
+        tag = page_of(lax.broadcasted_iota(jnp.int32, (1, keys), 1), lengths) + 1
+        tag = jnp.where(jnp.concatenate([pads[0, 0:1], pads[1, 0:1]], axis=1) > 0, tag, 0)
+        for i in range(rows // 128):
+            at = own + 128 * i + lax.broadcasted_iota(jnp.int32, (128, 1), 0)
+            page = page_of(at, lengths) + 1
+            for j in range(keys // 128):
+                key_at = 128 * j + lax.broadcasted_iota(jnp.int32, (1, 128), 1)
+                allowed = (page == tag[:, 128 * j : 128 * j + 128]) | (key_at == at)
+                code = jnp.where(allowed, buckets[128 * i : 128 * i + 128, 128 * j : 128 * j + 128], BUCKETS)
+                code_ref[128 * j : 128 * j + 128, 128 * i : 128 * i + 128] = code.T
+        head = lax.broadcasted_iota(jnp.int32, (16, 128), 0)
+        bucket = lax.broadcasted_iota(jnp.int32, (16, 128), 1)
+        place_of = bucket * H + head
+        tab = jnp.full((16, 128), masked_score, f32)
+        for i in range(BUCKETS * H // 128):
+            row = jnp.broadcast_to(lines[1:2, 128 * i : 128 * i + 128].astype(f32), (16, 128))
+            inside = jnp.clip(place_of - 128 * i, 0, 127)
+            got = jnp.take_along_axis(row, inside, axis=1, mode="promise_in_bounds")
+            tab = jnp.where((place_of // 128 == i) & (bucket < BUCKETS) & (head < H), got, tab)
+        tab_ref[...] = tab
+    STEP_ROWS = keys
+    out = []
+    vt = v_ref[...].T
+    for hh in range(2):
+        qm = half(q_ref[...], hh)
+        line = jnp.broadcast_to(tab_ref[pl.ds(2 * pair + hh, 1), :], (STEP_ROWS, 128))
+
+        def score(i, top):
+            at = pl.multiple_of(i * STEP_ROWS, STEP_ROWS)
+            s = lax.dot_general(k_ref[pl.ds(at, STEP_ROWS), :], qm, NT, preferred_element_type=f32)
+            cols = []
+            for j in range(rows // 128):
+                code = code_ref[pl.ds(at, STEP_ROWS), 128 * j : 128 * j + 128]
+                bias = jnp.take_along_axis(line, code, axis=1, mode="promise_in_bounds")
+                cols.append(jnp.where(bias < 0.5 * masked_score, masked_score, s[:, 128 * j : 128 * j + 128] + bias))
+            s = jnp.concatenate(cols, axis=1)
+            s_scr[pl.ds(at, STEP_ROWS), :] = s
+            return jnp.maximum(top, jnp.max(s.reshape(STEP_ROWS // 8, 8, rows), axis=0))
+
+        top = lax.fori_loop(0, keys // STEP_ROWS, score, jnp.full((8, rows), -jnp.inf, f32))
+        top = jnp.max(top, axis=0, keepdims=True)
+
+        def expo(i, total):
+            at = pl.multiple_of(i * STEP_ROWS, STEP_ROWS)
+            e = jnp.exp(s_scr[pl.ds(at, STEP_ROWS), :] - top)
+            s_scr[pl.ds(at, STEP_ROWS), :] = e
+            return total + jnp.sum(e.reshape(STEP_ROWS // 8, 8, rows), axis=0)
+
+        total = lax.fori_loop(0, keys // STEP_ROWS, expo, jnp.zeros((8, rows), f32))
+        inverse = 1.0 / jnp.sum(total, axis=0, keepdims=True)
+
+        def scale(i, _):
+            at = pl.multiple_of(i * STEP_ROWS, STEP_ROWS)
+            p_ref[hh, pl.ds(at, STEP_ROWS), :] = (s_scr[pl.ds(at, STEP_ROWS), :] * inverse).astype(bf)
+            return 0
+
+        lax.fori_loop(0, keys // STEP_ROWS, scale, 0)
+        out.append(jnp.dot(vt, p_ref[hh], preferred_element_type=f32))
+    sub = lax.broadcasted_iota(jnp.int32, out[0].shape, 0)
+    ctx_ref[...] = jnp.where(sub < 64, out[0], out[1]).T.astype(bf)
+
+
+def attend(query, key_all, value_all, buckets, page_lengths, pads, lines):
+    rows, keys = query.shape[0], key_all.shape[0]
+    bf = jnp.bfloat16
+    const = lambda p: (0, 0)
+    return pl.pallas_call(
+        attend_kernel,
+        grid=(H // 2,),
+        out_shape=[
+            jax.ShapeDtypeStruct((rows, D), bf),
+            jax.ShapeDtypeStruct((H, keys, rows), bf),
+            jax.ShapeDtypeStruct((keys, rows), jnp.int32),
+        ],
+        in_specs=[
+            pl.BlockSpec(memory_space=pltpu.SMEM),
+            pl.BlockSpec((rows, 128), lambda p: (0, p)),
+            pl.BlockSpec((keys, 128), lambda p: (0, p)),
+            pl.BlockSpec((keys, 128), lambda p: (0, p)),
+            pl.BlockSpec((rows, keys), const),
+            pl.BlockSpec((2, 8, rows), lambda p: (0, 0, 0)),
+            pl.BlockSpec((8, D), const),
+        ],
+        out_specs=[pl.BlockSpec((rows, 128), lambda p: (0, p)), pl.BlockSpec((2, keys, rows), lambda p: (p, 0, 0)), pl.BlockSpec((keys, rows), const)],
+        scratch_shapes=[pltpu.VMEM((keys, rows), jnp.float32), pltpu.VMEM((16, 128), jnp.float32)],
+        compiler_params=pltpu.CompilerParams(vmem_limit_bytes=56 << 20),
+        name="attend",
+    )(page_lengths, query, key_all, value_all, buckets, pads, lines)
+
+
+def attend_back_kernel(q_ref, k_ref, v_ref, do_ref, p_ref, code_ref, dq_ref, dk_ref, dv_ref, tab_ref, spread, held):
+    pair = pl.program_id(0)
+    keys, rows = code_ref.shape
+    f32, bf = jnp.float32, jnp.bfloat16
+    STEP_ROWS = keys
+    kt = k_ref[...].T
+    dq = []
+    for hh in range(2):
+        qm = half(q_ref[...], hh)
+        dom = half(do_ref[...], hh)
+
+        def inner(i, total):
+            at = pl.multiple_of(i * STEP_ROWS, STEP_ROWS)
+            g = lax.dot_general(v_ref[pl.ds(at, STEP_ROWS), :], dom, NT, preferred_element_type=f32)
+            w = g * p_ref[hh, pl.ds(at, STEP_ROWS), :].astype(f32)
+            return total + jnp.sum(w.reshape(STEP_ROWS // 8, 8, rows), axis=0)
+
+        total = lax.fori_loop(0, keys // STEP_ROWS, inner, jnp.zeros((8, rows), f32))
+        total = jnp.sum(total, axis=0, keepdims=True)
+
+        def grads(i, acc):
+            at = pl.multiple_of(i * STEP_ROWS, STEP_ROWS)
+            sl = pl.ds(at, STEP_ROWS)
+            g = lax.dot_general(v_ref[sl, :], dom, NT, preferred_element_type=f32)
+            p = p_ref[hh, sl, :]
+            ds = p.astype(f32) * (g - total)
+            wide = ds.reshape(STEP_ROWS // 8, 8, rows)
+            if hh == 0:
+                held[...] = wide
+            else:
+                both = jnp.concatenate([held[...], wide], axis=1).astype(bf)
+                spread[:, pl.ds(pl.multiple_of(pair * 16, 16), 16), :] = both
+            ds = ds.astype(bf)
+            dv = jnp.dot(p, dom, preferred_element_type=f32)
+            dk = jnp.dot(ds, qm, preferred_element_type=f32)
+            if hh == 0:
+                dv_ref[sl, :] = dv
+                dk_ref[sl, :] = dk
+            else:
+                dv_ref[sl, :] += dv
+                dk_ref[sl, :] += dk
+            return acc + lax.dot_general(k_ref[sl, :], ds, TN, preferred_element_type=f32)
+
+        dq.append(lax.fori_loop(0, keys // STEP_ROWS, grads, jnp.zeros((128, rows), f32)))
+    sub = lax.broadcasted_iota(jnp.int32, dq[0].shape, 0)
+    dq_ref[...] = jnp.where(sub < 64, dq[0], dq[1]).T * 0.125
+
+    @pl.when(pair == H // 2 - 1)
+    def _():
+        bucket = lax.broadcasted_iota(jnp.int32, (BUCKETS, rows), 0)
+
+        def count(i, acc):
+            code = code_ref[pl.ds(pl.multiple_of(i * 8, 8), 8), :]
+            hot = jnp.concatenate(
+                [jnp.where(jnp.broadcast_to(code[r : r + 1], bucket.shape) == bucket, 1.0, 0.0) for r in range(8)]
+            ).astype(bf)
+            return acc + lax.dot_general(spread[i], hot, NT, preferred_element_type=f32)
+
+        acc = lax.fori_loop(0, keys // 8, count, jnp.zeros((8 * H, 8 * BUCKETS), f32), unroll=8)
+        a = lax.broadcasted_iota(jnp.int32, acc.shape, 0) % 8
+        b = lax.broadcasted_iota(jnp.int32, acc.shape, 1) // BUCKETS
+        acc = jnp.where(a == b, acc, 0.0)
+        heads = jnp.sum(acc.reshape(H, 8, 8 * BUCKETS), axis=1)
+        lane = lax.broadcasted_iota(jnp.int32, (8 * BUCKETS, D), 1) // H
+        wide = jnp.where(lane == lax.broadcasted_iota(jnp.int32, lane.shape, 0) % BUCKETS, 1.0, 0.0)
+        out = jnp.dot(heads, wide, precision=lax.Precision.HIGHEST, preferred_element_type=f32)
+        mine = lax.broadcasted_iota(jnp.int32, out.shape, 1) % H == lax.broadcasted_iota(jnp.int32, out.shape, 0)
+        out = jnp.sum(jnp.where(mine, out, 0.0), axis=0, keepdims=True)
+        tab_ref[...] = jnp.broadcast_to(out, tab_ref.shape)
+
+
+def soft_back(query, key_all, value_all, grad_context, soft, code):
+    rows, keys = query.shape[0], key_all.shape[0]
+    f32 = jnp.float32
+    row = pl.BlockSpec((rows, 128), lambda p: (0, p))
+    key = pl.BlockSpec((keys, 128), lambda p: (0, p))
+    dq, dk, dv, tab = pl.pallas_call(
+        attend_back_kernel,
+        grid=(H // 2,),
+        out_shape=[
+            jax.ShapeDtypeStruct((rows, D), f32),
+            jax.ShapeDtypeStruct((keys, D), f32),
+            jax.ShapeDtypeStruct((keys, D), f32),
+            jax.ShapeDtypeStruct((8, D), f32),
+        ],
+        in_specs=[row, key, key, row, pl.BlockSpec((2, keys, rows), lambda p: (p, 0, 0)), pl.BlockSpec((keys, rows), lambda p: (0, 0))],
+        out_specs=[row, key, key, pl.BlockSpec((8, D), lambda p: (0, 0))],
+        scratch_shapes=[pltpu.VMEM((keys // 8, 8 * H, rows), jnp.bfloat16), pltpu.VMEM((keys // 8, 8, rows), f32)],
+        compiler_params=pltpu.CompilerParams(vmem_limit_bytes=58 << 20),
+        name="attend_back",
+    )(query, key_all, value_all, grad_context, soft, code)
+    return dq, dk, dv, tab
+
+
+def meet_partner():
+    dp, c = lax.axis_index("dp"), lax.axis_index("seq")
+    partner = (dp, 1 - c)
+    bar = pltpu.get_barrier_semaphore()
+    pl.semaphore_signal(bar, inc=1, device_id=partner, device_id_type=MESH)
+    pl.semaphore_wait(bar, 1)
+    return c, partner
+
+
+def enter_kernel(tiles, tokens, feats, pad, hidden, low, query, keys, values, pads, wl, wq, wk, wv, vecs, vf, lsem, sends, recvs):
+    f32, bf = jnp.float32, jnp.bfloat16
+    rows = tokens.shape[0]
+    loads = [pltpu.make_async_copy(tiles.at[vector_at(ch)], vecs.at[i], lsem.at[i]) for i, ch in enumerate((0, 1, 4))]
+    loads += pieces(tiles, wl, 0, 16, lsem, 4) + pieces(tiles, wk, 112, 96, lsem, 8)
+    loads += pieces(tiles, wv, 208, 96, lsem, 12) + pieces(tiles, wq, 16, 96, lsem, 16)
+    for c in loads:
+        c.start()
+    c, partner = meet_partner()
+    own = pl.ds(c * rows, rows)
+
+    def share(ref, i):
+        return rcopy(ref.at[own], ref.at[own], sends.at[i], recvs.at[i], partner)
+
+    pads[pl.ds(c, 1)] = pad[...].reshape(1, 8, rows)
+    pair_pads = rcopy(pads.at[pl.ds(c, 1)], pads.at[pl.ds(c, 1)], sends.at[2], recvs.at[2], partner)
+    pair_pads.start()
+    for copy in loads:
+        copy.wait()
+    vf[...] = vecs[...].astype(f32)
+    h = tokens[...].astype(f32) + jnp.dot(feats[...], matrix(wl[...]), preferred_element_type=f32) + vf[0, 0:1, :]
+    hidden[...] = h
+    low[...] = h.astype(bf)
+    keys[own, :] = jnp.dot(low[...], matrix(wk[...]), preferred_element_type=f32).astype(bf)
+    send_keys = share(keys, 0)
+    send_keys.start()
+    values[own, :] = (jnp.dot(low[...], matrix(wv[...]), preferred_element_type=f32) + vf[2, 0:1, :]).astype(bf)
+    send_values = share(values, 1)
+    send_values.start()
+    query[...] = ((jnp.dot(low[...], matrix(wq[...]), preferred_element_type=f32) + vf[1, 0:1, :]) * 0.125).astype(bf)
+    for copy in (pair_pads, send_keys, send_values):
+        copy.wait()
+
+
+def enter(tiles, tokens, feats, pad):
+    rows = tokens.shape[0]
+    f32, bf = jnp.float32, jnp.bfloat16
+    vm, any_ = pl.BlockSpec(memory_space=pltpu.VMEM), pl.BlockSpec(memory_space=pl.ANY)
+    S, sem = jax.ShapeDtypeStruct, pltpu.SemaphoreType.DMA
+    w = pltpu.VMEM((96, 8, D), bf)
+    return pl.pallas_call(
+        enter_kernel,
+        out_shape=[S((rows, D), f32), S((rows, D), bf), S((rows, D), bf), S((2 * rows, D), bf), S((2 * rows, D), bf), S((2, 8, rows), jnp.int32)],
+        in_specs=[any_, vm, vm, vm],
+        out_specs=[vm] * 6,
+        scratch_shapes=[pltpu.VMEM((16, 8, D), bf), w, w, w, pltpu.VMEM((3, 8, D), bf), pltpu.VMEM((3, 8, D), f32), sem((20,)), sem((3,)), sem((3,))],
+        compiler_params=pltpu.CompilerParams(collective_id=2, has_side_effects=True, vmem_limit_bytes=40 << 20),
+        name="enter",
+    )(tiles, tokens, feats, pad)
+
+
+def leave_kernel(tiles, dq, dk, dv, gfi, low, feats, table, grads_in, input_grad, grads,
+                 wq, wk, wv, out, come, back, dwl, dwq, dwk, dwv, vgrads, lsem, ssem, sends, recvs):
+    f32, bf = jnp.float32, jnp.bfloat16
+    rows = gfi.shape[0]
+    loads = pieces(tiles, wk, 112, 96, lsem, 0) + pieces(tiles, wv, 208, 96, lsem, 4) + pieces(tiles, wq, 16, 96, lsem, 8)
+    for c in loads:
+        c.start()
+    c, partner = meet_partner()
+    own, other = pl.ds(c * rows, rows), pl.ds((1 - c) * rows, rows)
+    swaps = []
+    for i, ref in enumerate((dk, dv)):
+        out[i] = ref[other, :].astype(bf)
+        swaps.append(rcopy(out.at[i], come.at[i], sends.at[i], recvs.at[i], partner))
+        swaps[i].start()
+    back[0] = dq[...].astype(bf)
+    query_bias = jnp.sum(col_sum(dq[...]), axis=0, keepdims=True)
+    for copy in loads:
+        copy.wait()
+
+    def through(i, w, dw):
+        dw[...] = lax.dot_general(low[...], back[i], TN, preferred_element_type=f32).astype(bf).reshape(96, 8, D)
+        return lax.dot_general(back[i], matrix(w[...]), NT, preferred_element_type=f32)
+
+    input_grad[...] = gfi[...] + through(0, wq, dwq)
+    stores = pieces(grads, dwq, 16, 96, ssem, 0, True)
+    swaps[0].wait_recv()
+    back[1] = (dk[own, :] + come[0].astype(f32)).astype(bf)
+    input_grad[...] += through(1, wk, dwk)
+    stores += pieces(grads, dwk, 112, 96, ssem, 4, True)
+    swaps[1].wait_recv()
+    grad_value = dv[own, :] + come[1].astype(f32)
+    value_bias = jnp.sum(col_sum(grad_value), axis=0, keepdims=True)
+    back[2] = grad_value.astype(bf)
+    total = input_grad[...] + through(2, wv, dwv)
+    stores += pieces(grads, dwv, 208, 96, ssem, 8, True)
+    input_grad[...] = total
+    layout_bias = jnp.sum(col_sum(total), axis=0, keepdims=True)
+    dwl[...] = lax.dot_general(feats[...], total.astype(bf), TN, preferred_element_type=f32).astype(bf).reshape(16, 8, D)
+    stores += pieces(grads, dwl, 0, 16, ssem, 12, True)
+
+    def block(lines):
+        return jnp.concatenate(lines + [jnp.zeros((8 - len(lines), D), f32)]).astype(bf)
+
+    vgrads[0] = block([layout_bias, table[0:1, :]])
+    vgrads[1] = block([query_bias])
+    vgrads[2] = block([value_bias])
+    vgrads[3] = jnp.zeros((8, D), bf)
+    held = {0: 0, 1: 1, 4: 2}
+    for i, chip in enumerate(ch for ch in range(16) if ch not in (5, 10, 15)):
+        stores.append(pltpu.make_async_copy(vgrads.at[held.get(chip, 3)], grads.at[vector_at(chip)], ssem.at[16 + i]))
+    for copy in stores:
+        copy.start()
+    for copy in stores:
+        copy.wait()
+    for swap in swaps:
+        swap.wait_send()
+
+
+def leave(tiles, dq, dk, dv, gfi, low, feats, table, grads):
+    rows = gfi.shape[0]
+    f32, bf = jnp.float32, jnp.bfloat16
+    vm, any_ = pl.BlockSpec(memory_space=pltpu.VMEM), pl.BlockSpec(memory_space=pl.ANY)
+    S, sem = jax.ShapeDtypeStruct, pltpu.SemaphoreType.DMA
+    w = pltpu.VMEM((96, 8, D), bf)
+    return pl.pallas_call(
+        leave_kernel,
+        out_shape=[S((rows, D), f32), S(grads.shape, bf)],
+        in_specs=[any_] + [vm] * 7 + [any_],
+        out_specs=[vm, any_],
+        scratch_shapes=[w, w, w, pltpu.VMEM((2, rows, D), bf), pltpu.VMEM((2, rows, D), bf), pltpu.VMEM((3, rows, D), bf),
+                        pltpu.VMEM((16, 8, D), bf), w, w, w, pltpu.VMEM((4, 8, D), bf), sem((12,)), sem((32,)), sem((2,)), sem((2,))],
+        input_output_aliases={8: 1},
+        compiler_params=pltpu.CompilerParams(collective_id=3, has_side_effects=True, vmem_limit_bytes=56 << 20),
+        name="leave",
+    )(tiles, dq, dk, dv, gfi, low, feats, table, grads)
+
+
+def from_tiles(tiles):
+    got = {}
     for name, first, count in WEIGHTS:
-        got = jnp.concatenate([tiles[s : s + n] for s, n in slots_of(first, count)])
+        block = jnp.concatenate([tiles[s : s + n] for s, _, n in slots_of(first, count)])
         if name == 12:
-            got = got.reshape(96, 4, 8, D).transpose(0, 2, 1, 3).reshape(D, FF)
-        pieces[name] = got.reshape(-1, FF if name == 12 else D)
+            block = block.reshape(96, 4, 8, D).transpose(0, 2, 1, 3)
+        got[name] = block.reshape(-1, FF if name == 12 else D)
     for name, chip, row in VECTORS:
-        block = gathered[chip, vector_slot(chip)]
+        block = tiles[vector_at(chip)]
         if name == 13:
-            pieces[name] = block[row : row + 4].reshape(FF)
+            got[name] = block[row : row + 4].reshape(FF)
         elif name == 2:
-            pieces[name] = block[row, : BUCKETS * H].reshape(BUCKETS, H)
+            got[name] = block[row, : BUCKETS * H].reshape(BUCKETS, H)
         else:
-            pieces[name] = block[row]
-    return Params(*[pieces[i] for i in range(18)])
-
-
-def pack_gradients(pieces):
-    by_name = [p.astype(jnp.bfloat16) for p in pieces]
+            got[name] = block[row]
+    return [got[i] for i in range(18)]
+
+
+def to_tiles(whole):
+    by_name = [p.astype(jnp.bfloat16) for p in whole]
     weights = []
     for name, first, count in WEIGHTS:
         got = by_name[name]
@@ -844,277 +1305,35 @@
             at = w
         parts.append(tiles[at - first :])
     parts.extend(block for w, block in cuts if w == 1168)
-    return jnp.concatenate(parts).reshape(16, CHIP, 8, D)
+    return jnp.concatenate(parts)
 
 
 def per_device(
-    custom,
-    tokens,
-    cotangent,
-    page_boxes,
-    page_lengths,
-    padding,
-    buckets,
-    master,
-    first_moment,
-    second_moment,
+    custom, tokens, cotangent, page_boxes, page_lengths, padding, buckets, master, first_moment, second_moment
 ):
-    blocks_here = tokens.shape[0]
     rows = tokens.shape[1]
-    count_rows = blocks_here * rows
     if custom:
-        entry_part = unpack_gathered(gather_weights(master))
+        tiles = gather_weights(master).reshape(16 * CHIP, 8, D)
     else:
-        shard_low = master.astype(jnp.bfloat16)
-        flat_params = lax.all_gather(shard_low, ("dp", "seq"), axis=0, tiled=True)
-        entry_part = unpack(flat_params)
-    layers = [entry_part]
-    places = lax.axis_index("seq") * rows + jnp.arange(rows, dtype=jnp.int32)
-    page_ends = running_sum(page_lengths)
-    page_of = jnp.sum((places[None, :, None] >= page_ends[:, None, :]).astype(jnp.int32), axis=2)
-    own_tags = jnp.where(padding > 0, page_of + 1, 0).astype(jnp.bfloat16)
-    query_tags = (page_of + 1).astype(jnp.float32)
-    key_places = jnp.arange(BLOCK, dtype=jnp.int32)
-    bucket_ids = jnp.arange(BUCKETS, dtype=jnp.int32)
-    onehot = (buckets[:, None, :, :] == bucket_ids[None, :, None, None]).astype(jnp.bfloat16)
-    score_bias = jnp.einsum(
-        "bh,cbqk->chqk", entry_part.bias_table, onehot, preferred_element_type=jnp.float32
-    )
-    features_low = layout_features(page_boxes.reshape(4, count_rows)).astype(jnp.bfloat16)
-    hidden = (
-        tokens.reshape(count_rows, D).astype(jnp.float32)
-        + matmul_low(features_low, entry_part.layout_weight)
-        + as_float(entry_part.layout_bias)
-    )
-    saved = []
-    for weights in layers:
-        inputs_low = hidden.astype(jnp.bfloat16)
-        query_low = (
-            (matmul_low(inputs_low, weights.query_weight) + as_float(weights.query_bias))
-            * 0.125
-        ).astype(jnp.bfloat16)
-        key_low = matmul_low(inputs_low, weights.key_weight).astype(jnp.bfloat16)
-        value_low = (
-            matmul_low(inputs_low, weights.value_weight) + as_float(weights.value_bias)
-        ).astype(jnp.bfloat16)
-        key_all, value_all, tags_all = (
-            lax.all_gather(key_low.reshape(blocks_here, rows, D), "seq", axis=1, tiled=True),
-            lax.all_gather(value_low.reshape(blocks_here, rows, D), "seq", axis=1, tiled=True),
-            lax.all_gather(own_tags, "seq", axis=1, tiled=True),
-        )
-        allowed = (tags_all[:, None, :].astype(jnp.float32) == query_tags[:, :, None]) | (
-            key_places[None, None, :] == places[None, :, None]
-        )
-        allowed = allowed[:, None, :, :]
-        scores = attention_scores(query_low, key_all, score_bias, allowed, blocks_here, rows)
-        top_score = jnp.max(scores, axis=-1, keepdims=True)
-        expo_score = jnp.exp(scores - top_score)
-        total_exp = jnp.sum(expo_score, axis=-1, keepdims=True)
-        soft = expo_score / total_exp
-        log_total = top_score + jnp.log(total_exp)
-        value_heads = value_all.reshape(blocks_here, BLOCK, H, HD)
-        context = jnp.einsum(
-            "chqk,ckhd->cqhd",
-            soft.astype(jnp.bfloat16),
-            value_heads,
-            preferred_element_type=jnp.float32,
-        )
-        context_low = context.reshape(count_rows, D).astype(jnp.bfloat16)
-        first_in = (
-            hidden
-            + matmul_low(context_low, weights.output_weight)
-            + as_float(weights.output_bias)
-        )
-        first_out = layer_norm(
-            first_in, as_float(weights.first_gain), as_float(weights.first_shift)
-        )
-        first_low = first_out.astype(jnp.bfloat16)
-        up_sum = matmul_low(first_low, weights.up_weight) + as_float(weights.up_bias)
-        activated = gelu_exact(up_sum).astype(jnp.bfloat16)
-        second_in = (
-            first_out
-            + matmul_low(activated, weights.down_weight)
-            + as_float(weights.down_bias)
-        )
-        stash = SimpleNamespace(
-            inputs_low=inputs_low,
-            query_low=query_low,
-            key_low=key_low,
-            value_low=value_low,
-            allowed=allowed,
-            log_total=log_total,
-            context_low=context_low,
-            first_in=first_in,
-            first_low=first_low,
-            up_sum=up_sum,
-            activated=activated,
-            second_in=second_in,
-        )
-        stash.key_all = key_all
-        stash.value_all = value_all
-        saved.append(stash)
-        hidden = layer_norm(
-            second_in, as_float(weights.second_gain), as_float(weights.second_shift)
-        )
-    grad_out = cotangent.reshape(count_rows, D).astype(jnp.float32)
-    table_grad = jnp.zeros((BUCKETS, H), jnp.float32)
-    layer_grads = []
-    for number in reversed(range(LAYERS)):
-        weights = layers[number]
-        stash = saved[number]
-        norm_pair = jax.vjp(
-            layer_norm,
-            stash.second_in,
-            as_float(weights.second_gain),
-            as_float(weights.second_shift),
-        )
-        grad_second, grad_gain_two, grad_shift_two = norm_pair[1](grad_out)
-        grad_down_bias = jnp.sum(grad_second, axis=0)
-        down_back = grad_second.astype(jnp.bfloat16)
-        grad_down_weight = jnp.einsum(
-            "nf,nd->fd", stash.activated, down_back, preferred_element_type=jnp.float32
-        )
-        grad_activated = jnp.einsum(
-            "nd,fd->nf", down_back, weights.down_weight, preferred_element_type=jnp.float32
-        )
-        gelu_pair = jax.vjp(gelu_exact, stash.up_sum)
-        grad_up = gelu_pair[1](grad_activated)[0]
-        grad_up_bias = jnp.sum(grad_up, axis=0)
-        up_back = grad_up.astype(jnp.bfloat16)
-        grad_up_weight = jnp.einsum(
-            "nd,nf->df", stash.first_low, up_back, preferred_element_type=jnp.float32
-        )
-        grad_first = grad_second + jnp.einsum(
-            "nf,df->nd", up_back, weights.up_weight, preferred_element_type=jnp.float32
-        )
-        first_pair = jax.vjp(
-            layer_norm,
-            stash.first_in,
-            as_float(weights.first_gain),
-            as_float(weights.first_shift),
-        )
-        grad_first_in, grad_gain_one, grad_shift_one = first_pair[1](grad_first)
-        grad_output_bias = jnp.sum(grad_first_in, axis=0)
-        attend_back = grad_first_in.astype(jnp.bfloat16)
-        grad_output_weight = jnp.einsum(
-            "nd,ne->de", stash.context_low, attend_back, preferred_element_type=jnp.float32
-        )
-        grad_context = jnp.einsum(
-            "ne,de->nd", attend_back, weights.output_weight, preferred_element_type=jnp.float32
-        ).astype(jnp.bfloat16)
-        grad_context = grad_context.reshape(blocks_here, rows, H, HD)
-        key_all = stash.key_all
-        value_all = stash.value_all
-        scores = attention_scores(
-            stash.query_low, key_all, score_bias, stash.allowed, blocks_here, rows
-        )
-        soft = jnp.exp(scores - stash.log_total)
-        key_heads = key_all.reshape(blocks_here, BLOCK, H, HD)
-        value_heads = value_all.reshape(blocks_here, BLOCK, H, HD)
-        grad_soft = jnp.einsum(
-            "cqhd,ckhd->chqk", grad_context, value_heads, preferred_element_type=jnp.float32
-        )
-        inner_sum = jnp.sum(soft * grad_soft, axis=-1, keepdims=True)
-        grad_scores = (soft * (grad_soft - inner_sum)).astype(jnp.bfloat16)
-        table_grad = jnp.einsum(
-            "chqk,cbqk->bh", grad_scores, onehot, preferred_element_type=jnp.float32
-        )
-        query_heads = stash.query_low.reshape(blocks_here, rows, H, HD)
-        grad_query = (
-            jnp.einsum(
-                "chqk,ckhd->cqhd", grad_scores, key_heads, preferred_element_type=jnp.float32
-            ).reshape(count_rows, D)
-            * 0.125
-        )
-        grad_key_all = jnp.einsum(
-            "chqk,cqhd->ckhd", grad_scores, query_heads, preferred_element_type=jnp.float32
-        ).reshape(blocks_here, BLOCK, D)
-        grad_value_all = jnp.einsum(
-            "chqk,cqhd->ckhd",
-            soft.astype(jnp.bfloat16),
-            grad_context,
-            preferred_element_type=jnp.float32,
-        ).reshape(blocks_here, BLOCK, D)
-        grad_key, grad_value = (
-            lax.psum_scatter(
-                grad_key_all.astype(jnp.bfloat16), "seq", scatter_dimension=1, tiled=True
-            ).astype(jnp.float32),
-            lax.psum_scatter(
-                grad_value_all.astype(jnp.bfloat16), "seq", scatter_dimension=1, tiled=True
-            ).astype(jnp.float32),
-        )
-        grad_key = grad_key.reshape(count_rows, D)
-        grad_value = grad_value.reshape(count_rows, D)
-        grad_query_bias = jnp.sum(grad_query, axis=0)
-        grad_value_bias = jnp.sum(grad_value, axis=0)
-        query_back = grad_query.astype(jnp.bfloat16)
-        key_back = grad_key.astype(jnp.bfloat16)
-        value_back = grad_value.astype(jnp.bfloat16)
-        grad_query_weight = jnp.einsum(
-            "nd,ne->de", stash.inputs_low, query_back, preferred_element_type=jnp.float32
-        )
-        grad_key_weight = jnp.einsum(
-            "nd,ne->de", stash.inputs_low, key_back, preferred_element_type=jnp.float32
-        )
-        grad_value_weight = jnp.einsum(
-            "nd,ne->de", stash.inputs_low, value_back, preferred_element_type=jnp.float32
-        )
-        grad_out = grad_first_in + jnp.einsum(
-            "ne,de->nd", query_back, weights.query_weight, preferred_element_type=jnp.float32
-        )
-        grad_out = grad_out + jnp.einsum(
-            "ne,de->nd", key_back, weights.key_weight, preferred_element_type=jnp.float32
-        )
-        grad_out = grad_out + jnp.einsum(
-            "ne,de->nd", value_back, weights.value_weight, preferred_element_type=jnp.float32
-        )
-        layer_grads.insert(
-            0,
-            [
-                grad_query_weight,
-                grad_query_bias,
-                grad_key_weight,
-                grad_value_weight,
-                grad_value_bias,
-                grad_output_weight,
-                grad_output_bias,
-                grad_gain_one,
-                grad_shift_one,
-                grad_up_weight,
-                grad_up_bias,
-                grad_down_weight,
-                grad_down_bias,
-                grad_gain_two,
-                grad_shift_two,
-            ],
-        )
-    embed_back = grad_out.astype(jnp.bfloat16)
-    grad_layout_weight = jnp.einsum(
-        "nf,nd->fd", features_low, embed_back, preferred_element_type=jnp.float32
-    )
-    grad_layout_bias = jnp.sum(grad_out, axis=0)
-    all_pieces = [grad_layout_weight, grad_layout_bias, table_grad]
-    layer_list = layer_grads[0]
-    all_pieces = all_pieces + layer_list
+        tiles = to_tiles(unpack(lax.all_gather(master.astype(jnp.bfloat16), ("dp", "seq"), axis=0, tiled=True)))
+    feats = layout_features(page_boxes.reshape(4, rows)).astype(jnp.bfloat16)
+    pad = jnp.broadcast_to(padding, (8, rows))
+    hidden, low, query, keys, values, pads = enter(tiles, tokens[0], feats, pad)
+    ctx, soft, code = attend(query, keys, values, buckets[0], page_lengths, pads, tiles[vector_at(0)])
+    activations, grad_first_in, grad_context, grads = middle(tiles, ctx, hidden, cotangent[0])
+    dq, dk, dv, table = soft_back(query, keys, values, grad_context, soft, code)
+    input_grad, grads = leave(tiles, dq, dk, dv, grad_first_in, low, feats, table, grads)
     if custom:
-        param_step, new_first, new_second = reduce_and_step(
-            pack_gradients(all_pieces), master, first_moment, second_moment
-        )
+        stepped = reduce_and_step(grads.reshape(16, CHIP, 8, D), master, first_moment, second_moment)
     else:
-        flat_grad = jnp.concatenate([piece.reshape(-1) for piece in all_pieces])
-        grad_shard = lax.psum_scatter(flat_grad, ("dp", "seq"), scatter_dimension=0, tiled=True)
-        square = lax.psum(jnp.sum(grad_shard * grad_shard), ("dp", "seq"))
+        flat = jnp.concatenate([p.astype(jnp.float32).reshape(-1) for p in from_tiles(grads)])
+        grad = lax.psum_scatter(flat, ("dp", "seq"), scatter_dimension=0, tiled=True)
+        square = lax.psum(jnp.sum(grad * grad), ("dp", "seq"))
         factor = jnp.minimum(1.0, lax.rsqrt(square / RAW + 1e-06))
-        shard_size = master.shape[0]
-        global_index = lax.axis_index(("dp", "seq")) * shard_size + jnp.arange(
-            shard_size, dtype=jnp.int32
-        )
-        param_step, new_first, new_second = adam_update(
-            master, first_moment, second_moment, grad_shard * factor, global_index
-        )
-    activations = hidden.reshape(blocks_here, rows, D).astype(jnp.bfloat16)
-    input_grad = grad_out.reshape(blocks_here, rows, D)
-    return (activations, input_grad, param_step, new_first, new_second)
+        size = master.shape[0]
+        index = lax.axis_index(("dp", "seq")) * size + jnp.arange(size, dtype=jnp.int32)
+        stepped = adam_update(master, first_moment, second_moment, grad * factor, index)
+    return (activations[None], input_grad[None]) + tuple(stepped)
 
 
 def solution(mesh):

time: 562 us -> 303 us (0.54); the launches traced: 555 us -> 302 us
  matrix products: 178 us -> 0 us
  local copies, waits for them, and re-layouts: 144 us -> 13.9 us
  Pallas kernels: 172 us -> 287 us
  other arithmetic: 41.1 us -> 0.57 us
  between operations: 17.4 us -> 0.87 us
    dot_general x28 -> x0, matrix products: 178 us -> none  [the longest x7 33.3 us: matmul_low(): return jnp.dot(left, right, preferred_element_type=jnp.float32)]
    pallas_call x0 -> x5, Pallas kernels: none -> 115 us  [the longest x1 33.9 us: middle(): pl.pallas_call(middle_kernel, out_shape=[S((rows, D), bf), S((rows, D), f...]
    unnamed x161 -> x39, local copies, waits for them, and re-layouts: 58.3 us -> 9.89 us
    dot_general x1 -> x0, local copies, waits for them, and re-layouts: 30.4 us -> none  [per_device(): jnp.einsum('bh,cbqk->chqk', entry_part.bias_table, onehot, preferred_elem...]
    another operation x3 -> x0, local copies, waits for them, and re-layouts: 23.4 us -> none
    reduce_sum x12 -> x0, other arithmetic: 18.5 us -> none  [the longest x1 10.9 us: per_device(): total_exp = jnp.sum(expo_score, axis=-1, keepdims=True)]
    another operation x1 -> x2, other arithmetic: 16.6 us -> 0.55 us
    slice x10 -> x0, local copies, waits for them, and re-layouts: 10.8 us -> none  [the longest x8 10.1 us: unpack_gathered(): got = jnp.concatenate([tiles[s:s + n] for s, n in slots_of(first, count)])]
  transfers between devices with their start and end apart: 4 -> 0, of which waited for: 0 -> 0; matrix products, arithmetic and copies ran while one was open for 36% -> 0% of each run, Pallas kernels for 0% -> 0%
where the time goes in v1:
time: 303 us; the launch traced here: 302 us
  Pallas kernels  287 us (95%)
  local copies, waits for them, and re-layouts  13.9 us (5%)
    pallas_call x1, Pallas kernels, reduce_and_step(): pl.pallas_call(reduce_kernel, out_shape=[jax.ShapeDtypeStruct((ROWS, 128)...  99.1 us
    pallas_call x1, Pallas kernels, gather_weights(): pl.pallas_call(gather_kernel, out_shape=jax.ShapeDtypeStruct((16, CHIP, 8...  72.8 us
    pallas_call x1, Pallas kernels, middle(): pl.pallas_call(middle_kernel, out_shape=[S((rows, D), bf), S((rows, D), f...  33.9 us
    pallas_call x1, Pallas kernels, soft_back(): pl.pallas_call(attend_back_kernel, grid=(H // 2,), out_shape=[jax.ShapeDt...  32.8 us
    pallas_call x1, Pallas kernels, attend(): pl.pallas_call(attend_kernel, grid=(H // 2,), out_shape=[jax.ShapeDtypeSt...  28.5 us
    pallas_call x1, Pallas kernels, leave(): pl.pallas_call(leave_kernel, out_shape=[S((rows, D), f32), S(grads.shape,...  12.9 us
    unnamed x39, local copies, waits for them, and re-layouts  9.89 us
    pallas_call x1, Pallas kernels, enter(): pl.pallas_call(enter_kernel, out_shape=[S((rows, D), f32), S((rows, D), b...  6.62 us

profile of v1, /device:TPU:0, one launch (start us, length us, event | category | flops | bytes accessed | tf_op | source)
XLA Modules:
  0.0 301.8 jit_solution(16597761259731175858)
XLA Ops:
  0.6 1.2 pad_bitcast_fusion.2.x_ref.m_ref
  1.9 0.0 copy-start
  1.9 0.0 copy-start.16
  1.9 72.8 %gather_weights.1 = bf16[16,74,8,768]{3,2,1,0:T(8,128)(2,1)} custom-call(f32[1760,128]{1,0:T(8,128)S(1)} %pad_bitcast_fusion.2.x_ref.m_ref), custom_call_target="tpu_custom_call" | custom-call | tf_op jit(solution)/shard_map/gather_weights/pallas_call | solution.py:351
  74.8 0.5 fusion
  75.4 0.1 copy.16.feats
  75.5 6.6 %enter.1 = (f32[512,768]{1,0:T(8,128)S(1)}, bf16[512,768]{1,0:T(8,128)(2,1)S(1)}, bf16[512,768]{1,0:T(8,128)(2,1)S(1)}, bf16[1024,768]{1,0:T(8,128)(2,1)S(1)}, b...) custom-call(bf16[1184,8,768]{2,1,0:T(8,128)(2,1)} %bitcast.29, bf16[512,768]{1,0:T(8,128)(2,1)S(1)} %bitcast.28, ...), custom_call_target="tpu_custom_call" | custom-call | tf_op jit(solution)/shard_map/enter/pallas_call | solution.py:1178
  82.2 1.1 copy-done.1
  83.3 1.1 copy-done.2
  84.4 0.9 copy-done.3
  85.3 1.1 copy-done.4
  86.5 0.9 copy-done.7
  87.4 1.3 slice_bitcast_fusion.lines
  88.7 28.5 %attend.1 = (bf16[512,768]{1,0:T(8,128)(2,1)}, bf16[12,1024,512]{2,1,0:T(8,128)(2,1)}, s32[1024,512]{1,0:T(8,128)}) custom-call(s32[1,4]{1,0:T(1,128)} %lengths.1, bf16[512,768]{1,0:T(8,128)(2,1)} %copy-done.3, bf16[1024,768]{1,0:T(8,128)(2,1)} %copy-done.1, bf16[1024,768]{1,0:T(8,128)(2,1)} %copy-done.2, s32[512,1024]{1,0:T(8,128)} %bitcast.34, ...), custom_call_target="tpu_custom_call" | custom-call | tf_op jit(solution)/shard_map/attend/pallas_call | solution.py:1011
  117.2 33.9 %middle.1 = (bf16[512,768]{1,0:T(8,128)(2,1)}, f32[512,768]{1,0:T(8,128)}, bf16[512,768]{1,0:T(8,128)(2,1)}, bf16[1184,8,768]{2,1,0:T(8,128)(2,1)}) custom-call(bf16[1184,8,768]{2,1,0:T(8,128)(2,1)} %bitcast.31, bf16[512,768]{1,0:T(8,128)(2,1)} %get-tuple-element.31.ctx, f32[512,768]{1,0:T(8,128)} %copy-done.4, bf16[512,768]{1,0:T(8,128)(2,1)} %bitcast.39), custom_call_target="tpu_custom_call" | custom-call | tf_op jit(solution)/shard_map/middle/pallas_call | solution.py:901
  151.1 32.8 %attend_back.1 = (f32[512,768]{1,0:T(8,128)}, f32[1024,768]{1,0:T(8,128)}, f32[1024,768]{1,0:T(8,128)}, f32[8,768]{1,0:T(8,128)}) custom-call(bf16[512,768]{1,0:T(8,128)(2,1)} %copy-done.3, bf16[1024,768]{1,0:T(8,128)(2,1)} %copy-done.1, bf16[1024,768]{1,0:T(8,128)(2,1)} %copy-done.2, bf16[512,768]{1,0:T(8,128)(2,1)} %get-tuple-element.34.do_ref, ...), custom_call_target="tpu_custom_call" | custom-call | tf_op jit(solution)/shard_map/attend_back/pallas_call | solution.py:1111
  183.9 12.9 %leave.1 = (f32[512,768]{1,0:T(8,128)}, bf16[1184,8,768]{2,1,0:T(8,128)(2,1)}) custom-call(bf16[1184,8,768]{2,1,0:T(8,128)(2,1)} %bitcast.32, f32[512,768]{1,0:T(8,128)} %get-tuple-element.37.dq, f32[1024,768]{1,0:T(8,128)} %get-tuple-element.38.dk, f32[1024,768]{1,0:T(8,128)} %get-tuple-element.39.dv, ...), custom_call_target="tpu_custom_call", output_to_operand_aliasing={{1}: (8, {})} | custom-call | tf_op jit(solution)/shard_map/leave/pallas_call | solution.py:1253
  196.8 1.3 pad_bitcast_fusion
  198.1 99.1 %reduce_and_step.1 = (f32[1760,128]{1,0:T(8,128)}, f32[1760,128]{1,0:T(8,128)}, f32[1760,128]{1,0:T(8,128)}) custom-call(bf16[16,74,8,768]{3,2,1,0:T(8,128)(2,1)} %bitcast.33, f32[1760,128]{1,0:T(8,128)} %copy-done, f32[1760,128]{1,0:T(8,128)} %get-tuple-element.52.one_ref, f32[1760,128]{1,0:T(8,128)} %get-tuple-element.51.two_ref), custom_call_target="tpu_custom_call" | custom-call | tf_op jit(solution)/shard_map/reduce_and_step/pallas_call | solution.py:681
  297.2 1.1 copy.26
  298.4 0.5 copy-done.14
  298.9 1.0 copy.27
  299.9 1.0 copy.28
  300.9 1.0 copy.29
  (31 shorter events, 0.1 us)
Async XLA Ops:
  1.9 72.9 %copy-start = (f32[1760,128]{1,0:T(8,128)}, f32[1760,128]{1,0:T(8,128)S(1)}, u32[]{:S(2)}) copy-start(f32[1760,128]{1,0:T(8,128)S(1)} %pad_bitcast_fusion.2.x_ref.m_ref) | copy-start | bytes 2703364
  1.9 72.9 %copy-start.15 = (s32[4,1,512]{2,1,0:T(1,128)S(1)}, s32[4,1,512]{2,1,0:T(1,128)}, u32[]{:S(2)}) copy-start(s32[4,1,512]{2,1,0:T(1,128)} %param.11) | copy-start | bytes 24580
  1.9 73.6 %copy-start.16 = (s32[1,512]{1,0:T(1,128)S(1)}, s32[1,512]{1,0:T(1,128)}, u32[]{:S(2)}) copy-start(s32[1,512]{1,0:T(1,128)} %param.13) | copy-start | bytes 6148
  1.9 73.6 %copy-start.6 = (bf16[1,512,768]{2,1,0:T(8,128)(2,1)S(1)}, bf16[1,512,768]{2,1,0:T(8,128)(2,1)}, u32[]{:S(2)}) copy-start(bf16[1,512,768]{2,1,0:T(8,128)(2,1)} %param.9) | copy-start | bytes 2359300
  75.5 6.7 %copy-start.5 = (bf16[512,128]{1,0:T(8,128)(2,1)}, bf16[512,128]{1,0:T(8,128)(2,1)S(1)}, u32[]{:S(2)}) copy-start(bf16[512,128]{1,0:T(8,128)(2,1)S(1)} %copy.16.feats) | copy-start | bytes 393220
  82.2 1.1 copy-start.1
  83.3 1.1 copy-start.2
  84.4 0.9 copy-start.3
  85.3 1.1 copy-start.4
  86.5 0.9 copy-start.7
  87.4 1.3 copy-start.8
  183.9 12.9 %copy-start.10 = (f32[224580]{0:T(1024)S(1)}, f32[224580]{0:T(1024)}, u32[]{:S(2)}) copy-start(f32[224580]{0:T(1024)} %param.17) | copy-start | bytes 2694964
  183.9 12.9 %copy-start.11 = (f32[224580]{0:T(1024)S(1)}, f32[224580]{0:T(1024)}, u32[]{:S(2)}) copy-start(f32[224580]{0:T(1024)} %param.16) | copy-start | bytes 2694964
  198.1 99.1 %copy-start.9 = (f32[512,768]{1,0:T(8,128)S(1)}, f32[512,768]{1,0:T(8,128)}, u32[]{:S(2)}) copy-start(f32[512,768]{1,0:T(8,128)} %get-tuple-element.44) | copy-start | bytes 4718596
  297.2 1.7 copy-start.14
  297.2 2.7 copy-start.13
  298.9 2.0 copy-start.12

commit v2 on v1

v2 whole, which is shorter than its diff:
```python
import functools

import jax
import jax.numpy as jnp
from jax import lax
from jax.experimental import pallas as pl
from jax.experimental.pallas import tpu as pltpu
from jax.sharding import PartitionSpec as P

D = 768
H = 12
HD = 64
FF = 3072
BUCKETS = 32
FREQ = 16
LF = 128
LAYERS = 1
BLOCK = 1024
STEP = 10
ENTRY = 99456
LAYER_PARAMS = 7087104
RAW = 7186560


beta_one = 0.8
beta_two = 0.98
adam_eps = 1e-06
learn_rate = 0.0006
layer_decay = 0.8
weight_decay = 0.1
norm_eps = 1e-05
masked_score = -1000000000.0


SHAPES = (
    (LF, D), (D,), (BUCKETS, H),
    (D, D), (D,), (D, D), (D, D), (D,), (D, D), (D,), (D,), (D,),
    (D, FF), (FF,), (FF, D), (D,), (D,), (D,),
)


def unpack(flat_params):
    pieces, offset = [], 0
    for shape in SHAPES:
        amount = shape[0] * (shape[1] if len(shape) > 1 else 1)
        pieces.append(flat_params[offset : offset + amount].reshape(shape))
        offset = offset + amount
    return pieces


def adam_update(master, first_moment, second_moment, gradient, global_index):
    exponent = jnp.where(
        global_index < ENTRY,
        LAYERS,
        jnp.maximum(LAYERS - 1 - (global_index - ENTRY) // LAYER_PARAMS, 0),
    )
    rate = jnp.where(
        global_index < RAW, learn_rate * jnp.power(layer_decay, exponent.astype(jnp.float32)), 0.0
    )
    moment_one = beta_one * first_moment + (1.0 - beta_one) * gradient
    moment_two = beta_two * second_moment + (1.0 - beta_two) * gradient * gradient
    fixed_one = moment_one / (1.0 - beta_one**STEP)
    fixed_two = moment_two / (1.0 - beta_two**STEP)
    param_step = -rate * (fixed_one / (jnp.sqrt(fixed_two) + adam_eps) + weight_decay * master)
    return (param_step, moment_one, moment_two)


def layout_features(page_boxes):
    rates_sin = jnp.power(10000.0, -jnp.arange(FREQ, dtype=jnp.float32) / FREQ)
    angles = page_boxes.astype(jnp.float32)[:, :, None] * rates_sin
    stacked = jnp.stack([jnp.sin(angles), jnp.cos(angles)], axis=1)
    return jnp.transpose(stacked, (2, 0, 1, 3)).reshape(page_boxes.shape[1], LF)


MESH = pl.DeviceIdType.MESH
SHARD = 224580
ROWS = 1760
TAIL, HEAD = 160, 176
WIN = 2176
SLOTS = 37
CHIP = 74
PARTS = ((0, 19), (19, 18))


def place():
    k = lax.axis_index("dp")
    return k, lax.axis_index("seq"), k // 4, (k // 2) % 2, k % 2


def shard_start(d):
    return d * 1754 + (d * 68) // 128, (d * 68) % 128


def early_vectors(k):
    return (k == 0) | (k == 4) | (k == 5)


def vector_row(k, other):
    at = other
    for chip, row in ((0, 768), (1, 5385), (4, 14607), (5, 19221), (10, 37671), (15, 56127)):
        at = jnp.where(k == chip, row, at)
    return at


def tile_start(w):
    at = w * 48
    for first, shift in ((16, 777 - 16 * 48), (112, 5391 - 112 * 48), (208, 9999 - 208 * 48), (304, 14613 - 304 * 48), (784, 37695 - 784 * 48)):
        at = jnp.where(w >= first, w * 48 + shift, at)
    wide = (w >= 400) & (w < 784)
    v = w - 400
    at = jnp.where(wide, 19239 + (v // 4) * 192 + (v % 4) * 6, at)
    return at, wide


def neighbours(k, c, z, y, x):
    t = k >= 0
    return [
        (t, (k, 1 - c)),
        (t, (z * 4 + y * 2 + 1 - x, c)),
        (t, (z * 4 + (1 - y) * 2 + x, c)),
        (z < 3, (jnp.minimum(k + 4, 15), c)),
        (z > 0, (jnp.maximum(k - 4, 0), c)),
        ((c == 1) & (k < 15), (jnp.minimum(k + 1, 15), 0)),
        ((c == 0) & (k > 0), (jnp.maximum(k - 1, 0), 1)),
    ]


def greet(k, c, z, y, x):
    bar = pltpu.get_barrier_semaphore()
    for cond, dev in neighbours(k, c, z, y, x):
        @pl.when(cond)
        def _():
            pl.semaphore_signal(bar, inc=1, device_id=dev, device_id_type=MESH)
    peers = 3
    for cond, _ in neighbours(k, c, z, y, x)[3:]:
        peers = peers + jnp.where(cond, 1, 0)
    pl.semaphore_wait(bar, peers)


def rcopy(src, dst, ssem, rsem, dev):
    return pltpu.make_async_remote_copy(src_ref=src, dst_ref=dst, send_sem=ssem, recv_sem=rsem, device_id=dev, device_id_type=MESH)


FRONT = 344
WIN2 = 2464
EDGE = 4
ENTRY_ROWS = 777


WEIGHTS = (
    (0, 0, 16),
    (3, 16, 96),
    (5, 112, 96),
    (6, 208, 96),
    (8, 304, 96),
    (12, 400, 384),
    (14, 784, 384),
)
VECTORS = (
    (1, 0, 0),
    (2, 0, 1),
    (4, 1, 0),
    (7, 4, 0),
    (9, 5, 0),
    (10, 5, 1),
    (11, 5, 2),
    (13, 10, 0),
    (15, 15, 0),
    (16, 15, 1),
    (17, 15, 2),
)


def slots_of(first, count):
    runs = []
    for w in range(first, first + count):
        chip, at = divmod(w, 73)
        slot = chip * CHIP + at + (1 if at >= vector_slot(chip) else 0)
        if runs and runs[-1][0] + runs[-1][2] == slot:
            runs[-1][2] += 1
        else:
            runs.append([slot, w - first, 1])
    return runs


def vector_slot(chip):
    return 36 if chip in (0, 4, 5) else 73


def vector_at(chip):
    return chip * CHIP + vector_slot(chip)


def pieces(tiles, held, first, count, sems, base, out=False):
    made = []
    for i, (slot, at, n) in enumerate(slots_of(first, count)):
        a, b = tiles.at[pl.ds(slot, n)], held.at[pl.ds(at, n)]
        a, b = (b, a) if out else (a, b)
        made.append(pltpu.make_async_copy(a, b, sems.at[base + i]))
    return made


def matrix(tile_rows):
    return tile_rows.reshape(-1, D)


def col_sum(v):
    return jnp.sum(v.reshape(-1, 8, v.shape[-1]), axis=0)


def norm_stats(v):
    mean = jnp.mean(v, axis=-1, keepdims=True)
    center = v - mean
    spread = jnp.mean(center * center, axis=-1, keepdims=True)
    inv = lax.rsqrt(spread + norm_eps)
    return center * inv, inv


def norm_back(grad, gain, hat, inv):
    g = grad * gain
    return inv * (g - jnp.mean(g, axis=-1, keepdims=True) - hat * jnp.mean(g * hat, axis=-1, keepdims=True))


ROOT_HALF = 0.7071067811865476
ROOT_TAU = 0.3989422804014327


def middle_kernel(tiles, ctx, hidden, cot, act_out, gfi_out, gctx_out, grads,
                  wo, wup, wdn, vecs, vf, act, slope, low1, hat1, inv1, hat2, inv2, a, sums, dwo, dwup, dwdn, vgrads, lsem, ssem):
    f32, bf = jnp.float32, jnp.bfloat16
    rows = ctx.shape[0]
    R = 64
    steps = rows // R
    loads_o = pieces(tiles, wo, 304, 96, lsem, 0)
    loads_u = pieces(tiles, wup, 400, 384, lsem, 4)
    loads_d = pieces(tiles, wdn, 784, 384, lsem, 12)
    loads_v = [pltpu.make_async_copy(tiles.at[vector_at(c)], vecs.at[i], lsem.at[20 + i]) for i, c in enumerate((5, 10, 15))]
    for c in loads_v + loads_o + loads_u + loads_d:
        c.start()
    up4 = wup.reshape(96, 4, 8, D)
    dup4 = dwup.reshape(96, 4, 8, D)

    def vec(i, r):
        return vf[i, pl.ds(r, 1), :]

    def each(f):
        @pl.loop(0, steps)
        def _(i):
            f(pl.ds(pl.multiple_of(i * R, R), R))

    for c in loads_v + loads_o:
        c.wait()
    vf[...] = vecs[...].astype(f32)
    a[...] = jnp.dot(ctx[...], matrix(wo[...]), preferred_element_type=f32)

    def first(sl):
        hat, inv = norm_stats(hidden[sl, :] + a[sl, :] + vec(0, 0))
        hat1[sl, :] = hat
        inv1[sl, :] = inv
        out = hat * vec(0, 1) + vec(0, 2)
        a[sl, :] = out
        low1[sl, :] = out.astype(bf)

    each(first)
    for c in loads_u + loads_d:
        c.wait()

    def up(j, _):
        for half in range(2):
            sl = pl.ds(half * (rows // 2), rows // 2)
            u = jnp.dot(low1[sl, :], matrix(up4[:, j]), preferred_element_type=f32) + vec(1, j)
            share = 0.5 * (1.0 + lax.erf(u * ROOT_HALF))
            act[j, sl, :] = (u * share).astype(bf)
            slope[j, sl, :] = share + u * jnp.exp(-0.5 * u * u) * ROOT_TAU
        return 0

    lax.fori_loop(0, 4, up, 0)

    def down(j, _):
        a[...] += jnp.dot(act[j], matrix(wdn[pl.ds(96 * j, 96)]), preferred_element_type=f32)
        return 0

    lax.fori_loop(0, 4, down, 0)
    sums[...] = jnp.zeros_like(sums)

    def second(sl):
        hat, inv = norm_stats(a[sl, :] + vec(2, 0))
        act_out[sl, :] = (hat * vec(2, 1) + vec(2, 2)).astype(bf)
        g = cot[sl, :].astype(f32)
        sums[6] += col_sum(g * hat)
        sums[7] += col_sum(g)
        back = norm_back(g, vec(2, 1), hat, inv)
        sums[5] += col_sum(back)
        a[sl, :] = back
        hat2[sl, :] = back.astype(bf)

    each(second)
    down_back = hat2

    def back(j, _):
        for half in range(2):
            sl = pl.ds(half * (rows // 2), rows // 2)
            g = lax.dot_general(down_back[sl, :], matrix(wdn[pl.ds(96 * j, 96)]), NT, preferred_element_type=f32) * slope[j, sl, :]
            sums[8 + j] += col_sum(g)
            act_back[sl, :] = g.astype(bf)
        dwdn[pl.ds(96 * j, 96)] = lax.dot_general(act[j], down_back[...], TN, preferred_element_type=f32).astype(bf).reshape(96, 8, D)
        dup4[:, j] = lax.dot_general(low1[...], act_back[...], TN, preferred_element_type=f32).astype(bf).reshape(96, 8, D)
        a[...] += lax.dot_general(act_back[...], matrix(up4[:, j]), NT, preferred_element_type=f32)
        return 0

    act_back = inv2
    lax.fori_loop(0, 4, back, 0)
    stores = pieces(grads, dwup, 400, 384, ssem, 4, True) + pieces(grads, dwdn, 784, 384, ssem, 12, True)
    for c in stores:
        c.start()

    def third(sl):
        g = a[sl, :]
        sums[3] += col_sum(g * hat1[sl, :])
        sums[4] += col_sum(g)
        back = norm_back(g, vec(0, 1), hat1[sl, :], inv1[sl, :])
        sums[2] += col_sum(back)
        gfi_out[sl, :] = back
        hat2[sl, :] = back.astype(bf)

    each(third)
    gctx_out[...] = lax.dot_general(hat2[...], matrix(wo[...]), NT, preferred_element_type=f32).astype(bf)
    dwo[...] = lax.dot_general(ctx[...], hat2[...], TN, preferred_element_type=f32).astype(bf).reshape(96, 8, D)
    for i, held in enumerate(((2, 3, 4), (8, 9, 10, 11), (5, 6, 7))):
        lines = [jnp.sum(sums[s], axis=0, keepdims=True) for s in held]
        lines.append(jnp.zeros((8 - len(held), D), f32))
        vgrads[i] = jnp.concatenate(lines).astype(bf)
    last = pieces(grads, dwo, 304, 96, ssem, 0, True)
    quiet = [ch for ch in range(6, 15) if ch != 10]
    vgrads[3] = jnp.zeros((8, D), bf)
    last += [pltpu.make_async_copy(vgrads.at[min(i, 3)], grads.at[vector_at(ch)], ssem.at[20 + i]) for i, ch in enumerate([5, 10, 15] + quiet)]
    for c in last:
        c.start()
    for c in stores + last:
        c.wait()


def middle(tiles, ctx, hidden, cot):
    rows = ctx.shape[0]
    f32, bf = jnp.float32, jnp.bfloat16
    vm, any_ = pl.BlockSpec(memory_space=pltpu.VMEM), pl.BlockSpec(memory_space=pl.ANY)
    S = jax.ShapeDtypeStruct
    return pl.pallas_call(
        middle_kernel,
        out_shape=[S((rows, D), bf), S((rows, D), f32), S((rows, D), bf), S((16 * CHIP, 8, D), bf)],
        in_specs=[any_, vm, vm, vm],
        out_specs=[vm, vm, vm, any_],
        scratch_shapes=[
            pltpu.VMEM((96, 8, D), bf), pltpu.VMEM((384, 8, D), bf), pltpu.VMEM((384, 8, D), bf), pltpu.VMEM((3, 8, D), bf), pltpu.VMEM((3, 8, D), f32),
            pltpu.VMEM((4, rows, D), bf), pltpu.VMEM((4, rows, D), f32), pltpu.VMEM((rows, D), bf),
            pltpu.VMEM((rows, D), f32), pltpu.VMEM((rows, 1), f32), pltpu.VMEM((rows, D), bf), pltpu.VMEM((rows, D), bf),
            pltpu.VMEM((rows, D), f32), pltpu.VMEM((12, 8, D), f32),
            pltpu.VMEM((96, 8, D), bf), pltpu.VMEM((384, 8, D), bf), pltpu.VMEM((384, 8, D), bf), pltpu.VMEM((4, 8, D), bf),
            pltpu.SemaphoreType.DMA((24,)), pltpu.SemaphoreType.DMA((32,)),
        ],
        compiler_params=pltpu.CompilerParams(vmem_limit_bytes=58 << 20),
        name="middle",
    )(tiles, ctx, hidden, cot)


NT = (((1,), (1,)), ((), ()))
TN = (((0,), (0,)), ((), ()))


def half(ref_value, hh):
    lanes = lax.broadcasted_iota(jnp.int32, ref_value.shape, 1)
    keep = lanes < 64 if hh == 0 else lanes >= 64
    return jnp.where(keep, ref_value, jnp.zeros_like(ref_value))


def page_of(at, lengths):
    end, page = 0, jnp.zeros(at.shape, jnp.int32)
    for i in range(4):
        end = end + lengths[0, i]
        page = page + jnp.where(at >= end, 1, 0)
    return page


def fill_codes(code_ref, buckets, pads, lengths):
    keys, rows = code_ref.shape
    own = lax.axis_index("seq") * rows
    tag = page_of(lax.broadcasted_iota(jnp.int32, (1, keys), 1), lengths) + 1
    tag = jnp.where(jnp.concatenate([pads[0, 0:1], pads[1, 0:1]], axis=1) > 0, tag, 0)
    for i in range(rows // 128):
        at = own + 128 * i + lax.broadcasted_iota(jnp.int32, (128, 1), 0)
        page = page_of(at, lengths) + 1
        for j in range(keys // 128):
            key_at = 128 * j + lax.broadcasted_iota(jnp.int32, (1, 128), 1)
            allowed = (page == tag[:, 128 * j : 128 * j + 128]) | (key_at == at)
            code = jnp.where(allowed, buckets[128 * i : 128 * i + 128, 128 * j : 128 * j + 128], BUCKETS)
            code_ref[128 * j : 128 * j + 128, 128 * i : 128 * i + 128] = code.T


def fill_table(tab_ref, lines):
    f32 = jnp.float32
    head = lax.broadcasted_iota(jnp.int32, (16, 128), 0)
    bucket = lax.broadcasted_iota(jnp.int32, (16, 128), 1)
    place_of = bucket * H + head
    tab = jnp.full((16, 128), masked_score, f32)
    for i in range(BUCKETS * H // 128):
        row = jnp.broadcast_to(lines[1:2, 128 * i : 128 * i + 128].astype(f32), (16, 128))
        inside = jnp.clip(place_of - 128 * i, 0, 127)
        got = jnp.take_along_axis(row, inside, axis=1, mode="promise_in_bounds")
        tab = jnp.where((place_of // 128 == i) & (bucket < BUCKETS) & (head < H), got, tab)
    tab_ref[...] = tab


def soft_pair(pair, q, k, code_ref, tab_ref, s_scr, p_ref):
    keys, rows = s_scr.shape
    f32, bf = jnp.float32, jnp.bfloat16
    for hh in range(2):
        qm = half(q, hh)
        line = jnp.broadcast_to(tab_ref[pl.ds(2 * pair + hh, 1), :], (keys, 128))
        s = lax.dot_general(k, qm, NT, preferred_element_type=f32)
        cols = []
        for j in range(rows // 128):
            code = code_ref[:, 128 * j : 128 * j + 128]
            bias = jnp.take_along_axis(line, code, axis=1, mode="promise_in_bounds")
            cols.append(jnp.where(bias < 0.5 * masked_score, masked_score, s[:, 128 * j : 128 * j + 128] + bias))
        s = jnp.concatenate(cols, axis=1)
        s_scr[...] = s
        top = jnp.max(jnp.max(s.reshape(keys // 8, 8, rows), axis=0), axis=0, keepdims=True)
        e = jnp.exp(s_scr[...] - top)
        s_scr[...] = e
        inverse = 1.0 / jnp.sum(jnp.sum(e.reshape(keys // 8, 8, rows), axis=0), axis=0, keepdims=True)
        p_ref[hh] = (s_scr[...] * inverse).astype(bf)


def context_pair(v, p_ref):
    vt = v.T
    out = [jnp.dot(vt, p_ref[hh], preferred_element_type=jnp.float32) for hh in range(2)]
    sub = lax.broadcasted_iota(jnp.int32, out[0].shape, 0)
    return jnp.where(sub < 64, out[0], out[1]).T.astype(jnp.bfloat16)


def attend_kernel(lengths, q_ref, k_ref, v_ref, buckets, pads, lines, ctx_ref, p_ref, code_ref, s_scr, tab_ref):
    pair = pl.program_id(0)

    @pl.when(pair == 0)
    def _():
        fill_codes(code_ref, buckets, pads, lengths)
        fill_table(tab_ref, lines)

    soft_pair(pair, q_ref[...], k_ref[...], code_ref, tab_ref, s_scr, p_ref)
    ctx_ref[...] = context_pair(v_ref[...], p_ref)


def attend(query, key_all, value_all, buckets, page_lengths, pads, lines):
    rows, keys = query.shape[0], key_all.shape[0]
    bf = jnp.bfloat16
    const = lambda p: (0, 0)
    return pl.pallas_call(
        attend_kernel,
        grid=(H // 2,),
        out_shape=[
            jax.ShapeDtypeStruct((rows, D), bf),
            jax.ShapeDtypeStruct((H, keys, rows), bf),
            jax.ShapeDtypeStruct((keys, rows), jnp.int32),
        ],
        in_specs=[
            pl.BlockSpec(memory_space=pltpu.SMEM),
            pl.BlockSpec((rows, 128), lambda p: (0, p)),
            pl.BlockSpec((keys, 128), lambda p: (0, p)),
            pl.BlockSpec((keys, 128), lambda p: (0, p)),
            pl.BlockSpec((rows, keys), const),
            pl.BlockSpec((2, 8, rows), lambda p: (0, 0, 0)),
            pl.BlockSpec((8, D), const),
        ],
        out_specs=[pl.BlockSpec((rows, 128), lambda p: (0, p)), pl.BlockSpec((2, keys, rows), lambda p: (p, 0, 0)), pl.BlockSpec((keys, rows), const)],
        scratch_shapes=[pltpu.VMEM((keys, rows), jnp.float32), pltpu.VMEM((16, 128), jnp.float32)],
        compiler_params=pltpu.CompilerParams(vmem_limit_bytes=56 << 20),
        name="attend",
    )(page_lengths, query, key_all, value_all, buckets, pads, lines)


def table_row(acc, shape):
    f32 = jnp.float32
    a = lax.broadcasted_iota(jnp.int32, acc.shape, 0) % 8
    b = lax.broadcasted_iota(jnp.int32, acc.shape, 1) // BUCKETS
    acc = jnp.where(a == b, acc, 0.0)
    heads = jnp.sum(acc.reshape(H, 8, 8 * BUCKETS), axis=1)
    lane = lax.broadcasted_iota(jnp.int32, (8 * BUCKETS, D), 1) // H
    wide = jnp.where(lane == lax.broadcasted_iota(jnp.int32, lane.shape, 0) % BUCKETS, 1.0, 0.0)
    out = jnp.dot(heads, wide, precision=lax.Precision.HIGHEST, preferred_element_type=f32)
    mine = lax.broadcasted_iota(jnp.int32, out.shape, 1) % H == lax.broadcasted_iota(jnp.int32, out.shape, 0)
    out = jnp.sum(jnp.where(mine, out, 0.0), axis=0, keepdims=True)
    return jnp.broadcast_to(out, shape)


def attend_back_kernel(q_ref, k_ref, v_ref, do_ref, p_ref, code_ref, dq_ref, dk_ref, dv_ref, tab_ref, spread, held):
    pair = pl.program_id(0)
    keys, rows = code_ref.shape
    f32, bf = jnp.float32, jnp.bfloat16
    STEP_ROWS = keys
    kt = k_ref[...].T
    dq = []
    for hh in range(2):
        qm = half(q_ref[...], hh)
        dom = half(do_ref[...], hh)

        def inner(i, total):
            at = pl.multiple_of(i * STEP_ROWS, STEP_ROWS)
            g = lax.dot_general(v_ref[pl.ds(at, STEP_ROWS), :], dom, NT, preferred_element_type=f32)
            w = g * p_ref[hh, pl.ds(at, STEP_ROWS), :].astype(f32)
            return total + jnp.sum(w.reshape(STEP_ROWS // 8, 8, rows), axis=0)

        total = lax.fori_loop(0, keys // STEP_ROWS, inner, jnp.zeros((8, rows), f32))
        total = jnp.sum(total, axis=0, keepdims=True)

        def grads(i, acc):
            at = pl.multiple_of(i * STEP_ROWS, STEP_ROWS)
            sl = pl.ds(at, STEP_ROWS)
            g = lax.dot_general(v_ref[sl, :], dom, NT, preferred_element_type=f32)
            p = p_ref[hh, sl, :]
            ds = p.astype(f32) * (g - total)
            wide = ds.reshape(STEP_ROWS // 8, 8, rows)
            if hh == 0:
                held[...] = wide
            else:
                both = jnp.concatenate([held[...], wide], axis=1).astype(bf)
                spread[:, pl.ds(pl.multiple_of(pair * 16, 16), 16), :] = both
            ds = ds.astype(bf)
            dv = jnp.dot(p, dom, preferred_element_type=f32)
            dk = jnp.dot(ds, qm, preferred_element_type=f32)
            if hh == 0:
                dv_ref[sl, :] = dv
                dk_ref[sl, :] = dk
            else:
                dv_ref[sl, :] += dv
                dk_ref[sl, :] += dk
            return acc + lax.dot_general(k_ref[sl, :], ds, TN, preferred_element_type=f32)

        dq.append(lax.fori_loop(0, keys // STEP_ROWS, grads, jnp.zeros((128, rows), f32)))
    sub = lax.broadcasted_iota(jnp.int32, dq[0].shape, 0)
    dq_ref[...] = jnp.where(sub < 64, dq[0], dq[1]).T * 0.125

    @pl.when(pair == H // 2 - 1)
    def _():
        bucket = lax.broadcasted_iota(jnp.int32, (BUCKETS, rows), 0)

        def count(i, acc):
            code = code_ref[pl.ds(pl.multiple_of(i * 8, 8), 8), :]
            hot = jnp.concatenate(
                [jnp.where(jnp.broadcast_to(code[r : r + 1], bucket.shape) == bucket, 1.0, 0.0) for r in range(8)]
            ).astype(bf)
            return acc + lax.dot_general(spread[i], hot, NT, preferred_element_type=f32)

        acc = lax.fori_loop(0, keys // 8, count, jnp.zeros((8 * H, 8 * BUCKETS), f32), unroll=8)
        tab_ref[...] = table_row(acc, tab_ref.shape)


def soft_back(query, key_all, value_all, grad_context, soft, code):
    rows, keys = query.shape[0], key_all.shape[0]
    f32 = jnp.float32
    row = pl.BlockSpec((rows, 128), lambda p: (0, p))
    key = pl.BlockSpec((keys, 128), lambda p: (0, p))
    dq, dk, dv, tab = pl.pallas_call(
        attend_back_kernel,
        grid=(H // 2,),
        out_shape=[
            jax.ShapeDtypeStruct((rows, D), f32),
            jax.ShapeDtypeStruct((keys, D), f32),
            jax.ShapeDtypeStruct((keys, D), f32),
            jax.ShapeDtypeStruct((8, D), f32),
        ],
        in_specs=[row, key, key, row, pl.BlockSpec((2, keys, rows), lambda p: (p, 0, 0)), pl.BlockSpec((keys, rows), lambda p: (0, 0))],
        out_specs=[row, key, key, pl.BlockSpec((8, D), lambda p: (0, 0))],
        scratch_shapes=[pltpu.VMEM((keys // 8, 8 * H, rows), jnp.bfloat16), pltpu.VMEM((keys // 8, 8, rows), f32)],
        compiler_params=pltpu.CompilerParams(vmem_limit_bytes=58 << 20),
        name="attend_back",
    )(query, key_all, value_all, grad_context, soft, code)
    return dq, dk, dv, tab


def meet_partner():
    dp, c = lax.axis_index("dp"), lax.axis_index("seq")
    partner = (dp, 1 - c)
    bar = pltpu.get_barrier_semaphore()
    pl.semaphore_signal(bar, inc=1, device_id=partner, device_id_type=MESH)
    pl.semaphore_wait(bar, 1)
    return c, partner


def enter_kernel(tiles, tokens, feats, pad, hidden, low, query, keys, values, pads, wl, wq, wk, wv, vecs, vf, lsem, sends, recvs):
    f32, bf = jnp.float32, jnp.bfloat16
    rows = tokens.shape[0]
    loads = [pltpu.make_async_copy(tiles.at[vector_at(ch)], vecs.at[i], lsem.at[i]) for i, ch in enumerate((0, 1, 4))]
    loads += pieces(tiles, wl, 0, 16, lsem, 4) + pieces(tiles, wk, 112, 96, lsem, 8)
    loads += pieces(tiles, wv, 208, 96, lsem, 12) + pieces(tiles, wq, 16, 96, lsem, 16)
    for c in loads:
        c.start()
    c, partner = meet_partner()
    own = pl.ds(c * rows, rows)

    def share(ref, i):
        return rcopy(ref.at[own], ref.at[own], sends.at[i], recvs.at[i], partner)

    pads[pl.ds(c, 1)] = pad[...].reshape(1, 8, rows)
    pair_pads = rcopy(pads.at[pl.ds(c, 1)], pads.at[pl.ds(c, 1)], sends.at[2], recvs.at[2], partner)
    pair_pads.start()
    for copy in loads:
        copy.wait()
    vf[...] = vecs[...].astype(f32)
    h = tokens[...].astype(f32) + jnp.dot(feats[...], matrix(wl[...]), preferred_element_type=f32) + vf[0, 0:1, :]
    hidden[...] = h
    low[...] = h.astype(bf)
    keys[own, :] = jnp.dot(low[...], matrix(wk[...]), preferred_element_type=f32).astype(bf)
    send_keys = share(keys, 0)
    send_keys.start()
    values[own, :] = (jnp.dot(low[...], matrix(wv[...]), preferred_element_type=f32) + vf[2, 0:1, :]).astype(bf)
    send_values = share(values, 1)
    send_values.start()
    query[...] = ((jnp.dot(low[...], matrix(wq[...]), preferred_element_type=f32) + vf[1, 0:1, :]) * 0.125).astype(bf)
    for copy in (pair_pads, send_keys, send_values):
        copy.wait()


def enter(tiles, tokens, feats, pad):
    rows = tokens.shape[0]
    f32, bf = jnp.float32, jnp.bfloat16
    vm, any_ = pl.BlockSpec(memory_space=pltpu.VMEM), pl.BlockSpec(memory_space=pl.ANY)
    S, sem = jax.ShapeDtypeStruct, pltpu.SemaphoreType.DMA
    w = pltpu.VMEM((96, 8, D), bf)
    return pl.pallas_call(
        enter_kernel,
        out_shape=[S((rows, D), f32), S((rows, D), bf), S((rows, D), bf), S((2 * rows, D), bf), S((2 * rows, D), bf), S((2, 8, rows), jnp.int32)],
        in_specs=[any_, vm, vm, vm],
        out_specs=[vm] * 6,
        scratch_shapes=[pltpu.VMEM((16, 8, D), bf), w, w, w, pltpu.VMEM((3, 8, D), bf), pltpu.VMEM((3, 8, D), f32), sem((20,)), sem((3,)), sem((3,))],
        compiler_params=pltpu.CompilerParams(collective_id=2, has_side_effects=True, vmem_limit_bytes=40 << 20),
        name="enter",
    )(tiles, tokens, feats, pad)


def leave_kernel(tiles, dq, dk, dv, gfi, low, feats, table, grads_in, input_grad, grads,
                 wq, wk, wv, out, come, back, dwl, dwq, dwk, dwv, vgrads, lsem, ssem, sends, recvs):
    f32, bf = jnp.float32, jnp.bfloat16
    rows = gfi.shape[0]
    loads = pieces(tiles, wk, 112, 96, lsem, 0) + pieces(tiles, wv, 208, 96, lsem, 4) + pieces(tiles, wq, 16, 96, lsem, 8)
    for c in loads:
        c.start()
    c, partner = meet_partner()
    own, other = pl.ds(c * rows, rows), pl.ds((1 - c) * rows, rows)
    swaps = []
    for i, ref in enumerate((dk, dv)):
        out[i] = ref[other, :].astype(bf)
        swaps.append(rcopy(out.at[i], come.at[i], sends.at[i], recvs.at[i], partner))
        swaps[i].start()
    back[0] = dq[...].astype(bf)
    query_bias = jnp.sum(col_sum(dq[...]), axis=0, keepdims=True)
    for copy in loads:
        copy.wait()

    def through(i, w, dw):
        dw[...] = lax.dot_general(low[...], back[i], TN, preferred_element_type=f32).astype(bf).reshape(96, 8, D)
        return lax.dot_general(back[i], matrix(w[...]), NT, preferred_element_type=f32)

    input_grad[...] = gfi[...] + through(0, wq, dwq)
    stores = pieces(grads, dwq, 16, 96, ssem, 0, True)
    swaps[0].wait_recv()
    back[1] = (dk[own, :] + come[0].astype(f32)).astype(bf)
    input_grad[...] += through(1, wk, dwk)
    stores += pieces(grads, dwk, 112, 96, ssem, 4, True)
    swaps[1].wait_recv()
    grad_value = dv[own, :] + come[1].astype(f32)
    value_bias = jnp.sum(col_sum(grad_value), axis=0, keepdims=True)
    back[2] = grad_value.astype(bf)
    total = input_grad[...] + through(2, wv, dwv)
    stores += pieces(grads, dwv, 208, 96, ssem, 8, True)
    input_grad[...] = total
    layout_bias = jnp.sum(col_sum(total), axis=0, keepdims=True)
    dwl[...] = lax.dot_general(feats[...], total.astype(bf), TN, preferred_element_type=f32).astype(bf).reshape(16, 8, D)
    stores += pieces(grads, dwl, 0, 16, ssem, 12, True)

    def block(lines):
        return jnp.concatenate(lines + [jnp.zeros((8 - len(lines), D), f32)]).astype(bf)

    vgrads[0] = block([layout_bias, table[0:1, :]])
    vgrads[1] = block([query_bias])
    vgrads[2] = block([value_bias])
    vgrads[3] = jnp.zeros((8, D), bf)
    held = {0: 0, 1: 1, 4: 2}
    for i, chip in enumerate(ch for ch in range(5)):
        stores.append(pltpu.make_async_copy(vgrads.at[held.get(chip, 3)], grads.at[vector_at(chip)], ssem.at[16 + i]))
    for copy in stores:
        copy.start()
    for copy in stores:
        copy.wait()
    for swap in swaps:
        swap.wait_send()


def leave(tiles, dq, dk, dv, gfi, low, feats, table, grads):
    rows = gfi.shape[0]
    f32, bf = jnp.float32, jnp.bfloat16
    vm, any_ = pl.BlockSpec(memory_space=pltpu.VMEM), pl.BlockSpec(memory_space=pl.ANY)
    S, sem = jax.ShapeDtypeStruct, pltpu.SemaphoreType.DMA
    w = pltpu.VMEM((96, 8, D), bf)
    return pl.pallas_call(
        leave_kernel,
        out_shape=[S((rows, D), f32), S(grads.shape, bf)],
        in_specs=[any_] + [vm] * 7 + [any_],
        out_specs=[vm, any_],
        scratch_shapes=[w, w, w, pltpu.VMEM((2, rows, D), bf), pltpu.VMEM((2, rows, D), bf), pltpu.VMEM((3, rows, D), bf),
                        pltpu.VMEM((16, 8, D), bf), w, w, w, pltpu.VMEM((4, 8, D), bf), sem((12,)), sem((32,)), sem((2,)), sem((2,))],
        input_output_aliases={8: 1},
        compiler_params=pltpu.CompilerParams(collective_id=3, has_side_effects=True, vmem_limit_bytes=56 << 20),
        name="leave",
    )(tiles, dq, dk, dv, gfi, low, feats, table, grads)


def forward_kernel(x_ref, tokens, feats, pad, buckets, lengths,
                   g_ref, hidden, low, query, keys, values, ctx, soft, code_out,
                   xv, tail, head, win, chunk, lsem, hsend, hrecv, own,
                   zs, zr, xas, xar, xbs, xbr, yas, yar, ybs, ybr, cs, cr,
                   pads, hidden_v, low_v, query_v, keys_v, values_v, ctx_v, code, buckets_v, tokens_v, feats_v, p_v, s_scr, tab,
                   wl, wq, wk, wv, vrows, vf, ksend, krecv, wsem, isem, osem, psem):
    f32, bf = jnp.float32, jnp.bfloat16
    rows = tokens.shape[0]
    k, c, z, y, x = place()
    d = 2 * k + c
    inputs = [pltpu.make_async_copy(r, v, isem.at[i]) for i, (r, v) in enumerate(((buckets, buckets_v), (tokens, tokens_v), (feats, feats_v)))]
    for copy in inputs:
        copy.start()
    pads[pl.ds(c, 1)] = pad[...].reshape(1, 8, rows)
    greet(k, c, z, y, x)
    load = pltpu.make_async_copy(x_ref, xv, lsem)
    load.start()
    prev = (jnp.where(c == 1, k, jnp.maximum(k - 1, 0)), 1 - c)
    nxt = (jnp.where(c == 0, k, jnp.minimum(k + 1, 15)), 1 - c)
    to_next = rcopy(x_ref.at[pl.ds(ROWS - TAIL, TAIL)], tail, hsend.at[0], hrecv.at[0], nxt)
    to_prev = rcopy(x_ref.at[pl.ds(0, HEAD)], head, hsend.at[1], hrecv.at[1], prev)

    @pl.when(d < 31)
    def _():
        to_next.start()

    @pl.when(d > 0)
    def _():
        to_prev.start()

    win[...] = jnp.zeros_like(win)
    lanes = lax.broadcasted_iota(jnp.int32, (80, 128), 1)
    q, sh = shard_start(d)
    load.wait()

    @pl.loop(0, ROWS // 80)
    def _(i):
        r = pl.multiple_of(i * 80, 8)
        rolled = pltpu.roll(xv[pl.ds(r, 80), :], sh, 1)
        win[pl.ds(160 + r, 80), :] += jnp.where(lanes >= sh, rolled, 0.0)
        win[pl.ds(161 + r, 80), :] += jnp.where(lanes < sh, rolled, 0.0)

    @pl.when(d > 0)
    def _():
        to_next.wait_recv()
        qp, shp = shard_start(d - 1)
        lanes = lax.broadcasted_iota(jnp.int32, (TAIL, 128), 1)
        rolled = pltpu.roll(tail[...], shp, 1)
        at = 1760 - (q - qp)
        win[pl.ds(at, TAIL), :] += jnp.where(lanes >= shp, rolled, 0.0)
        win[pl.ds(at + 1, TAIL), :] += jnp.where(lanes < shp, rolled, 0.0)

    @pl.when(d < 31)
    def _():
        to_prev.wait_recv()
        qn, shn = shard_start(d + 1)
        lanes = lax.broadcasted_iota(jnp.int32, (HEAD, 128), 1)
        rolled = pltpu.roll(head[...], shn, 1)
        at = 160 + (qn - q)
        win[pl.ds(at, HEAD), :] += jnp.where(lanes >= shn, rolled, 0.0)
        win[pl.ds(at + 1, HEAD), :] += jnp.where(lanes < shn, rolled, 0.0)

    early = early_vectors(k)
    nw0 = jnp.where(early, 36, 37)
    vecs = early == (c == 0)
    first = jnp.where(c == 0, 73 * k, 73 * k + nw0)
    base = q - 160

    @pl.loop(0, SLOTS)
    def _(t):
        at, wide = tile_start(first + t)
        is_vec = vecs & (t == 36)
        at = jnp.where(is_vec, vector_row(k, q), at) - base
        wide = wide & jnp.logical_not(is_vec)

        @pl.when(wide)
        def _():
            parts = [win[pl.ds(at + j, 8, stride=24), :] for j in range(6)]
            chunk[t] = jnp.concatenate(parts, axis=1).astype(jnp.bfloat16)

        @pl.when(jnp.logical_not(wide))
        def _():
            parts = [win[pl.ds(at + j, 8, stride=6), :] for j in range(6)]
            chunk[t] = jnp.concatenate(parts, axis=1).astype(jnp.bfloat16)

    @pl.when(d < 31)
    def _():
        to_next.wait_send()

    @pl.when(d > 0)
    def _():
        to_prev.wait_send()

    xdev, ydev, cdev = (z * 4 + y * 2 + 1 - x, c), (z * 4 + (1 - y) * 2 + x, c), (k, 1 - c)
    zdev = {1: (jnp.minimum(k + 4, 15), c), -1: (jnp.maximum(k - 4, 0), c)}

    def gsl(chip, p):
        off, n = PARTS[p]
        return g_ref.at[chip, pl.ds(37 * c + off, n)]

    def src(chip, p, mine=False):
        off, n = PARTS[p]
        return chunk.at[pl.ds(off, n)] if mine else gsl(chip, p)

    def chip_of(zo, yo, xo):
        return zo * 4 + yo * 2 + xo

    def zcopy(zo, p, way, mine=False):
        chip = chip_of(zo, y, x)
        w = (way + 1) // 2
        return rcopy(src(chip, p, mine), gsl(chip, p), zs.at[w, zo, p], zr.at[zo, p], zdev[way])

    def xcopy(zo, yo, xo, p, mine=False):
        chip = chip_of(zo, yo, xo)
        s, r = (xas, xar) if p == 0 else (xbs, xbr)
        i = zo if p == 0 else zo * 2 + yo
        return rcopy(src(chip, p, mine), gsl(chip, p), s.at[i], r.at[i], xdev)

    def ycopy(zo, yo, xo, p, mine=False):
        chip = chip_of(zo, yo, xo)
        s, r = (ybs, ybr) if p == 1 else (yas, yar)
        i = zo if p == 1 else zo * 2 + xo
        return rcopy(src(chip, p, mine), gsl(chip, p), s.at[i], r.at[i], ydev)

    def ccopy(chip, p, mine=False):
        return rcopy(src(chip, p, mine), gsl(chip, p), cs.at[chip, p], cr.at[chip, p], cdev)

    pair_pads = rcopy(pads.at[pl.ds(c, 1)], pads.at[pl.ds(c, 1)], ksend.at[2], krecv.at[2], cdev)
    pair_pads.start()
    mine = [pltpu.make_async_copy(chunk.at[pl.ds(*PARTS[p])], gsl(k, p), own.at[p]) for p in (0, 1)]

    def own_z(way):
        for p in (0, 1):
            zcopy(z, p, way, True).start()

    def pass_on(zz, zo):
        way = 1 if zo < zz else -1
        for p in (0, 1):
            zcopy(zo, p, way).wait_recv()
            if 0 <= zz + way <= 3:
                zcopy(zo, p, way).start()

    def spread(zz, zo):
        xcopy(zo, y, x, 0).start()
        ycopy(zo, y, x, 1).start()
        ycopy(zo, y, x, 0).start()
        xcopy(zo, y, x, 1).start()
        for p in (0, 1):
            ccopy(chip_of(zo, y, x), p).start()

    def column(zz, zo):
        way = 1 if zo < zz else -1
        for p in (0, 1):
            zcopy(zo, p, way).wait_recv()
            if 0 <= zz + way <= 3:
                zcopy(zo, p, way).start()
            if p == 0:
                xcopy(zo, y, x, 0).start()
                ycopy(zo, y, x, 0).start()
            else:
                ycopy(zo, y, x, 1).start()
                xcopy(zo, y, x, 1).start()
            ccopy(chip_of(zo, y, x), p).start()

    def beside(zz, zo):
        xcopy(zo, y, 1 - x, 0).wait_recv()
        ycopy(zo, y, 1 - x, 0).start()
        ccopy(chip_of(zo, y, 1 - x), 0).start()
        ycopy(zo, 1 - y, x, 1).wait_recv()
        xcopy(zo, 1 - y, x, 1).start()
        ccopy(chip_of(zo, 1 - y, x), 1).start()

    def last(zz, zo):
        ycopy(zo, 1 - y, x, 0).wait_recv()
        ccopy(chip_of(zo, 1 - y, x), 0).start()
        xcopy(zo, y, 1 - x, 1).wait_recv()
        ccopy(chip_of(zo, y, 1 - x), 1).start()
        ycopy(zo, 1 - y, 1 - x, 0).wait_recv()
        ccopy(chip_of(zo, 1 - y, 1 - x), 0).start()
        xcopy(zo, 1 - y, 1 - x, 1).wait_recv()
        ccopy(chip_of(zo, 1 - y, 1 - x), 1).start()

    def raise_own(zz, zo):
        own_z(1)

    before = {
        0: ((beside, 0), (column, 1), (last, 0)),
        1: ((beside, 1), (column, 0), (raise_own, 1), (pass_on, 2), (last, 1), (beside, 0), (pass_on, 3), (spread, 2), (last, 0)),
        2: ((beside, 2), (pass_on, 3), (column, 0), (last, 2), (beside, 0), (column, 1), (last, 0)),
        3: ((beside, 3), (last, 3), (column, 0), (beside, 0), (column, 1), (last, 0)),
    }
    after = {
        0: {0: ((beside, 1), (column, 2)), 1: ((last, 1), (beside, 2)), 2: ((column, 3), (last, 2)), 3: ((beside, 3),), 4: ((last, 3),)},
        1: {0: ((beside, 2), (spread, 3)), 1: ((last, 2),), 2: ((beside, 3),), 3: ((last, 3),)},
        2: {0: ((beside, 1), (spread, 3)), 1: ((last, 1),), 2: ((beside, 3),), 3: ((last, 3),)},
        3: {0: ((beside, 1), (column, 2)), 1: ((last, 1),), 2: ((beside, 2),), 3: ((last, 2),)},
    }

    for way, holds in ((1, (z == 0) | (z == 2)), (-1, z > 0)):
        @pl.when(holds)
        def _():
            own_z(way)
    xcopy(z, y, x, 0, True).start()
    ycopy(z, y, x, 1, True).start()
    ycopy(z, y, x, 0, True).start()
    xcopy(z, y, x, 1, True).start()
    for p in (0, 1):
        mine[p].start()
        ccopy(k, p, True).start()
    for copy in inputs:
        copy.wait()
    pair_pads.wait()
    fill_codes(code, buckets_v, pads, lengths)
    outs = [pltpu.make_async_copy(code, code_out, osem.at[0])]
    outs[0].start()
    for zz in range(4):
        @pl.when(z == zz)
        def _():
            for f, zo in before[zz]:
                f(zz, zo)
    for p in (0, 1):
        mine[p].wait()

    def from_partner(chip):
        for p in (0, 1):
            off, n = PARTS[p]
            theirs = g_ref.at[chip, pl.ds(37 * (1 - c) + off, n)]
            rcopy(theirs, theirs, cs.at[chip, p], cr.at[chip, p], cdev).wait_recv()

    for chip in range(3):
        from_partner(chip)

    tiles = g_ref.reshape(16 * CHIP, 8, D)
    loads = [pltpu.make_async_copy(tiles.at[vector_at(ch)], vrows.at[i], wsem.at[i]) for i, ch in enumerate((0, 1))]
    loads += pieces(tiles, wl, 0, 16, wsem, 4) + pieces(tiles, wk, 112, 96, wsem, 8) + pieces(tiles, wq, 16, 96, wsem, 16)
    for copy in loads:
        copy.start()
    for copy in loads:
        copy.wait()
    vf[0] = vrows[0].astype(f32)
    vf[1] = vrows[1].astype(f32)
    fill_table(tab, vrows.at[0])
    h = tokens_v[...].astype(f32) + jnp.dot(feats_v[...], matrix(wl[...]), preferred_element_type=f32) + vf[0, 0:1, :]
    hidden_v[...] = h
    low_v[...] = h.astype(bf)
    half_rows = pl.ds(c * rows, rows)

    def share(ref, i):
        return rcopy(ref.at[half_rows], ref.at[half_rows], ksend.at[i], krecv.at[i], cdev)

    keys_v[half_rows, :] = jnp.dot(low_v[...], matrix(wk[...]), preferred_element_type=f32).astype(bf)
    share(keys_v, 0).start()
    query_v[...] = ((jnp.dot(low_v[...], matrix(wq[...]), preferred_element_type=f32) + vf[1, 0:1, :]) * 0.125).astype(bf)
    share(keys_v, 0).wait()
    outs += [pltpu.make_async_copy(v, r, osem.at[1 + i]) for i, (v, r) in enumerate(((hidden_v, hidden), (low_v, low), (query_v, query), (keys_v, keys)))]
    for copy in outs[1:]:
        copy.start()

    def make_values():
        for chip in (3, 4):
            from_partner(chip)
        copies = [pltpu.make_async_copy(tiles.at[vector_at(4)], vrows.at[2], wsem.at[2])] + pieces(tiles, wv, 208, 96, wsem, 12)
        for copy in copies:
            copy.start()
        for copy in copies:
            copy.wait()
        vf[2] = vrows[2].astype(f32)
        values_v[half_rows, :] = (jnp.dot(low_v[...], matrix(wv[...]), preferred_element_type=f32) + vf[2, 0:1, :]).astype(bf)
        share(values_v, 1).start()

    def keep(pair):
        return pltpu.make_async_copy(p_v.at[pl.ds(2 * pair, 2)], soft.at[pl.ds(2 * pair, 2)], psem.at[pair])

    def pair_of_heads(pair, _):
        lanes = pl.ds(pl.multiple_of(pair * 128, 128), 128)
        soft_pair(pair, query_v[:, lanes], keys_v[:, lanes], code, tab, s_scr, p_v.at[pl.ds(2 * pair, 2)])
        keep(pair).start()
        for i in range(5):
            for zz in range(4):
                if i in after[zz]:
                    @pl.when((pair == i) & (z == zz))
                    def _():
                        for f, zo in after[zz][i]:
                            f(zz, zo)
        pl.when(pair == 2)(make_values)
        return 0

    lax.fori_loop(0, H // 2, pair_of_heads, 0)
    share(values_v, 1).wait()
    outs.append(pltpu.make_async_copy(values_v, values, osem.at[5]))
    outs[-1].start()

    def context(pair, _):
        lanes = pl.ds(pl.multiple_of(pair * 128, 128), 128)
        ctx_v[:, lanes] = context_pair(values_v[:, lanes], p_v.at[pl.ds(2 * pair, 2)])
        return 0

    lax.fori_loop(0, H // 2, context, 0)
    outs.append(pltpu.make_async_copy(ctx_v, ctx, osem.at[6]))
    outs[-1].start()

    for p in (0, 1):
        for way in (1, -1):
            for zo in range(4):
                @pl.when(((z - zo) * way >= 0) & (z + way >= 0) & (z + way <= 3))
                def _():
                    zcopy(zo, p, way).wait_send()
    for zo in range(4):
        xcopy(zo, y, x, 0).wait_send()
        ycopy(zo, y, x, 1).wait_send()
        for o in range(2):
            ycopy(zo, y, o, 0).wait_send()
            xcopy(zo, o, x, 1).wait_send()
    for chip in range(16):
        for p in (0, 1):
            ccopy(chip, p).wait_send()
    for chip in range(5, 16):
        from_partner(chip)
    for pair in range(H // 2):
        keep(pair).wait()
    for copy in outs:
        copy.wait()


def gather_and_attend(master, tokens, feats, pad, buckets, page_lengths):
    x = jnp.pad(master, (0, ROWS * 128 - SHARD)).reshape(ROWS, 128)
    sem = pltpu.SemaphoreType.DMA
    any_, vm = pl.BlockSpec(memory_space=pl.ANY), pl.BlockSpec(memory_space=pltpu.VMEM)
    rows, key_rows = buckets.shape
    f32, bf = jnp.float32, jnp.bfloat16
    S, V = jax.ShapeDtypeStruct, pltpu.VMEM
    w = V((96, 8, D), bf)
    return pl.pallas_call(
        forward_kernel,
        out_shape=[
            S((16, CHIP, 8, D), bf), S((rows, D), f32), S((rows, D), bf), S((rows, D), bf), S((key_rows, D), bf), S((key_rows, D), bf),
            S((rows, D), bf), S((H, key_rows, rows), bf), S((key_rows, rows), jnp.int32),
        ],
        in_specs=[any_, any_, any_, vm, any_, pl.BlockSpec(memory_space=pltpu.SMEM)],
        out_specs=[any_] * 9,
        scratch_shapes=[
            V((ROWS, 128), f32), V((TAIL, 128), f32), V((HEAD, 128), f32), V((WIN, 128), f32), V((SLOTS, 8, D), bf),
            sem, sem((2,)), sem((2,)), sem((2,)),
            sem((2, 4, 2)), sem((4, 2)),
            sem((4,)), sem((4,)), sem((8,)), sem((8,)),
            sem((8,)), sem((8,)), sem((4,)), sem((4,)),
            sem((16, 2)), sem((16, 2)),
            V((2, 8, rows), jnp.int32), V((rows, D), f32), V((rows, D), bf), V((rows, D), bf), V((key_rows, D), bf), V((key_rows, D), bf),
            V((rows, D), bf), V((key_rows, rows), jnp.int32), V((rows, key_rows), jnp.int32), V((rows, D), bf), V((rows, LF), bf),
            V((H, key_rows, rows), bf), V((key_rows, rows), f32), V((16, 128), f32),
            V((16, 8, D), bf), w, w, w, V((3, 8, D), bf), V((3, 8, D), f32),
            sem((3,)), sem((3,)), sem((20,)), sem((3,)), sem((7,)), sem((H // 2,)),
        ],
        compiler_params=pltpu.CompilerParams(collective_id=0, has_side_effects=True, vmem_limit_bytes=60 << 20),
        name="gather_and_attend",
    )(x, tokens, feats, pad, buckets, page_lengths)


def guarded(cond, f):
    if cond is True:
        f()
    elif cond is not False:
        pl.when(cond)(f)


class Reducer:
    def __init__(self, where, zs, want, spare, g_ref, acc, crecv, a1, b1, a2, b2, asem, cs, cr, a1s, a1r, b1s, b1r, a2s, a2r, b2s, b2r):
        self.k, self.c, self.z, self.y, self.x = where
        self.zs, self.want, self.spare = zs, want, spare
        self.g_ref, self.acc, self.crecv = g_ref, acc, crecv
        self.bufs = (a1, b1, a2, b2)
        self.asem, self.cs, self.cr = asem, cs, cr
        self.sems = ((a1s, a1r), (b1s, b1r), (a2s, a2r), (b2s, b2r))
        z, y, x, c = self.z, self.y, self.x, self.c
        self.xdev, self.ydev, self.cdev = (z * 4 + y * 2 + 1 - x, c), (z * 4 + (1 - y) * 2 + x, c), (self.k, 1 - c)

    def at(self, zo, oy, ox):
        return zo, (1 - self.y if oy else self.y), (1 - self.x if ox else self.x)

    def chip(self, zo, yo, xo):
        return zo * 4 + yo * 2 + xo

    def local(self, zo, yo, xo):
        return self.chip(zo, yo, xo)

    def load(self, item):
        i = self.local(*item)
        return pltpu.make_async_copy(self.g_ref.at[self.chip(*item), pl.ds(37 * self.c, 37)], self.acc.at[i], self.asem.at[i])

    def ccopy(self, item):
        i = self.local(*item)
        return rcopy(self.g_ref.at[self.chip(*item), pl.ds(37 * (1 - self.c), 37)], self.crecv.at[i + self.spare], self.cs.at[i], self.cr.at[i], self.cdev)

    def hop(self, which, item, slot, p, dev):
        s, r = self.sems[which]
        return rcopy(self.acc.at[self.local(*item), pl.ds(*PARTS[p])], self.bufs[which].at[slot], s.at[slot], r.at[slot], dev)

    def a1(self, zo, xo):
        return self.hop(0, (zo, 1 - self.y, xo), self.zs.index(zo) * 2 + xo, 0, self.ydev)

    def b1(self, zo, yo):
        return self.hop(1, (zo, yo, 1 - self.x), self.zs.index(zo) * 2 + yo, 1, self.xdev)

    def a2(self, zo):
        return self.hop(2, (zo, self.y, 1 - self.x), self.zs.index(zo), 0, self.xdev)

    def b2(self, zo):
        return self.hop(3, (zo, 1 - self.y, self.x), self.zs.index(zo), 1, self.ydev)

    def gain(self, item, p, which, slot):
        off, n = PARTS[p]
        i, acc, buf = self.local(*item), self.acc, self.bufs[which]
        acc[i, pl.ds(off, n)] = acc[i, pl.ds(off, n)] + buf[slot]

    def begin(self, zo, oy, ox):
        item = self.at(zo, oy, ox)

        def go():
            self.load(item).start()
            self.ccopy(item).start()
        guarded(self.want(*item), go)

    def first(self, zo, oy, ox):
        item = self.at(zo, oy, ox)

        def go():
            self.load(item).wait()
            self.ccopy(item).wait_recv()
            i = self.local(*item)
            self.acc[i] = self.acc[i] + self.crecv[i + self.spare]
            if oy:
                self.a1(zo, item[2]).start()
            if ox:
                self.b1(zo, item[1]).start()
        guarded(self.want(*item), go)

    def second(self, zo):
        ia, ib = self.at(zo, 0, 1), self.at(zo, 1, 0)
        n = self.zs.index(zo) * 2

        def go_a():
            self.a1(zo, 1 - self.x).wait_recv()
            self.gain(ia, 0, 0, n + 1 - self.x)
            self.a2(zo).start()

        def go_b():
            self.b1(zo, 1 - self.y).wait_recv()
            self.gain(ib, 1, 1, n + 1 - self.y)
            self.b2(zo).start()
        guarded(self.want(*ia), go_a)
        guarded(self.want(*ib), go_b)

    def third(self, zo):
        item = self.at(zo, 0, 0)
        n = self.zs.index(zo)

        def go():
            self.a1(zo, self.x).wait_recv()
            self.b1(zo, self.y).wait_recv()
            self.a2(zo).wait_recv()
            self.b2(zo).wait_recv()
            i = self.local(*item)
            for p, (h, u), at in ((0, (0, 2), self.x), (1, (1, 3), self.y)):
                off, m = PARTS[p]
                self.acc[i, pl.ds(off, m)] = (self.acc[i, pl.ds(off, m)] + self.bufs[h][n * 2 + at]) + self.bufs[u][n]
        guarded(self.want(*item), go)

    def finish(self):
        for zo in self.zs:
            for oy in (0, 1):
                for ox in (0, 1):
                    item = self.at(zo, oy, ox)

                    def sent(item=item, oy=oy, ox=ox, zo=zo):
                        self.ccopy(item).wait_send()
                        if oy:
                            self.a1(zo, item[2]).wait_send()
                        if ox:
                            self.b1(zo, item[1]).wait_send()
                        if ox and not oy:
                            self.a2(zo).wait_send()
                        if oy and not ox:
                            self.b2(zo).wait_send()
                    guarded(self.want(*item), sent)


def reducer_scratch():
    bf, sem = jnp.bfloat16, pltpu.SemaphoreType.DMA
    tile = (8, D)
    return [
        pltpu.VMEM((16, 37) + tile, bf), pltpu.VMEM((11, 37) + tile, bf),
        pltpu.VMEM((8, 19) + tile, bf), pltpu.VMEM((8, 18) + tile, bf), pltpu.VMEM((4, 19) + tile, bf), pltpu.VMEM((4, 18) + tile, bf),
        sem((16,)), sem((16,)), sem((16,)),
        sem((8,)), sem((8,)), sem((8,)), sem((8,)), sem((4,)), sem((4,)), sem((4,)), sem((4,)),
    ]


def early_item(zo, yo, xo):
    return zo >= 2 if zo != 1 else yo + xo > 0


def late_item(zo, yo, xo):
    return zo == 0 if zo != 1 else yo + xo == 0


ZCUTS = ((0, 10), (10, 9), (19, 9), (28, 9))


class Chain:
    def __init__(self, where, acc, up, dn, us, ur, ds_, dr):
        self.k, self.c, self.z, self.y, self.x = where
        self.acc = acc
        self.ways = {1: (up, us, ur, (jnp.minimum(self.k + 4, 15), self.c)), -1: (dn, ds_, dr, (jnp.maximum(self.k - 4, 0), self.c))}

    def chip(self, zo):
        return zo * 4 + self.y * 2 + self.x

    def copy(self, zo, way, p):
        buf, s, r, dev = self.ways[way]
        part = pl.ds(*ZCUTS[p])
        return rcopy(self.acc.at[self.chip(zo), part], buf.at[zo, part], s.at[zo, p], r.at[zo, p], dev)

    def move(self, zs, zo, way, take=True, give=True, also=None):
        cond = self.z == zs if also is None else (self.z == zs) & also

        @pl.when(cond)
        def _():
            i = self.chip(zo)
            for p in range(4):
                if take:
                    self.copy(zo, way, p).wait_recv()
                    part = pl.ds(*ZCUTS[p])
                    self.acc[i, part] = self.acc[i, part] + self.ways[way][0][zo, part]
                if give:
                    self.copy(zo, way, p).start()

    def sent(self, zs, zo, way):
        @pl.when(self.z == zs)
        def _():
            for p in range(4):
                self.copy(zo, way, p).wait_send()


def chain_scratch():
    bf, sem = jnp.bfloat16, pltpu.SemaphoreType.DMA
    return [pltpu.VMEM((4, 37, 8, D), bf)] * 2 + [sem((4, 4))] * 4


def backward_kernel(tiles, q_ref, k_ref, v_ref, do_ref, p_hbm, code_hbm, gfi_in, low_in, feats_in, grads_in, m_ref, one_ref, two_ref,
                    grad_out, grads, step_ref, new1_ref, new2_ref, spread,
                    pbuf, qv, kv, vv, dov, psem, code_ref, csem, dsv, dssem, group, gsem, counts, dks, dvs, out, come, sends, recvs, back, bias,
                    wq, wk, wv, low, gfi, feats, dwl, dwq, dwk, dwv, vgrads, wsem, ssem, isem,
                    total, ebuf, sq, sqr, win, mv, onev, twov, lsem, es, er, qs, qr, *scratch):
    f32, bf = jnp.float32, jnp.bfloat16
    where = place()
    k, c, z, y, x = where
    d = 2 * k + c
    shared = grads.reshape(16, CHIP, 8, D)
    rs = Reducer(where, (0, 1, 2, 3), early_item, -5, shared, *scratch[:17])
    late = Reducer(where, (0, 1, 2, 3), late_item, 6, shared, *scratch[:17])
    acc = rs.acc
    zc = Chain(where, acc, *scratch[17:])
    xdev, ydev, cdev = rs.xdev, rs.ydev, rs.cdev
    column_devs = [((z + s) % 4 * 4 + y * 2 + x, c) for s in (1, 2, 3)]
    prev = (jnp.where(c == 1, k, jnp.maximum(k - 1, 0)), 1 - c)
    nxt = (jnp.where(c == 0, k, jnp.minimum(k + 1, 15)), 1 - c)
    bar = pltpu.get_barrier_semaphore()
    far_next, far_prev = (c == 1) & (k < 15), (c == 0) & (k > 0)
    for dev in [xdev, ydev, cdev] + column_devs:
        pl.semaphore_signal(bar, inc=1, device_id=dev, device_id_type=MESH)

    @pl.when(far_next)
    def _():
        pl.semaphore_signal(bar, inc=1, device_id=nxt, device_id_type=MESH)

    @pl.when(far_prev)
    def _():
        pl.semaphore_signal(bar, inc=1, device_id=prev, device_id_type=MESH)

    keys, rows = code_ref.shape

    def fetch_soft(pair, hh):
        return pltpu.make_async_copy(p_hbm.at[2 * pair + hh], pbuf.at[hh], psem.at[0, hh])

    def fetch(p):
        slot = p % 2
        lanes = pl.ds(pl.multiple_of(p * 128, 128), 128)
        return [pltpu.make_async_copy(r.at[:, lanes], v.at[slot], psem.at[1 + i, slot]) for i, (r, v) in enumerate(((q_ref, qv), (k_ref, kv), (v_ref, vv), (do_ref, dov)))]

    for copy in fetch(0) + [fetch_soft(0, 0), fetch_soft(0, 1)]:
        copy.start()
    pl.semaphore_wait(bar, 6 + jnp.where(far_next | far_prev, 1, 0))
    corners = ((1, 1), (1, 0), (0, 1), (0, 0))
    for zo in (3, 2):
        for oy, ox in corners:
            rs.begin(zo, oy, ox)
    code_copy = pltpu.make_async_copy(code_hbm, code_ref, csem.at[0])
    inputs = [pltpu.make_async_copy(r, v, isem.at[i]) for i, (r, v) in enumerate(((low_in, low), (gfi_in, gfi), (feats_in, feats)))]
    loads = pieces(tiles, wq, 16, 96, wsem, 8) + pieces(tiles, wv, 208, 96, wsem, 4) + pieces(tiles, wk, 112, 96, wsem, 0)
    shards = [pltpu.make_async_copy(r, v, lsem.at[i]) for i, (r, v) in enumerate(((m_ref, mv), (one_ref, onev), (two_ref, twov)))]
    for copy in [code_copy] + inputs + loads + shards:
        copy.start()
    own, other = pl.ds(c * rows, rows), pl.ds((1 - c) * rows, rows)

    def swap(pair):
        return rcopy(out.at[pair], come.at[pair], sends.at[pair], recvs.at[pair], cdev)

    def settle(pair):
        slot = pair % 2
        swap(pair).wait_recv()
        lanes = pl.ds(pl.multiple_of(pair * 128, 128), 128)
        dk = dks[slot, own, :] + come[pair, 0].astype(f32)
        dv = dvs[slot, own, :] + come[pair, 1].astype(f32)
        back[1, :, lanes] = dk.astype(bf)
        back[2, :, lanes] = dv.astype(bf)
        bias[1, :, lanes] = col_sum(dv)

    def lay(pair, hh):
        return pltpu.make_async_copy(dsv.at[hh], spread.at[:, 2 * pair + hh], dssem.at[hh])

    plan = {
        0: [(rs.first, 3, 1, 0), (rs.first, 3, 0, 1), (rs.first, 2, 1, 1)],
        1: [(rs.second, 3), (rs.first, 2, 1, 0), (rs.first, 2, 0, 1)],
        2: [(rs.first, 3, 0, 0), (rs.first, 2, 0, 0), (rs.begin, 1, 1, 1), (rs.begin, 1, 1, 0), (rs.begin, 1, 0, 1), (rs.begin, 1, 0, 0)],
        3: [(rs.second, 2), (rs.third, 3), (zc.move, 0, 3, 1, False)],
        4: [(rs.first, 1, 1, 1)],
        5: [(rs.first, 1, 1, 0), (rs.first, 1, 0, 1), (zc.move, 1, 3, 1)],
    }
    rs.first(3, 1, 1)

    def pair_of_heads(pair, _):
        slot = pair % 2

        @pl.when(pair < H // 2 - 1)
        def _():
            for copy in fetch(pair + 1):
                copy.start()

        for copy in fetch(pair):
            copy.wait()
        lanes = pl.ds(pl.multiple_of(pair * 128, 128), 128)
        dq = []
        for hh in range(2):
            fetch_soft(pair, hh).wait()
            qm = half(qv[slot], hh)
            dom = half(dov[slot], hh)
            g = lax.dot_general(vv[slot], dom, NT, preferred_element_type=f32)
            p = pbuf[hh]
            pf = p.astype(f32)
            inner = jnp.sum(jnp.sum((g * pf).reshape(keys // 8, 8, rows), axis=0), axis=0, keepdims=True)
            ds = (pf * (g - inner)).astype(bf)

            @pl.when(pair > 0)
            def _():
                lay(pair - 1, hh).wait()

            dsv[hh] = ds.reshape(keys // 8, 8, rows)
            lay(pair, hh).start()
            dv = jnp.dot(p, dom, preferred_element_type=f32)

            @pl.when(pair < H // 2 - 1)
            def _():
                fetch_soft(pair + 1, hh).start()

            dk = jnp.dot(ds, qm, preferred_element_type=f32)
            if hh == 0:
                dvs[slot] = dv
                dks[slot] = dk
            else:
                dvs[slot] += dv
                dks[slot] += dk
            dq.append(lax.dot_general(kv[slot], ds, TN, preferred_element_type=f32))
        out[pair, 0] = dks[slot, other, :].astype(bf)
        out[pair, 1] = dvs[slot, other, :].astype(bf)
        swap(pair).start()
        sub = lax.broadcasted_iota(jnp.int32, dq[0].shape, 0)
        dqf = jnp.where(sub < 64, dq[0], dq[1]).T * 0.125
        back[0, :, lanes] = dqf.astype(bf)
        bias[0, :, lanes] = col_sum(dqf)

        @pl.when(pair > 0)
        def _():
            settle(pair - 1)

        for i, steps in plan.items():
            @pl.when(pair == i)
            def _():
                for f, *a in steps:
                    f(*a)
        return 0

    lax.fori_loop(0, H // 2, pair_of_heads, 0)
    for hh in range(2):
        lay(H // 2 - 1, hh).wait()
    for copy in inputs + loads:
        copy.wait()

    def through(i, w, dw):
        dw[...] = lax.dot_general(low[...], back[i], TN, preferred_element_type=f32).astype(bf).reshape(96, 8, D)
        return lax.dot_general(back[i], matrix(w[...]), NT, preferred_element_type=f32)

    stores = []

    def keep(dw, first, count, base):
        made = pieces(grads, dw, first, count, ssem, base, True)
        for copy in made:
            copy.start()
        stores.extend(made)

    gfi[...] += through(0, wq, dwq)
    keep(dwq, 16, 96, 0)
    settle(H // 2 - 1)
    gfi[...] += through(2, wv, dwv)
    keep(dwv, 208, 96, 8)
    whole = gfi[...] + through(1, wk, dwk)
    keep(dwk, 112, 96, 4)
    gfi[...] = whole
    shown = pltpu.make_async_copy(gfi, grad_out, isem.at[6])
    shown.start()
    layout_bias = jnp.sum(col_sum(whole), axis=0, keepdims=True)
    dwl[...] = lax.dot_general(feats[...], whole.astype(bf), TN, preferred_element_type=f32).astype(bf).reshape(16, 8, D)
    keep(dwl, 0, 16, 12)

    def block(lines):
        return jnp.concatenate(lines + [jnp.zeros((8 - len(lines), D), f32)]).astype(bf)

    vgrads[0] = block([layout_bias])
    vgrads[1] = block([jnp.sum(bias[0], axis=0, keepdims=True)])
    vgrads[2] = block([jnp.sum(bias[1], axis=0, keepdims=True)])
    vgrads[3] = jnp.zeros((8, D), bf)
    held = {0: 0, 1: 1, 4: 2}
    for i, ch in enumerate((0, 1, 2, 3, 4)):
        copy = pltpu.make_async_copy(vgrads.at[held.get(ch, 3)], grads.at[vector_at(ch)], ssem.at[16 + i])
        copy.start()
        stores.append(copy)
    rs.third(2)
    zc.move(0, 2, 1, take=False)
    zc.move(3, 2, -1, take=False)
    for copy in stores:
        copy.wait()
    for oy, ox in corners:
        for zo in (1, 0):
            late.begin(zo, oy, ox)
    zc.move(2, 3, 1)

    GROUPS = 16

    def take_groups(i):
        return pltpu.make_async_copy(spread.at[pl.ds(i * GROUPS, GROUPS)], group.at[i % 2], gsem.at[i % 2])

    bucket = lax.broadcasted_iota(jnp.int32, (BUCKETS, rows), 0)
    steps = keys // 8 // GROUPS
    code_copy.wait()
    take_groups(0).start()
    counts[...] = jnp.zeros_like(counts)

    def count_some(first, n):
        for i in range(first, first + n):
            if i + 1 < steps:
                take_groups(i + 1).start()
            take_groups(i).wait()

            def count(j, run, i=i):
                code = code_ref[pl.ds(pl.multiple_of((i * GROUPS + j) * 8, 8), 8), :]
                hot = jnp.concatenate(
                    [jnp.where(jnp.broadcast_to(code[r : r + 1], bucket.shape) == bucket, 1.0, 0.0) for r in range(8)]
                ).astype(bf)
                return run + lax.dot_general(group[i % 2, j].reshape(8 * H, rows), hot, NT, preferred_element_type=f32)

            counts[...] = lax.fori_loop(0, GROUPS, count, counts[...], unroll=8)

    early_one, late_one = rs.want(1, y, x), late.want(1, y, x)
    for zo in (1, 0):
        late.first(zo, 1, 1)
    for oy, ox in ((1, 0), (0, 1)):
        for zo in (1, 0):
            late.first(zo, oy, ox)
    rs.second(1)
    rs.first(1, 0, 0)
    count_some(0, 2)
    zc.move(1, 2, 1)
    for zo in (1, 0):
        late.first(zo, 0, 0)
    rs.third(1)
    zc.move(0, 1, 1, take=False, also=early_one)
    zc.move(3, 1, -1, take=False, also=early_one)
    count_some(2, 2)
    for zo in (1, 0):
        late.second(zo)
    count_some(4, 2)
    zc.move(2, 1, -1, also=early_one)
    late.third(1)
    zc.move(0, 1, 1, take=False, also=late_one)
    zc.move(3, 1, -1, take=False, also=late_one)
    late.third(0)
    zc.move(3, 0, -1, take=False)
    count_some(6, 2)
    zc.move(2, 1, -1, also=late_one)
    zc.move(2, 0, -1)
    table = table_row(counts[...], (8, D))
    zc.move(1, 0, -1)

    total[...] = acc[k].astype(f32)

    def add(way, zo):
        buf = zc.ways[way][0]
        for p in range(4):
            zc.copy(zo, way, p).wait_recv()
        total[...] = total[...] + buf[zo].astype(f32)

    @pl.when(z == 0)
    def _():
        add(-1, 0)

    @pl.when(z == 1)
    def _():
        add(1, 1)
        add(-1, 1)

    @pl.when(z == 2)
    def _():
        add(1, 2)
        add(-1, 2)

    @pl.when(z == 3)
    def _():
        add(1, 3)

    early = early_vectors(k)
    nw0 = jnp.where(early, 36, 37)
    vecs = early == (c == 0)
    mine = jnp.where(vecs, 36, 37)
    to_next = rcopy(total.at[pl.ds(mine - EDGE, EDGE)], ebuf.at[0], es.at[0], er.at[0], nxt)
    to_prev = rcopy(total.at[pl.ds(0, EDGE)], ebuf.at[1], es.at[1], er.at[1], prev)

    @pl.when(d < 31)
    def _():
        to_next.start()

    @pl.when(d > 0)
    def _():
        to_prev.start()

    def square(i, run):
        t = total[i]
        t = t * t
        for j in range(6):
            run = run + t[:, 128 * j:128 * j + 128]
        return run

    squares = lax.fori_loop(0, 37, square, jnp.zeros((8, 128), f32))
    lines = [jnp.sum(squares, axis=0, keepdims=True)] + [table[0:1, 128 * i : 128 * i + 128] for i in range(3)]
    sq[0] = jnp.concatenate(lines + [jnp.zeros((4, 128), f32)])
    rounds = [rcopy(sq.at[i], sqr.at[i], qs.at[i], qr.at[i], dev) for i, dev in enumerate((cdev, xdev, ydev))]
    hops = [rcopy(sq.at[3], sqr.at[3 + i], qs.at[3 + i], qr.at[3 + i], column_devs[i]) for i in range(3)]
    rounds[0].start()
    q, sh = shard_start(d)
    base = q - FRONT

    def flatten(ref, i, at, wide):
        @pl.when(wide)
        def _():
            t = ref[i]
            for j in range(6):
                win[pl.ds(at + j, 8, stride=24), :] = t[:, 128 * j:128 * j + 128]

        @pl.when(jnp.logical_not(wide))
        def _():
            t = ref[i]
            for j in range(6):
                win[pl.ds(at + j, 8, stride=6), :] = t[:, 128 * j:128 * j + 128]

    own_vectors = vecs & (vector_row(k, -1) >= 0)

    @pl.when(own_vectors)
    def _():
        flatten(total, 36, vector_row(k, q) - base, k < 0)

    w0 = jnp.where(c == 0, 73 * k, 73 * k + nw0)

    @pl.loop(0, mine)
    def _(t):
        at, wide = tile_start(w0 + t)
        flatten(total, t, at - base, wide)

    rounds[0].wait_recv()
    sq[1] = sq[0] + sqr[0]
    rounds[1].start()
    @pl.when(d > 0)
    def _():
        to_next.wait_recv()

        @pl.loop(0, EDGE)
        def _(t):
            at, wide = tile_start(w0 - EDGE + t)
            flatten(ebuf.at[0], t, at - base, wide)

    @pl.when(d < 31)
    def _():
        to_prev.wait_recv()

        @pl.loop(0, EDGE)
        def _(t):
            at, wide = tile_start(w0 + mine + t)
            flatten(ebuf.at[1], t, at - base, wide)

    rounds[1].wait_recv()
    sq[2] = sq[1] + sqr[1]
    rounds[2].start()
    rounds[2].wait_recv()
    sq[3] = sq[2] + sqr[2]
    for h in hops:
        h.start()
    for h in hops:
        h.wait_recv()
    summed = (sq[3] + sqr[4]) + (sqr[3] + sqr[5])

    @pl.when(d == 0)
    def _():
        for i in range(3):
            win[pl.ds(FRONT + 774 + i, 1), :] = summed[1 + i : 2 + i]

    sub = lax.broadcasted_iota(jnp.int32, (8, 128), 0)
    entries = jnp.where(sub == 0, summed, jnp.where(sub < 4, summed * summed, 0.0))
    square_sum = jnp.sum(jnp.sum(entries, axis=1, keepdims=True), axis=0, keepdims=True)
    factor = jnp.minimum(1.0, lax.rsqrt(square_sum / RAW + 1e-06))
    for s in shards:
        s.wait()
    lanes = lax.broadcasted_iota(jnp.int32, (80, 128), 1)
    rowi = lax.broadcasted_iota(jnp.int32, (80, 128), 0)
    back = (128 - sh) % 128

    @pl.loop(0, ROWS // 80)
    def _(i):
        r = pl.multiple_of(i * 80, 8)
        here = pltpu.roll(win[pl.ds(FRONT + r, 80), :], back, 1)
        there = pltpu.roll(win[pl.ds(FRONT + 1 + r, 80), :], back, 1)
        grad = jnp.where(lanes < 128 - sh, here, there) * factor
        entry = (d == 0) & (rowi + r < ENTRY_ROWS)
        rate = jnp.where(entry, learn_rate * layer_decay, learn_rate)
        one = beta_one * onev[pl.ds(r, 80), :] + (1.0 - beta_one) * grad
        two = beta_two * twov[pl.ds(r, 80), :] + (1.0 - beta_two) * grad * grad
        fixed_one = one / (1.0 - beta_one ** STEP)
        fixed_two = two / (1.0 - beta_two ** STEP)
        step = -rate * (fixed_one / (jnp.sqrt(fixed_two) + adam_eps) + weight_decay * mv[pl.ds(r, 80), :])
        mv[pl.ds(r, 80), :] = step
        onev[pl.ds(r, 80), :] = one
        twov[pl.ds(r, 80), :] = two

    results = [pltpu.make_async_copy(v, r, lsem.at[i]) for i, (v, r) in enumerate(((mv, step_ref), (onev, new1_ref), (twov, new2_ref)))]
    for copy in results:
        copy.start()

    for h in rounds + hops:
        h.wait_send()

    @pl.when(d < 31)
    def _():
        to_next.wait_send()

    @pl.when(d > 0)
    def _():
        to_prev.wait_send()

    rs.finish()
    late.finish()
    for zs in (0, 1, 2):
        zc.sent(zs, 3, 1)
    for zs in (0, 1):
        zc.sent(zs, 2, 1)
    zc.sent(3, 2, -1)
    zc.sent(0, 1, 1)
    zc.sent(3, 1, -1)
    zc.sent(2, 1, -1)
    for zs in (1, 2, 3):
        zc.sent(zs, 0, -1)
    for pair in range(H // 2):
        swap(pair).wait_send()
    shown.wait()
    for copy in results:
        copy.wait()


def backward_and_step(tiles, query, key_all, value_all, grad_context, soft, code, gfi, low, feats, grads, master, first_moment, second_moment):
    def rows_of(v):
        return jnp.pad(v, (0, ROWS * 128 - SHARD)).reshape(ROWS, 128)

    rows, keys = query.shape[0], key_all.shape[0]
    f32, bf = jnp.float32, jnp.bfloat16
    any_ = pl.BlockSpec(memory_space=pl.ANY)
    S, V, sem = jax.ShapeDtypeStruct, pltpu.VMEM, pltpu.SemaphoreType.DMA
    w = V((96, 8, D), bf)
    tile = (8, D)
    line = V((ROWS, 128), f32)
    outs = pl.pallas_call(
        backward_kernel,
        out_shape=[S((rows, D), f32), S(grads.shape, bf)] + [S((ROWS, 128), f32)] * 3 + [S((keys // 8, H, 8, rows), bf)],
        in_specs=[any_] * 14,
        out_specs=[any_] * 6,
        scratch_shapes=[
            V((2, keys, rows), bf), V((2, rows, 128), bf), V((2, keys, 128), bf), V((2, keys, 128), bf), V((2, rows, 128), bf), sem((5, 2)),
            V((keys, rows), jnp.int32), sem((1,)), V((2, keys // 8, 8, rows), bf), sem((2,)), V((2, 16, H, 8, rows), bf), sem((2,)),
            V((8 * H, 8 * BUCKETS), f32),
            V((2, keys, 128), f32), V((2, keys, 128), f32), V((6, 2, rows, 128), bf), V((6, 2, rows, 128), bf), sem((6,)), sem((6,)),
            V((3, rows, D), bf), V((2, 8, D), f32),
            w, w, w, V((rows, D), bf), V((rows, D), f32), V((rows, LF), bf), V((16, 8, D), bf), w, w, w, V((4, 8, D), bf),
            sem((12,)), sem((24,)), sem((7,)),
            V((37,) + tile, f32), V((2, EDGE) + tile, f32), V((4, 8, 128), f32), V((6, 8, 128), f32),
            V((WIN2, 128), f32), line, line, line, sem((3,)), sem((2,)), sem((2,)), sem((6,)), sem((6,)),
        ] + reducer_scratch() + chain_scratch(),
        input_output_aliases={10: 1},
        compiler_params=pltpu.CompilerParams(collective_id=5, has_side_effects=True, vmem_limit_bytes=63 << 20),
        name="backward_and_step",
    )(tiles, query, key_all, value_all, grad_context, soft, code, gfi, low, feats, grads, rows_of(master), rows_of(first_moment), rows_of(second_moment))
    return outs[0], [o.reshape(-1)[:SHARD] for o in outs[2:5]]


def from_tiles(tiles):
    got = {}
    for name, first, count in WEIGHTS:
        block = jnp.concatenate([tiles[s : s + n] for s, _, n in slots_of(first, count)])
        if name == 12:
            block = block.reshape(96, 4, 8, D).transpose(0, 2, 1, 3)
        got[name] = block.reshape(-1, FF if name == 12 else D)
    for name, chip, row in VECTORS:
        block = tiles[vector_at(chip)]
        if name == 13:
            got[name] = block[row : row + 4].reshape(FF)
        elif name == 2:
            got[name] = block[row, : BUCKETS * H].reshape(BUCKETS, H)
        else:
            got[name] = block[row]
    return [got[i] for i in range(18)]


def to_tiles(whole):
    by_name = [p.astype(jnp.bfloat16) for p in whole]
    weights = []
    for name, first, count in WEIGHTS:
        got = by_name[name]
        if name == 12:
            got = got.reshape(96, 8, 4, D).transpose(0, 2, 1, 3)
        weights.append(got.reshape(count, 8, D))
    cuts = []
    for chip in range(16):
        held = [(r, by_name[n]) for n, c, r in VECTORS if c == chip]
        rows = [jnp.pad(v.reshape(-1), (0, -v.size % D)).reshape(-1, D) for _, v in held]
        block = jnp.concatenate(rows + [jnp.zeros((8 - sum(r.shape[0] for r in rows), D), jnp.bfloat16)])
        cuts.append((73 * chip + vector_slot(chip), block[None]))
    parts = []
    for (name, first, count), tiles in zip(WEIGHTS, weights):
        at = first
        for w, block in [c for c in cuts if first <= c[0] < first + count]:
            if w > at:
                parts.append(tiles[at - first : w - first])
            parts.append(block)
            at = w
        parts.append(tiles[at - first :])
    parts.extend(block for w, block in cuts if w == 1168)
    return jnp.concatenate(parts)


def per_device(
    custom, tokens, cotangent, page_boxes, page_lengths, padding, buckets, master, first_moment, second_moment
):
    rows = tokens.shape[1]
    feats = layout_features(page_boxes.reshape(4, rows)).astype(jnp.bfloat16)
    pad = jnp.broadcast_to(padding, (8, rows))
    if custom:
        tiles, hidden, low, query, keys, values, ctx, soft, code = gather_and_attend(
            master, tokens[0], feats, pad, buckets[0], page_lengths
        )
        tiles = tiles.reshape(16 * CHIP, 8, D)
    else:
        tiles = to_tiles(unpack(lax.all_gather(master.astype(jnp.bfloat16), ("dp", "seq"), axis=0, tiled=True)))
        hidden, low, query, keys, values, pads = enter(tiles, tokens[0], feats, pad)
        ctx, soft, code = attend(query, keys, values, buckets[0], page_lengths, pads, tiles[vector_at(0)])
    activations, grad_first_in, grad_context, grads = middle(tiles, ctx, hidden, cotangent[0])
    if custom:
        input_grad, stepped = backward_and_step(
            tiles, query, keys, values, grad_context, soft, code, grad_first_in, low, feats, grads, master, first_moment, second_moment
        )
    else:
        dq, dk, dv, table = soft_back(query, keys, values, grad_context, soft, code)
        input_grad, grads = leave(tiles, dq, dk, dv, grad_first_in, low, feats, table, grads)
        flat = jnp.concatenate([p.astype(jnp.float32).reshape(-1) for p in from_tiles(grads)])
        grad = lax.psum_scatter(flat, ("dp", "seq"), scatter_dimension=0, tiled=True)
        square = lax.psum(jnp.sum(grad * grad), ("dp", "seq"))
        factor = jnp.minimum(1.0, lax.rsqrt(square / RAW + 1e-06))
        size = master.shape[0]
        index = lax.axis_index(("dp", "seq")) * size + jnp.arange(size, dtype=jnp.int32)
        stepped = adam_update(master, first_moment, second_moment, grad * factor, index)
    return (activations[None], input_grad[None]) + tuple(stepped)


def solution(mesh):
    in_specs = (
        P("dp", "seq", None),
        P("dp", "seq", None),
        P(None, "dp", "seq"),
        P("dp", None),
        P("dp", "seq"),
        P("dp", "seq", None),
        P(("dp", "seq")),
        P(("dp", "seq")),
        P(("dp", "seq")),
    )
    out_specs = (
        P("dp", "seq", None),
        P("dp", "seq", None),
        P(("dp", "seq")),
        P(("dp", "seq")),
        P(("dp", "seq")),
    )
    custom = dict(mesh.shape) == {"dp": 16, "seq": 2}
    return jax.shard_map(
        functools.partial(per_device, custom), mesh=mesh, in_specs=in_specs, out_specs=out_specs, check_vma=False
    )
```

time: 303 us -> 269 us (0.89); the launches traced: 302 us -> 264 us
  Pallas kernels: 287 us -> 251 us
  local copies, waits for them, and re-layouts: 13.9 us -> 10.6 us
    pallas_call x6 -> x2, Pallas kernels: 253 us -> 217 us  [the longest x1 131 us: backward_and_step(): pl.pallas_call(backward_kernel, out_shape=[S((rows, D), f32), S(grads.sha...]
    unnamed x39 -> x17, local copies, waits for them, and re-layouts: 9.89 us -> 5.74 us
where the time goes in v2:
time: 269 us; the launch traced here: 264 us
  Pallas kernels  251 us (93%)
  local copies, waits for them, and re-layouts  10.6 us (4%)
    pallas_call x1, Pallas kernels, backward_and_step(): pl.pallas_call(backward_kernel, out_shape=[S((rows, D), f32), S(grads.sha...  131 us
    pallas_call x1, Pallas kernels, gather_and_attend(): pl.pallas_call(forward_kernel, out_shape=[S((16, CHIP, 8, D), bf), S((row...  86.2 us
    pallas_call x1, Pallas kernels, middle(): pl.pallas_call(middle_kernel, out_shape=[S((rows, D), bf), S((rows, D), f...  33.9 us
    unnamed x17, local copies, waits for them, and re-layouts  5.74 us

profile of v2, /device:TPU:0, one launch (start us, length us, event | category | flops | bytes accessed | tf_op | source)
XLA Modules:
  0.0 263.7 jit_solution(5320671457514439037)
XLA Ops:
  0.6 0.0 copy-start.5
  0.6 2.2 pad_bitcast_fusion.2.x_ref.m_ref
  2.8 0.7 convert_element_type.20
  3.5 0.5 fusion
  4.1 0.8 copy.16.feats.feats_in
  4.8 0.0 copy-done.5
  4.8 0.6 broadcast_in_dim.16.pad
  5.5 86.2 %gather_and_attend.1 = (bf16[16,74,8,768]{3,2,1,0:T(8,128)(2,1)}, f32[512,768]{1,0:T(8,128)}, bf16[512,768]{1,0:T(8,128)(2,1)}, bf16[512,768]{1,0:T(8,128)(2,1)}...) custom-call(f32[1760,128]{1,0:T(8,128)} %pad_bitcast_fusion.2.x_ref., ...), custom_call_target="tpu_custom_call" | custom-call | tf_op jit(solution)/shard_map/gather_and_attend/pallas_call | solution.py:1049
  91.7 0.0 copy-start
  91.7 0.0 copy-start.1
  91.7 33.9 %middle.1 = (bf16[512,768]{1,0:T(8,128)(2,1)}, f32[512,768]{1,0:T(8,128)}, bf16[512,768]{1,0:T(8,128)(2,1)}, bf16[1184,8,768]{2,1,0:T(8,128)(2,1)}) custom-call(bf16[1184,8,768]{2,1,0:T(8,128)(2,1)} %bitcast.25, bf16[512,768]{1,0:T(8,128)(2,1)} %get-tuple-element.23.ctx, f32[512,768]{1,0:T(8,128)} %get-tuple-element.24.hidden, bf16[512,768]{1,0:T(8,128)(2,1)} %bitcast.32), custom_call_target="tpu_custom_call" | custom-call | tf_op jit(solution)/shard_map/middle/pallas_call | solution.py:348
  125.6 0.0 copy-done
  125.7 0.0 copy-done.1
  125.7 1.3 pad_bitcast_fusion
  127.0 130.9 %backward_and_step.1 = (f32[512,768]{1,0:T(8,128)}, bf16[1184,8,768]{2,1,0:T(8,128)(2,1)}, f32[1760,128]{1,0:T(8,128)}, f32[1760,128]{1,0:T(8,128)}, f32[1760,12...) custom-call(bf16[1184,8,768]{2,1,0:T(8,128)(2,1)} %bitcast.26, ...), custom_call_target="tpu_custom_call", output_to_operand_aliasing={{1}: (10, {})} | custom-call | tf_op jit(solution)/shard_map/backward_and_step/pallas_call | solution.py:1711
  258.0 0.0 copy-start.4
  258.0 0.0 copy-start.3
  258.0 2.8 %copy.26 = f32[1,512,768]{2,1,0:T(8,128)} copy(f32[1,512,768]{2,1,0:T(8,128)} %bitcast.28) | data formatting | bytes 3145728
  260.8 0.0 copy-done.4
  260.8 1.0 copy.27
  261.7 0.0 copy-done.3
  261.7 1.0 copy.28
  262.7 0.0 copy-done.2
  262.7 1.0 copy.29
  (4 shorter events, 0.0 us)
Async XLA Ops:
  0.6 4.2 %copy-start.5 = (s32[1,512]{1,0:T(1,128)S(1)}, s32[1,512]{1,0:T(1,128)}, u32[]{:S(2)}) copy-start(s32[1,512]{1,0:T(1,128)} %param.13) | copy-start | bytes 6148
  91.7 34.0 %copy-start = (f32[224580]{0:T(1024)S(1)}, f32[224580]{0:T(1024)}, u32[]{:S(2)}) copy-start(f32[224580]{0:T(1024)} %param.17) | copy-start | bytes 2694964
  91.7 34.0 %copy-start.1 = (f32[224580]{0:T(1024)S(1)}, f32[224580]{0:T(1024)}, u32[]{:S(2)}) copy-start(f32[224580]{0:T(1024)} %param.16) | copy-start | bytes 2694964
  258.0 2.8 %copy-start.4 = (f32[1760,128]{1,0:T(8,128)S(1)}, f32[1760,128]{1,0:T(8,128)}, u32[]{:S(2)}) copy-start(f32[1760,128]{1,0:T(8,128)} %get-tuple-element.36) | copy-start | bytes 2703364
  258.0 3.8 %copy-start.3 = (f32[1760,128]{1,0:T(8,128)S(1)}, f32[1760,128]{1,0:T(8,128)}, u32[]{:S(2)}) copy-start(f32[1760,128]{1,0:T(8,128)} %get-tuple-element.37) | copy-start | bytes 2703364
  260.8 2.0 copy-start.2

commit v3 on v2

--- a/solution.py
+++ b/solution.py
@@ -369,7 +369,7 @@
 
 def half(ref_value, hh):
     lanes = lax.broadcasted_iota(jnp.int32, ref_value.shape, 1)
-    keep = lanes < 64 if hh == 0 else lanes >= 64
+    keep = lanes // 64 == hh
     return jnp.where(keep, ref_value, jnp.zeros_like(ref_value))
 
 
@@ -410,25 +410,24 @@
     tab_ref[...] = tab
 
 
-def soft_pair(pair, q, k, code_ref, tab_ref, s_scr, p_ref):
+def soft_head(head, q, k, code_ref, tab_ref, s_scr, p_ref):
     keys, rows = s_scr.shape
     f32, bf = jnp.float32, jnp.bfloat16
-    for hh in range(2):
-        qm = half(q, hh)
-        line = jnp.broadcast_to(tab_ref[pl.ds(2 * pair + hh, 1), :], (keys, 128))
-        s = lax.dot_general(k, qm, NT, preferred_element_type=f32)
-        cols = []
-        for j in range(rows // 128):
-            code = code_ref[:, 128 * j : 128 * j + 128]
-            bias = jnp.take_along_axis(line, code, axis=1, mode="promise_in_bounds")
-            cols.append(jnp.where(bias < 0.5 * masked_score, masked_score, s[:, 128 * j : 128 * j + 128] + bias))
-        s = jnp.concatenate(cols, axis=1)
-        s_scr[...] = s
-        top = jnp.max(jnp.max(s.reshape(keys // 8, 8, rows), axis=0), axis=0, keepdims=True)
-        e = jnp.exp(s_scr[...] - top)
-        s_scr[...] = e
-        inverse = 1.0 / jnp.sum(jnp.sum(e.reshape(keys // 8, 8, rows), axis=0), axis=0, keepdims=True)
-        p_ref[hh] = (s_scr[...] * inverse).astype(bf)
+    qm = half(q, head % 2)
+    line = jnp.broadcast_to(tab_ref[pl.ds(head, 1), :], (keys, 128))
+    s = lax.dot_general(k, qm, NT, preferred_element_type=f32)
+    cols = []
+    for j in range(rows // 128):
+        code = code_ref[:, 128 * j : 128 * j + 128]
+        bias = jnp.take_along_axis(line, code, axis=1, mode="promise_in_bounds")
+        cols.append(jnp.where(bias < 0.5 * masked_score, masked_score, s[:, 128 * j : 128 * j + 128] + bias))
+    s = jnp.concatenate(cols, axis=1)
+    s_scr[...] = s
+    top = jnp.max(jnp.max(s.reshape(keys // 8, 8, rows), axis=0), axis=0, keepdims=True)
+    e = jnp.exp(s_scr[...] - top)
+    s_scr[...] = e
+    inverse = 1.0 / jnp.sum(jnp.sum(e.reshape(keys // 8, 8, rows), axis=0), axis=0, keepdims=True)
+    p_ref[...] = (s_scr[...] * inverse).astype(bf)
 
 
 def context_pair(v, p_ref):
@@ -446,7 +445,8 @@
         fill_codes(code_ref, buckets, pads, lengths)
         fill_table(tab_ref, lines)
 
-    soft_pair(pair, q_ref[...], k_ref[...], code_ref, tab_ref, s_scr, p_ref)
+    for hh in range(2):
+        soft_head(2 * pair + hh, q_ref[...], k_ref[...], code_ref, tab_ref, s_scr, p_ref.at[hh])
     ctx_ref[...] = context_pair(v_ref[...], p_ref)
 
 
@@ -989,7 +989,8 @@
 
     def pair_of_heads(pair, _):
         lanes = pl.ds(pl.multiple_of(pair * 128, 128), 128)
-        soft_pair(pair, query_v[:, lanes], keys_v[:, lanes], code, tab, s_scr, p_v.at[pl.ds(2 * pair, 2)])
+        for hh in range(2):
+            soft_head(2 * pair + hh, query_v[:, lanes], keys_v[:, lanes], code, tab, s_scr, p_v.at[2 * pair + hh])
         keep(pair).start()
         for i in range(5):
             for zz in range(4):
@@ -1339,8 +1340,7 @@
         1: [(rs.second, 3), (rs.first, 2, 1, 0), (rs.first, 2, 0, 1)],
         2: [(rs.first, 3, 0, 0), (rs.first, 2, 0, 0), (rs.begin, 1, 1, 1), (rs.begin, 1, 1, 0), (rs.begin, 1, 0, 1), (rs.begin, 1, 0, 0)],
         3: [(rs.second, 2), (rs.third, 3), (zc.move, 0, 3, 1, False)],
-        4: [(rs.first, 1, 1, 1)],
-        5: [(rs.first, 1, 1, 0), (rs.first, 1, 0, 1), (zc.move, 1, 3, 1)],
+        5: [(rs.third, 2), (zc.move, 0, 2, 1, False), (zc.move, 3, 2, -1, False), (zc.move, 1, 3, 1)],
     }
     rs.first(3, 1, 1)
 
@@ -1449,15 +1449,11 @@
         copy = pltpu.make_async_copy(vgrads.at[held.get(ch, 3)], grads.at[vector_at(ch)], ssem.at[16 + i])
         copy.start()
         stores.append(copy)
-    rs.third(2)
-    zc.move(0, 2, 1, take=False)
-    zc.move(3, 2, -1, take=False)
     for copy in stores:
         copy.wait()
     for oy, ox in corners:
-        for zo in (1, 0):
+        for zo in (0, 1):
             late.begin(zo, oy, ox)
-    zc.move(2, 3, 1)
 
     GROUPS = 16
 
@@ -1486,35 +1482,39 @@
             counts[...] = lax.fori_loop(0, GROUPS, count, counts[...], unroll=8)
 
     early_one, late_one = rs.want(1, y, x), late.want(1, y, x)
-    for zo in (1, 0):
-        late.first(zo, 1, 1)
-    for oy, ox in ((1, 0), (0, 1)):
-        for zo in (1, 0):
-            late.first(zo, oy, ox)
+    for oy, ox in corners[:3]:
+        late.first(0, oy, ox)
+    for oy, ox in corners[:3]:
+        late.first(1, oy, ox)
+    late.second(0)
+    late.second(1)
+    rs.first(1, 1, 1)
+    rs.first(1, 1, 0)
+    rs.first(1, 0, 1)
+    late.first(0, 0, 0)
+    zc.move(2, 3, 1)
+    count_some(0, 1)
+    late.third(0)
+    zc.move(3, 0, -1, take=False)
+    late.first(1, 0, 0)
+    late.third(1)
+    zc.move(0, 1, 1, take=False, also=late_one)
+    zc.move(3, 1, -1, take=False, also=late_one)
     rs.second(1)
     rs.first(1, 0, 0)
-    count_some(0, 2)
     zc.move(1, 2, 1)
-    for zo in (1, 0):
-        late.first(zo, 0, 0)
+    count_some(1, 1)
+    zc.move(2, 0, -1)
+    zc.move(2, 1, -1, also=late_one)
+    count_some(2, 2)
+    zc.move(1, 0, -1)
     rs.third(1)
     zc.move(0, 1, 1, take=False, also=early_one)
     zc.move(3, 1, -1, take=False, also=early_one)
-    count_some(2, 2)
-    for zo in (1, 0):
-        late.second(zo)
-    count_some(4, 2)
+    count_some(4, 3)
     zc.move(2, 1, -1, also=early_one)
-    late.third(1)
-    zc.move(0, 1, 1, take=False, also=late_one)
-    zc.move(3, 1, -1, take=False, also=late_one)
-    late.third(0)
-    zc.move(3, 0, -1, take=False)
-    count_some(6, 2)
-    zc.move(2, 1, -1, also=late_one)
-    zc.move(2, 0, -1)
+    count_some(7, 1)
     table = table_row(counts[...], (8, D))
-    zc.move(1, 0, -1)
 
     total[...] = acc[k].astype(f32)
 

time: 269 us -> 257 us (0.955); the launches traced: 264 us -> 257 us
  Pallas kernels: 251 us -> 244 us
    pallas_call x1, Pallas kernels: 131 us -> 124 us  [backward_and_step(): pl.pallas_call(backward_kernel, out_shape=[S((rows, D), f32), S(grads.sha...]
where the time goes in v3:
time: 257 us
  Pallas kernels  244 us (95%)
  local copies, waits for them, and re-layouts  10.6 us (4%)
    pallas_call x1, Pallas kernels, backward_and_step(): pl.pallas_call(backward_kernel, out_shape=[S((rows, D), f32), S(grads.sha...  124 us
    pallas_call x1, Pallas kernels, gather_and_attend(): pl.pallas_call(forward_kernel, out_shape=[S((16, CHIP, 8, D), bf), S((row...  86.2 us
    pallas_call x1, Pallas kernels, middle(): pl.pallas_call(middle_kernel, out_shape=[S((rows, D), bf), S((rows, D), f...  33.9 us
    unnamed x17, local copies, waits for them, and re-layouts  5.74 us

profile of v3, /device:TPU:0, one launch (start us, length us, event | category | flops | bytes accessed | tf_op | source)
XLA Modules:
  0.0 256.6 jit_solution(13843271696376819970)
XLA Ops:
  0.6 0.0 copy-start.5
  0.6 2.2 pad_bitcast_fusion.2.x_ref.m_ref
  2.8 0.7 convert_element_type.20
  3.5 0.5 fusion
  4.1 0.8 copy.16.feats.feats_in
  4.8 0.0 copy-done.5
  4.8 0.6 broadcast_in_dim.16.pad
  5.5 86.2 %gather_and_attend.1 = (bf16[16,74,8,768]{3,2,1,0:T(8,128)(2,1)}, f32[512,768]{1,0:T(8,128)}, bf16[512,768]{1,0:T(8,128)(2,1)}, bf16[512,768]{1,0:T(8,128)(2,1)}...) custom-call(f32[1760,128]{1,0:T(8,128)} %pad_bitcast_fusion.2.x_ref., ...), custom_call_target="tpu_custom_call" | custom-call | tf_op jit(solution)/shard_map/gather_and_attend/pallas_call | solution.py:1050
  91.6 0.0 copy-start
  91.6 0.0 copy-start.1
  91.7 33.9 %middle.1 = (bf16[512,768]{1,0:T(8,128)(2,1)}, f32[512,768]{1,0:T(8,128)}, bf16[512,768]{1,0:T(8,128)(2,1)}, bf16[1184,8,768]{2,1,0:T(8,128)(2,1)}) custom-call(bf16[1184,8,768]{2,1,0:T(8,128)(2,1)} %bitcast.25, bf16[512,768]{1,0:T(8,128)(2,1)} %get-tuple-element.23.ctx, f32[512,768]{1,0:T(8,128)} %get-tuple-element.24.hidden, bf16[512,768]{1,0:T(8,128)(2,1)} %bitcast.32), custom_call_target="tpu_custom_call" | custom-call | tf_op jit(solution)/shard_map/middle/pallas_call | solution.py:348
  125.6 0.0 copy-done
  125.6 0.0 copy-done.1
  125.6 1.3 pad_bitcast_fusion
  127.0 123.9 %backward_and_step.1 = (f32[512,768]{1,0:T(8,128)}, bf16[1184,8,768]{2,1,0:T(8,128)(2,1)}, f32[1760,128]{1,0:T(8,128)}, f32[1760,128]{1,0:T(8,128)}, f32[1760,12...) custom-call(bf16[1184,8,768]{2,1,0:T(8,128)(2,1)} %bitcast.26, ...), custom_call_target="tpu_custom_call", output_to_operand_aliasing={{1}: (10, {})} | custom-call | tf_op jit(solution)/shard_map/backward_and_step/pallas_call | solution.py:1711
  250.8 0.0 copy-start.4
  250.8 0.0 copy-start.3
  250.9 2.8 %copy.26 = f32[1,512,768]{2,1,0:T(8,128)} copy(f32[1,512,768]{2,1,0:T(8,128)} %bitcast.28) | data formatting | bytes 3145728
  253.6 0.0 copy-done.4
  253.6 1.0 copy.27
  254.6 0.0 copy-done.3
  254.6 1.0 copy.28
  255.6 0.0 copy-done.2
  255.6 1.0 copy.29
  (4 shorter events, 0.0 us)
Async XLA Ops:
  0.6 4.2 %copy-start.5 = (s32[1,512]{1,0:T(1,128)S(1)}, s32[1,512]{1,0:T(1,128)}, u32[]{:S(2)}) copy-start(s32[1,512]{1,0:T(1,128)} %param.13) | copy-start | bytes 6148
  91.6 34.0 %copy-start = (f32[224580]{0:T(1024)S(1)}, f32[224580]{0:T(1024)}, u32[]{:S(2)}) copy-start(f32[224580]{0:T(1024)} %param.17) | copy-start | bytes 2694964
  91.6 34.0 %copy-start.1 = (f32[224580]{0:T(1024)S(1)}, f32[224580]{0:T(1024)}, u32[]{:S(2)}) copy-start(f32[224580]{0:T(1024)} %param.16) | copy-start | bytes 2694964
  250.8 2.8 %copy-start.4 = (f32[1760,128]{1,0:T(8,128)S(1)}, f32[1760,128]{1,0:T(8,128)}, u32[]{:S(2)}) copy-start(f32[1760,128]{1,0:T(8,128)} %get-tuple-element.36) | copy-start | bytes 2703364
  250.8 3.8 %copy-start.3 = (f32[1760,128]{1,0:T(8,128)S(1)}, f32[1760,128]{1,0:T(8,128)}, u32[]{:S(2)}) copy-start(f32[1760,128]{1,0:T(8,128)} %get-tuple-element.37) | copy-start | bytes 2703364
  253.6 2.0 copy-start.2

commit v4 on v3

--- a/solution.py
+++ b/solution.py
@@ -896,33 +896,51 @@
         xcopy(zo, 1 - y, 1 - x, 1).wait_recv()
         ccopy(chip_of(zo, 1 - y, 1 - x), 1).start()
 
-    def raise_own(zz, zo):
+    def own_first(zz, zo):
+        xcopy(z, y, x, 0, True).start()
+        ycopy(z, y, x, 1, True).start()
+
+    def own_second(zz, zo):
+        ycopy(z, y, x, 0, True).start()
+        xcopy(z, y, x, 1, True).start()
+        for p in (0, 1):
+            ccopy(k, p, True).start()
+
+    def values_now(zz, zo):
+        make_values()
+
+    def own_up(zz, zo):
         own_z(1)
 
+    def own_down(zz, zo):
+        own_z(-1)
+
+    begin = {
+        0: ((own_up, 0), (own_first, 0), (own_second, 0)),
+        1: ((own_first, 1), (own_down, 1)),
+        2: ((own_up, 2), (own_down, 2), (own_first, 2)),
+        3: ((own_down, 3), (own_first, 3)),
+    }
     before = {
         0: ((beside, 0), (column, 1), (last, 0)),
-        1: ((beside, 1), (column, 0), (raise_own, 1), (pass_on, 2), (last, 1), (beside, 0), (pass_on, 3), (spread, 2), (last, 0)),
-        2: ((beside, 2), (pass_on, 3), (column, 0), (last, 2), (beside, 0), (column, 1), (last, 0)),
-        3: ((beside, 3), (last, 3), (column, 0), (beside, 0), (column, 1), (last, 0)),
+        1: ((column, 0), (own_up, 1), (beside, 0), (column, 3), (column, 2), (last, 0)),
+        2: ((column, 3), (pass_on, 0), (spread, 0), (beside, 0), (column, 1), (own_second, 2), (last, 0)),
+        3: ((column, 2), (column, 0), (beside, 0), (beside, 2), (last, 0), (column, 1), (beside, 3)),
     }
     after = {
-        0: {0: ((beside, 1), (column, 2)), 1: ((last, 1), (beside, 2)), 2: ((column, 3), (last, 2)), 3: ((beside, 3),), 4: ((last, 3),)},
-        1: {0: ((beside, 2), (spread, 3)), 1: ((last, 2),), 2: ((beside, 3),), 3: ((last, 3),)},
-        2: {0: ((beside, 1), (spread, 3)), 1: ((last, 1),), 2: ((beside, 3),), 3: ((last, 3),)},
-        3: {0: ((beside, 1), (column, 2)), 1: ((last, 1),), 2: ((beside, 2),), 3: ((last, 2),)},
+        0: {-1: ((column, 3), (beside, 1)), 1: ((beside, 3),), 2: ((last, 1), (column, 2)), 8: ((values_now, 0), (beside, 2)), 10: ((last, 3),), 11: ((last, 2),)},
+        1: {4: ((own_second, 1),), 6: ((beside, 1), (beside, 3)), 7: ((beside, 2),), 8: ((last, 1), (values_now, 0)), 10: ((last, 3),), 11: ((last, 2),)},
+        2: {2: ((beside, 1),), 4: ((beside, 2),), 6: ((last, 1), (beside, 3)), 10: ((last, 2),), 11: ((values_now, 0), (last, 3))},
+        3: {5: ((last, 2), (beside, 1)), 8: ((own_second, 3),), 9: ((last, 1),), 11: ((last, 3), (values_now, 0))},
     }
 
-    for way, holds in ((1, (z == 0) | (z == 2)), (-1, z > 0)):
-        @pl.when(holds)
-        def _():
-            own_z(way)
-    xcopy(z, y, x, 0, True).start()
-    ycopy(z, y, x, 1, True).start()
-    ycopy(z, y, x, 0, True).start()
-    xcopy(z, y, x, 1, True).start()
     for p in (0, 1):
         mine[p].start()
-        ccopy(k, p, True).start()
+    for zz in range(4):
+        @pl.when(z == zz)
+        def _():
+            for f, zo in begin[zz]:
+                f(zz, zo)
     for copy in inputs:
         copy.wait()
     pair_pads.wait()
@@ -987,22 +1005,31 @@
     def keep(pair):
         return pltpu.make_async_copy(p_v.at[pl.ds(2 * pair, 2)], soft.at[pl.ds(2 * pair, 2)], psem.at[pair])
 
-    def pair_of_heads(pair, _):
-        lanes = pl.ds(pl.multiple_of(pair * 128, 128), 128)
-        for hh in range(2):
-            soft_head(2 * pair + hh, query_v[:, lanes], keys_v[:, lanes], code, tab, s_scr, p_v.at[2 * pair + hh])
-        keep(pair).start()
-        for i in range(5):
-            for zz in range(4):
+    for zz in range(4):
+        if -1 in after[zz]:
+            @pl.when(z == zz)
+            def _():
+                for f, zo in after[zz][-1]:
+                    f(zz, zo)
+
+    def one_head(head, _):
+        lanes = pl.ds(pl.multiple_of(head // 2 * 128, 128), 128)
+        soft_head(head, query_v[:, lanes], keys_v[:, lanes], code, tab, s_scr, p_v.at[head])
+
+        @pl.when(head % 2 == 1)
+        def _():
+            keep(head // 2).start()
+
+        for zz in range(4):
+            for i in range(H):
                 if i in after[zz]:
-                    @pl.when((pair == i) & (z == zz))
+                    @pl.when((head == i) & (z == zz))
                     def _():
                         for f, zo in after[zz][i]:
                             f(zz, zo)
-        pl.when(pair == 2)(make_values)
         return 0
 
-    lax.fori_loop(0, H // 2, pair_of_heads, 0)
+    lax.fori_loop(0, H, one_head, 0)
     share(values_v, 1).wait()
     outs.append(pltpu.make_async_copy(values_v, values, osem.at[5]))
     outs[-1].start()
@@ -1308,9 +1335,8 @@
         copy.start()
     pl.semaphore_wait(bar, 6 + jnp.where(far_next | far_prev, 1, 0))
     corners = ((1, 1), (1, 0), (0, 1), (0, 0))
-    for zo in (3, 2):
-        for oy, ox in corners:
-            rs.begin(zo, oy, ox)
+    for oy, ox in corners:
+        rs.begin(2, oy, ox)
     code_copy = pltpu.make_async_copy(code_hbm, code_ref, csem.at[0])
     inputs = [pltpu.make_async_copy(r, v, isem.at[i]) for i, (r, v) in enumerate(((low_in, low), (gfi_in, gfi), (feats_in, feats)))]
     loads = pieces(tiles, wq, 16, 96, wsem, 8) + pieces(tiles, wv, 208, 96, wsem, 4) + pieces(tiles, wk, 112, 96, wsem, 0)
@@ -1336,13 +1362,15 @@
         return pltpu.make_async_copy(dsv.at[hh], spread.at[:, 2 * pair + hh], dssem.at[hh])
 
     plan = {
-        0: [(rs.first, 3, 1, 0), (rs.first, 3, 0, 1), (rs.first, 2, 1, 1)],
-        1: [(rs.second, 3), (rs.first, 2, 1, 0), (rs.first, 2, 0, 1)],
-        2: [(rs.first, 3, 0, 0), (rs.first, 2, 0, 0), (rs.begin, 1, 1, 1), (rs.begin, 1, 1, 0), (rs.begin, 1, 0, 1), (rs.begin, 1, 0, 0)],
-        3: [(rs.second, 2), (rs.third, 3), (zc.move, 0, 3, 1, False)],
-        5: [(rs.third, 2), (zc.move, 0, 2, 1, False), (zc.move, 3, 2, -1, False), (zc.move, 1, 3, 1)],
+        0: [(rs.first, 2, 0, 0), (rs.first, 2, 0, 1), (rs.first, 2, 1, 0), (rs.first, 3, 1, 1), (rs.begin, 1, 1, 1), (rs.begin, 1, 1, 0), (rs.begin, 1, 0, 1), (rs.begin, 1, 0, 0)],
+        1: [(rs.first, 3, 1, 0), (rs.first, 3, 0, 0), (rs.second, 2), (rs.first, 1, 1, 1), (rs.first, 3, 0, 1)],
+        5: [(rs.second, 3)],
     }
-    rs.first(3, 1, 1)
+    rs.begin(3, 1, 1)
+    rs.begin(3, 1, 0)
+    rs.begin(3, 0, 1)
+    rs.begin(3, 0, 0)
+    rs.first(2, 1, 1)
 
     def pair_of_heads(pair, _):
         slot = pair % 2
@@ -1482,38 +1510,48 @@
             counts[...] = lax.fori_loop(0, GROUPS, count, counts[...], unroll=8)
 
     early_one, late_one = rs.want(1, y, x), late.want(1, y, x)
-    for oy, ox in corners[:3]:
-        late.first(0, oy, ox)
-    for oy, ox in corners[:3]:
-        late.first(1, oy, ox)
+    count_some(0, 1)
+    late.first(0, 1, 1)
+    late.first(1, 1, 1)
+    late.first(0, 1, 0)
+    late.first(1, 1, 0)
+    rs.third(3)
+    zc.move(0, 3, 1, take=False)
+    late.first(0, 0, 1)
+    late.first(1, 0, 1)
+    rs.third(2)
+    count_some(1, 1)
+    zc.move(1, 3, 1)
+    count_some(2, 1)
+    zc.move(3, 2, -1, take=False)
+    count_some(3, 1)
     late.second(0)
     late.second(1)
-    rs.first(1, 1, 1)
+    rs.first(1, 0, 0)
+    count_some(4, 1)
     rs.first(1, 1, 0)
     rs.first(1, 0, 1)
+    rs.second(1)
     late.first(0, 0, 0)
+    late.first(1, 0, 0)
+    count_some(5, 1)
+    zc.move(0, 2, 1, take=False)
+    count_some(6, 1)
+    zc.move(1, 2, 1)
     zc.move(2, 3, 1)
-    count_some(0, 1)
     late.third(0)
+    zc.move(1, 0, -1)
+    zc.move(2, 0, -1)
     zc.move(3, 0, -1, take=False)
-    late.first(1, 0, 0)
     late.third(1)
     zc.move(0, 1, 1, take=False, also=late_one)
     zc.move(3, 1, -1, take=False, also=late_one)
-    rs.second(1)
-    rs.first(1, 0, 0)
-    zc.move(1, 2, 1)
-    count_some(1, 1)
-    zc.move(2, 0, -1)
     zc.move(2, 1, -1, also=late_one)
-    count_some(2, 2)
-    zc.move(1, 0, -1)
     rs.third(1)
     zc.move(0, 1, 1, take=False, also=early_one)
     zc.move(3, 1, -1, take=False, also=early_one)
-    count_some(4, 3)
+    count_some(7, 1)
     zc.move(2, 1, -1, also=early_one)
-    count_some(7, 1)
     table = table_row(counts[...], (8, D))
 
     total[...] = acc[k].astype(f32)

time: 257 us -> 240 us (0.934)
  Pallas kernels: 244 us -> 226 us
    pallas_call x1, Pallas kernels: 124 us -> 110 us  [backward_and_step(): pl.pallas_call(backward_kernel, out_shape=[S((rows, D), f32), S(grads.sha...]
    pallas_call x1, Pallas kernels: 86.2 us -> 81.6 us  [gather_and_attend(): pl.pallas_call(forward_kernel, out_shape=[S((16, CHIP, 8, D), bf), S((row...]
where the time goes in v4:
time: 240 us; the launch traced here: 239 us
  Pallas kernels  226 us (94%)
  local copies, waits for them, and re-layouts  10.6 us (4%)
    pallas_call x1, Pallas kernels, backward_and_step(): pl.pallas_call(backward_kernel, out_shape=[S((rows, D), f32), S(grads.sha...  110 us
    pallas_call x1, Pallas kernels, gather_and_attend(): pl.pallas_call(forward_kernel, out_shape=[S((16, CHIP, 8, D), bf), S((row...  81.6 us
    pallas_call x1, Pallas kernels, middle(): pl.pallas_call(middle_kernel, out_shape=[S((rows, D), bf), S((rows, D), f...  33.9 us
    unnamed x17, local copies, waits for them, and re-layouts  5.74 us

profile of v4, /device:TPU:0, one launch (start us, length us, event | category | flops | bytes accessed | tf_op | source)
XLA Modules:
  0.0 238.6 jit_solution(6972495724276482455)
XLA Ops:
  0.6 0.0 copy-start.5
  0.6 2.2 pad_bitcast_fusion.2.x_ref.m_ref
  2.8 0.7 convert_element_type.20
  3.5 0.5 fusion
  4.1 0.8 copy.16.feats.feats_in
  4.8 0.0 copy-done.5
  4.8 0.6 broadcast_in_dim.16.pad
  5.5 81.6 %gather_and_attend.1 = (bf16[16,74,8,768]{3,2,1,0:T(8,128)(2,1)}, f32[512,768]{1,0:T(8,128)}, bf16[512,768]{1,0:T(8,128)(2,1)}, bf16[512,768]{1,0:T(8,128)(2,1)}...) custom-call(f32[1760,128]{1,0:T(8,128)} %pad_bitcast_fusion.2.x_ref., ...), custom_call_target="tpu_custom_call" | custom-call | tf_op jit(solution)/shard_map/gather_and_attend/pallas_call | solution.py:1077
  87.1 0.0 copy-start
  87.1 0.0 copy-start.1
  87.1 33.9 %middle.1 = (bf16[512,768]{1,0:T(8,128)(2,1)}, f32[512,768]{1,0:T(8,128)}, bf16[512,768]{1,0:T(8,128)(2,1)}, bf16[1184,8,768]{2,1,0:T(8,128)(2,1)}) custom-call(bf16[1184,8,768]{2,1,0:T(8,128)(2,1)} %bitcast.25, bf16[512,768]{1,0:T(8,128)(2,1)} %get-tuple-element.23.ctx, f32[512,768]{1,0:T(8,128)} %get-tuple-element.24.hidden, bf16[512,768]{1,0:T(8,128)(2,1)} %bitcast.32), custom_call_target="tpu_custom_call" | custom-call | tf_op jit(solution)/shard_map/middle/pallas_call | solution.py:348
  121.0 0.0 copy-done
  121.0 0.0 copy-done.1
  121.0 1.3 pad_bitcast_fusion
  122.4 110.5 %backward_and_step.1 = (f32[512,768]{1,0:T(8,128)}, bf16[1184,8,768]{2,1,0:T(8,128)(2,1)}, f32[1760,128]{1,0:T(8,128)}, f32[1760,128]{1,0:T(8,128)}, f32[1760,12...) custom-call(bf16[1184,8,768]{2,1,0:T(8,128)(2,1)} %bitcast.26, ...), custom_call_target="tpu_custom_call", output_to_operand_aliasing={{1}: (10, {})} | custom-call | tf_op jit(solution)/shard_map/backward_and_step/pallas_call | solution.py:1749
  232.9 0.0 copy-start.4
  232.9 0.0 copy-start.3
  232.9 2.8 %copy.26 = f32[1,512,768]{2,1,0:T(8,128)} copy(f32[1,512,768]{2,1,0:T(8,128)} %bitcast.28) | data formatting | bytes 3145728
  235.7 0.0 copy-done.4
  235.7 1.0 copy.27
  236.7 0.0 copy-done.3
  236.7 1.0 copy.28
  237.6 0.0 copy-done.2
  237.6 1.0 copy.29
  (4 shorter events, 0.0 us)
Async XLA Ops:
  0.6 4.2 %copy-start.5 = (s32[1,512]{1,0:T(1,128)S(1)}, s32[1,512]{1,0:T(1,128)}, u32[]{:S(2)}) copy-start(s32[1,512]{1,0:T(1,128)} %param.13) | copy-start | bytes 6148
  87.1 34.0 %copy-start = (f32[224580]{0:T(1024)S(1)}, f32[224580]{0:T(1024)}, u32[]{:S(2)}) copy-start(f32[224580]{0:T(1024)} %param.17) | copy-start | bytes 2694964
  87.1 34.0 %copy-start.1 = (f32[224580]{0:T(1024)S(1)}, f32[224580]{0:T(1024)}, u32[]{:S(2)}) copy-start(f32[224580]{0:T(1024)} %param.16) | copy-start | bytes 2694964
  232.9 2.8 %copy-start.4 = (f32[1760,128]{1,0:T(8,128)S(1)}, f32[1760,128]{1,0:T(8,128)}, u32[]{:S(2)}) copy-start(f32[1760,128]{1,0:T(8,128)} %get-tuple-element.36) | copy-start | bytes 2703364
  232.9 3.8 %copy-start.3 = (f32[1760,128]{1,0:T(8,128)S(1)}, f32[1760,128]{1,0:T(8,128)}, u32[]{:S(2)}) copy-start(f32[1760,128]{1,0:T(8,128)} %get-tuple-element.37) | copy-start | bytes 2703364
  235.7 2.0 copy-start.2

commit v5 on v4

--- a/solution.py
+++ b/solution.py
@@ -714,10 +714,27 @@
     )(tiles, dq, dk, dv, gfi, low, feats, table, grads)
 
 
+GATHER_PARTS = ((0, 8), (8, 7), (15, 7), (22, 7), (29, 4), (33, 4))
+GATHER_STEPS = (
+    ((647, 384, 128, 256, 385, 129, 257, 386, 130, 258, 387, 131, 259, 388, 132, 260, 389, 133, 261),
+     (17, 145, 8, 264, 19, 147, 12, 396, 20, 404, 10, 266, 9, 11, 13, 655, 397, 16, 18, 21, 663, 32, 33, 34, 35, 36, 37, 679, 405, 149, 268, 160, 288, 161, 289, 29, 413, 24, 25, 26, 27, 28, 671, 412, 162, 290),
+     {-1: (163, 291), 0: (49, 177, 40, 296, 64, 65, 66, 67, 68, 69, 711), 1: (42, 298, 51, 179, 192), 2: (320,), 3: (41, 43, 44, 45, 687, 193, 321, 48, 50, 52, 53, 695), 4: (194, 322), 5: (195, 323, 56, 57, 58, 59, 60, 61, 703), 6: (96, 224, 352), 7: (97, 225, 353), 8: (81, 209, 72, 328, 98, 99, 100, 101, 743), 9: (226, 74, 330), 10: (227, 354, -1), 11: (73, 75, 76, 77, 719, 83, 211, 355, 113, 241, 104, 360, 105, 106, 107, 108, 109, 751, 80, 82, 84, 85, 727, 362, 112, 114, 115, 116, 117, 759, 243, 120, 121, 122, 123, 124, 125, 767, 88, 89, 90, 91, 92, 93, 735)}),
+    ((679, 544, 416, 160, 288, 545, 417, 161, 289, 546),
+     (0, 384, 128, 256, 547, 1, 385, 129, 257, 548, 549, 2, 386, 130, 258, 64, 576, 8, 264, 3, 387, 131, 17, 145, 4, 388, 65, 577, 259, 5, 647, 66, 67, 68, 69, 711, 389, 162, 578, 10, 266, 12, 396, 20, 404, 579, 290, 9, 11, 13, 655, 397, 19, 147, 163, 16, 18, 21, 663, 405, 580, 291, 418, 581, 164, 292, 96, 608, 29, 413, 165, 293, 24, 25, 26, 27, 28, 671, 412, 49, 177, 40, 296, 419),
+     {-1: (97, 98, 99, 100, 101, 743, 51, 179, 44, 556, 52, 564, 42, 298, 420, 41, 43, 45, 687, 557, 48, 50, 53, 695, 565, 421, 181), 0: (300, 609, 428, 192, 320, 436), 1: (429, 193, 321, 61, 573), 2: (437, 56, 57, 58, 59, 60, 703, 572, 610, 194, 445, 322), 3: (444, 611, 195, 323), 4: (612, 224, 352), 5: (613, 108, 620, 225, 353), 6: (76, 588, 72, 73, 74, 75, 77, 719, 226, 116, 628, 354), 7: (589, 227, 109, 621, 355), 8: (84, 596, 81, 209, 80, 82, 83, 85, 727, 328, 117, 629), 9: (597, 211, 330), 10: (104, 105, 106, 107, 751, 112, 113, 114, 115, 759, 241, 360, -1), 11: (243, 362, 125, 637, 124, 636, 93, 605, 88, 89, 90, 91, 92, 735, 604, 120, 121, 122, 123, 767)}),
+    ((711, 576, 448, 192, 320, 577, 449, 193, 321, 578),
+     (32, 416, 160, 288, 579, 33, 417, 161, 289, 580, 581, 0, 384, 128, 256, 96, 608, 1, 385, 129, 257, 97, 609, 98, 99, 100, 101, 743, 2, 386, 130, 258, 610, 8, 264, 3, 387, 131, 611, 17, 145, 4, 388, 259, 5, 647, 389, 612, 49, 177, 10, 266, 12, 396, 613, 20, 404, 40, 296, 9, 11, 13, 655, 397, 19, 147, 16, 18, 21, 663, 405, 34, 162, 290, 418, 194, 322, 29, 413, 195, 24, 25, 26, 27, 28, 671, 412, 42, 298),
+     {-1: (35, 419, 163, 291, 36, 420, 196, 37, 679, 421, 323), 0: (197, 44, 428, 324, 52, 436), 1: (108, 620, 325, 41, 43, 45, 687, 429, 51, 179, 224, 76, 588, 72, 328), 2: (48, 50, 53, 695, 437, 116, 628, 73, 74, 75, 77, 719, 589, 61, 445, 81, 209, 109, 621), 3: (84, 596, 352, 60, 444, 56, 57, 58, 59, 703, 117, 629, 80, 82, 83, 85, 727, 450, 225), 4: (597, 353, 451, 226), 5: (354, 452, 227), 6: (453, 355, 460, 211), 7: (330, 461, 213, 468), 8: (332, 113, 241, 104, 105, 106, 107, 751, 469, 360, 112, 114, 115, 759), 9: (125, 637, 243, 124, 636, 362, 93, 477, 605), 10: (88, 89, 90, 91, 92, 735, 476, 604, -1), 11: (120, 121, 122, 123, 767)}),
+    ((743, 608, 224, 352, 609, 225, 353, 610, 226, 354, 611, 227, 355, 612, 613),
+     (32, 160, 288, 33, 161, 289, 0, 128, 256, 1, 129, 257, 2, 130, 8, 264, 258, 17, 145, 3, 131, 259, 4, 5, 647, 49, 177, 10, 266, 40, 296, 9, 11, 12, 13, 655, 19, 147, 228, 16, 18, 20, 21, 663, 34, 290, 162, 356, 229, 357, 64, 192, 24, 25, 26, 27, 28, 29, 671, 108, 620),
+     {-1: (42, 298, 35, 163, 291, 116, 628, 104, 105, 106, 107, 109, 751, 621, 117, 629, 112, 113, 114, 115, 759, 65, 193, 36, 37, 679, 320), 0: (360,), 1: (41, 43, 44, 45, 687, 51, 179, 241), 2: (48, 50, 52, 53, 695, 321, 243), 3: (362, 56, 57, 58, 59, 60, 61, 703, 245), 4: (364, 66, 194, 72, 328), 5: (81, 209, 322, 125, 637), 6: (67, 195, 120, 121, 122, 123, 124, 767, 636, 68, 69, 711, 323), 7: (74, 330), 8: (73, 75, 76, 77, 719), 9: (83, 211, 80, 82, 84, 85, 727), 10: (-1,), 11: (88, 89, 90, 91, 92, 93, 735)}),
+)
+
+
 def forward_kernel(x_ref, tokens, feats, pad, buckets, lengths,
                    g_ref, hidden, low, query, keys, values, ctx, soft, code_out,
                    xv, tail, head, win, chunk, lsem, hsend, hrecv, own,
-                   zs, zr, xas, xar, xbs, xbr, yas, yar, ybs, ybr, cs, cr,
+                   ssem, rsem, cr,
                    pads, hidden_v, low_v, query_v, keys_v, values_v, ctx_v, code, buckets_v, tokens_v, feats_v, p_v, s_scr, tab,
                    wl, wq, wk, wv, vrows, vf, ksend, krecv, wsem, isem, osem, psem):
     f32, bf = jnp.float32, jnp.bfloat16
@@ -808,139 +825,40 @@
         to_prev.wait_send()
 
     xdev, ydev, cdev = (z * 4 + y * 2 + 1 - x, c), (z * 4 + (1 - y) * 2 + x, c), (k, 1 - c)
-    zdev = {1: (jnp.minimum(k + 4, 15), c), -1: (jnp.maximum(k - 4, 0), c)}
-
-    def gsl(chip, p):
-        off, n = PARTS[p]
-        return g_ref.at[chip, pl.ds(37 * c + off, n)]
-
-    def src(chip, p, mine=False):
-        off, n = PARTS[p]
-        return chunk.at[pl.ds(off, n)] if mine else gsl(chip, p)
-
-    def chip_of(zo, yo, xo):
-        return zo * 4 + yo * 2 + xo
-
-    def zcopy(zo, p, way, mine=False):
-        chip = chip_of(zo, y, x)
-        w = (way + 1) // 2
-        return rcopy(src(chip, p, mine), gsl(chip, p), zs.at[w, zo, p], zr.at[zo, p], zdev[way])
-
-    def xcopy(zo, yo, xo, p, mine=False):
-        chip = chip_of(zo, yo, xo)
-        s, r = (xas, xar) if p == 0 else (xbs, xbr)
-        i = zo if p == 0 else zo * 2 + yo
-        return rcopy(src(chip, p, mine), gsl(chip, p), s.at[i], r.at[i], xdev)
-
-    def ycopy(zo, yo, xo, p, mine=False):
-        chip = chip_of(zo, yo, xo)
-        s, r = (ybs, ybr) if p == 1 else (yas, yar)
-        i = zo if p == 1 else zo * 2 + xo
-        return rcopy(src(chip, p, mine), gsl(chip, p), s.at[i], r.at[i], ydev)
-
-    def ccopy(chip, p, mine=False):
-        return rcopy(src(chip, p, mine), gsl(chip, p), cs.at[chip, p], cr.at[chip, p], cdev)
+    targets = {1: xdev, 2: ydev, 3: (jnp.minimum(k + 4, 15), c), 4: (jnp.maximum(k - 4, 0), c), 5: cdev}
+    tiles = g_ref.reshape(16 * CHIP, 8, D)
+
+    def step(zz, op):
+        if op < 0:
+            make_values()
+            return
+        link, item, p = op // 128, op // 8 % 16, op % 8
+        chip = item // 4 * 4 + (1 - y if item // 2 % 2 else y) * 2 + (1 - x if item % 2 else x)
+        off, n = (0, 37) if link == 5 else GATHER_PARTS[p]
+        there = g_ref.at[chip, pl.ds(37 * c + off, n)]
+        if link == 0:
+            rcopy(there, there, ssem.at[0], rsem.at[chip, p], xdev).wait_recv()
+            return
+        here = chunk.at[pl.ds(off, n)] if item == zz * 4 else there
+        rcopy(here, there, ssem.at[link - 1], cr.at[chip] if link == 5 else rsem.at[chip, p], targets[link]).start()
+
+    def steps_of(zz, which, head=0):
+        for op in GATHER_STEPS[zz][which] if which < 2 else GATHER_STEPS[zz][2].get(head, ()):
+            step(zz, op)
+
+    def sent_rows(zz, link):
+        ops = [op for w in (0, 1) for op in GATHER_STEPS[zz][w]] + [op for v in GATHER_STEPS[zz][2].values() for op in v]
+        return sum(37 if link == 5 else GATHER_PARTS[op % 8][1] for op in ops if op // 128 == link)
 
     pair_pads = rcopy(pads.at[pl.ds(c, 1)], pads.at[pl.ds(c, 1)], ksend.at[2], krecv.at[2], cdev)
     pair_pads.start()
-    mine = [pltpu.make_async_copy(chunk.at[pl.ds(*PARTS[p])], gsl(k, p), own.at[p]) for p in (0, 1)]
-
-    def own_z(way):
-        for p in (0, 1):
-            zcopy(z, p, way, True).start()
-
-    def pass_on(zz, zo):
-        way = 1 if zo < zz else -1
-        for p in (0, 1):
-            zcopy(zo, p, way).wait_recv()
-            if 0 <= zz + way <= 3:
-                zcopy(zo, p, way).start()
-
-    def spread(zz, zo):
-        xcopy(zo, y, x, 0).start()
-        ycopy(zo, y, x, 1).start()
-        ycopy(zo, y, x, 0).start()
-        xcopy(zo, y, x, 1).start()
-        for p in (0, 1):
-            ccopy(chip_of(zo, y, x), p).start()
-
-    def column(zz, zo):
-        way = 1 if zo < zz else -1
-        for p in (0, 1):
-            zcopy(zo, p, way).wait_recv()
-            if 0 <= zz + way <= 3:
-                zcopy(zo, p, way).start()
-            if p == 0:
-                xcopy(zo, y, x, 0).start()
-                ycopy(zo, y, x, 0).start()
-            else:
-                ycopy(zo, y, x, 1).start()
-                xcopy(zo, y, x, 1).start()
-            ccopy(chip_of(zo, y, x), p).start()
-
-    def beside(zz, zo):
-        xcopy(zo, y, 1 - x, 0).wait_recv()
-        ycopy(zo, y, 1 - x, 0).start()
-        ccopy(chip_of(zo, y, 1 - x), 0).start()
-        ycopy(zo, 1 - y, x, 1).wait_recv()
-        xcopy(zo, 1 - y, x, 1).start()
-        ccopy(chip_of(zo, 1 - y, x), 1).start()
-
-    def last(zz, zo):
-        ycopy(zo, 1 - y, x, 0).wait_recv()
-        ccopy(chip_of(zo, 1 - y, x), 0).start()
-        xcopy(zo, y, 1 - x, 1).wait_recv()
-        ccopy(chip_of(zo, y, 1 - x), 1).start()
-        ycopy(zo, 1 - y, 1 - x, 0).wait_recv()
-        ccopy(chip_of(zo, 1 - y, 1 - x), 0).start()
-        xcopy(zo, 1 - y, 1 - x, 1).wait_recv()
-        ccopy(chip_of(zo, 1 - y, 1 - x), 1).start()
-
-    def own_first(zz, zo):
-        xcopy(z, y, x, 0, True).start()
-        ycopy(z, y, x, 1, True).start()
-
-    def own_second(zz, zo):
-        ycopy(z, y, x, 0, True).start()
-        xcopy(z, y, x, 1, True).start()
-        for p in (0, 1):
-            ccopy(k, p, True).start()
-
-    def values_now(zz, zo):
-        make_values()
-
-    def own_up(zz, zo):
-        own_z(1)
-
-    def own_down(zz, zo):
-        own_z(-1)
-
-    begin = {
-        0: ((own_up, 0), (own_first, 0), (own_second, 0)),
-        1: ((own_first, 1), (own_down, 1)),
-        2: ((own_up, 2), (own_down, 2), (own_first, 2)),
-        3: ((own_down, 3), (own_first, 3)),
-    }
-    before = {
-        0: ((beside, 0), (column, 1), (last, 0)),
-        1: ((column, 0), (own_up, 1), (beside, 0), (column, 3), (column, 2), (last, 0)),
-        2: ((column, 3), (pass_on, 0), (spread, 0), (beside, 0), (column, 1), (own_second, 2), (last, 0)),
-        3: ((column, 2), (column, 0), (beside, 0), (beside, 2), (last, 0), (column, 1), (beside, 3)),
-    }
-    after = {
-        0: {-1: ((column, 3), (beside, 1)), 1: ((beside, 3),), 2: ((last, 1), (column, 2)), 8: ((values_now, 0), (beside, 2)), 10: ((last, 3),), 11: ((last, 2),)},
-        1: {4: ((own_second, 1),), 6: ((beside, 1), (beside, 3)), 7: ((beside, 2),), 8: ((last, 1), (values_now, 0)), 10: ((last, 3),), 11: ((last, 2),)},
-        2: {2: ((beside, 1),), 4: ((beside, 2),), 6: ((last, 1), (beside, 3)), 10: ((last, 2),), 11: ((values_now, 0), (last, 3))},
-        3: {5: ((last, 2), (beside, 1)), 8: ((own_second, 3),), 9: ((last, 1),), 11: ((last, 3), (values_now, 0))},
-    }
-
-    for p in (0, 1):
-        mine[p].start()
+    mine = pltpu.make_async_copy(chunk, g_ref.at[k, pl.ds(37 * c, 37)], own.at[0])
+
     for zz in range(4):
         @pl.when(z == zz)
         def _():
-            for f, zo in begin[zz]:
-                f(zz, zo)
+            steps_of(zz, 0)
+    mine.start()
     for copy in inputs:
         copy.wait()
     pair_pads.wait()
@@ -950,21 +868,16 @@
     for zz in range(4):
         @pl.when(z == zz)
         def _():
-            for f, zo in before[zz]:
-                f(zz, zo)
-    for p in (0, 1):
-        mine[p].wait()
+            steps_of(zz, 1)
+    mine.wait()
 
     def from_partner(chip):
-        for p in (0, 1):
-            off, n = PARTS[p]
-            theirs = g_ref.at[chip, pl.ds(37 * (1 - c) + off, n)]
-            rcopy(theirs, theirs, cs.at[chip, p], cr.at[chip, p], cdev).wait_recv()
+        theirs = g_ref.at[chip, pl.ds(37 * (1 - c), 37)]
+        rcopy(theirs, theirs, ssem.at[4], cr.at[chip], cdev).wait_recv()
 
     for chip in range(3):
         from_partner(chip)
 
-    tiles = g_ref.reshape(16 * CHIP, 8, D)
     loads = [pltpu.make_async_copy(tiles.at[vector_at(ch)], vrows.at[i], wsem.at[i]) for i, ch in enumerate((0, 1))]
     loads += pieces(tiles, wl, 0, 16, wsem, 4) + pieces(tiles, wk, 112, 96, wsem, 8) + pieces(tiles, wq, 16, 96, wsem, 16)
     for copy in loads:
@@ -1006,11 +919,10 @@
         return pltpu.make_async_copy(p_v.at[pl.ds(2 * pair, 2)], soft.at[pl.ds(2 * pair, 2)], psem.at[pair])
 
     for zz in range(4):
-        if -1 in after[zz]:
+        if -1 in GATHER_STEPS[zz][2]:
             @pl.when(z == zz)
             def _():
-                for f, zo in after[zz][-1]:
-                    f(zz, zo)
+                steps_of(zz, 2, -1)
 
     def one_head(head, _):
         lanes = pl.ds(pl.multiple_of(head // 2 * 128, 128), 128)
@@ -1022,11 +934,10 @@
 
         for zz in range(4):
             for i in range(H):
-                if i in after[zz]:
+                if i in GATHER_STEPS[zz][2]:
                     @pl.when((head == i) & (z == zz))
                     def _():
-                        for f, zo in after[zz][i]:
-                            f(zz, zo)
+                        steps_of(zz, 2, i)
         return 0
 
     lax.fori_loop(0, H, one_head, 0)
@@ -1043,21 +954,14 @@
     outs.append(pltpu.make_async_copy(ctx_v, ctx, osem.at[6]))
     outs[-1].start()
 
-    for p in (0, 1):
-        for way in (1, -1):
-            for zo in range(4):
-                @pl.when(((z - zo) * way >= 0) & (z + way >= 0) & (z + way <= 3))
-                def _():
-                    zcopy(zo, p, way).wait_send()
-    for zo in range(4):
-        xcopy(zo, y, x, 0).wait_send()
-        ycopy(zo, y, x, 1).wait_send()
-        for o in range(2):
-            ycopy(zo, y, o, 0).wait_send()
-            xcopy(zo, o, x, 1).wait_send()
-    for chip in range(16):
-        for p in (0, 1):
-            ccopy(chip, p).wait_send()
+    for zz in range(4):
+        @pl.when(z == zz)
+        def _():
+            for link in range(1, 6):
+                n = sent_rows(zz, link)
+                if n:
+                    whole = tiles.at[pl.ds(0, n)]
+                    rcopy(whole, whole, ssem.at[link - 1], cr.at[0], targets[link]).wait_send()
     for chip in range(5, 16):
         from_partner(chip)
     for pair in range(H // 2):
@@ -1085,10 +989,7 @@
         scratch_shapes=[
             V((ROWS, 128), f32), V((TAIL, 128), f32), V((HEAD, 128), f32), V((WIN, 128), f32), V((SLOTS, 8, D), bf),
             sem, sem((2,)), sem((2,)), sem((2,)),
-            sem((2, 4, 2)), sem((4, 2)),
-            sem((4,)), sem((4,)), sem((8,)), sem((8,)),
-            sem((8,)), sem((8,)), sem((4,)), sem((4,)),
-            sem((16, 2)), sem((16, 2)),
+            sem((5,)), sem((16, 6)), sem((16,)),
             V((2, 8, rows), jnp.int32), V((rows, D), f32), V((rows, D), bf), V((rows, D), bf), V((key_rows, D), bf), V((key_rows, D), bf),
             V((rows, D), bf), V((key_rows, rows), jnp.int32), V((rows, key_rows), jnp.int32), V((rows, D), bf), V((rows, LF), bf),
             V((H, key_rows, rows), bf), V((key_rows, rows), f32), V((16, 128), f32),
@@ -1310,7 +1211,8 @@
     nxt = (jnp.where(c == 0, k, jnp.minimum(k + 1, 15)), 1 - c)
     bar = pltpu.get_barrier_semaphore()
     far_next, far_prev = (c == 1) & (k < 15), (c == 0) & (k > 0)
-    for dev in [xdev, ydev, cdev] + column_devs:
+    plane_devs = [(z * 4 + (1 - y if oy else y) * 2 + (1 - x if ox else x), 1 - c if oc else c) for oc in (0, 1) for oy in (0, 1) for ox in (0, 1)][1:]
+    for dev in plane_devs + column_devs:
         pl.semaphore_signal(bar, inc=1, device_id=dev, device_id_type=MESH)
 
     @pl.when(far_next)
@@ -1333,7 +1235,7 @@
 
     for copy in fetch(0) + [fetch_soft(0, 0), fetch_soft(0, 1)]:
         copy.start()
-    pl.semaphore_wait(bar, 6 + jnp.where(far_next | far_prev, 1, 0))
+    pl.semaphore_wait(bar, 10 + jnp.where(far_next | far_prev, 1, 0))
     corners = ((1, 1), (1, 0), (0, 1), (0, 0))
     for oy, ox in corners:
         rs.begin(2, oy, ox)
@@ -1604,10 +1506,31 @@
 
     squares = lax.fori_loop(0, 37, square, jnp.zeros((8, 128), f32))
     lines = [jnp.sum(squares, axis=0, keepdims=True)] + [table[0:1, 128 * i : 128 * i + 128] for i in range(3)]
+    place_in = c * 4 + y * 2 + x
     sq[0] = jnp.concatenate(lines + [jnp.zeros((4, 128), f32)])
-    rounds = [rcopy(sq.at[i], sqr.at[i], qs.at[i], qr.at[i], dev) for i, dev in enumerate((cdev, xdev, ydev))]
-    hops = [rcopy(sq.at[3], sqr.at[3 + i], qs.at[3 + i], qr.at[3 + i], column_devs[i]) for i in range(3)]
-    rounds[0].start()
+    sqr[place_in] = sq[0]
+    rounds = [rcopy(sq.at[0], sqr.at[place_in], qs.at[i], qr.at[place_in], dev) for i, dev in enumerate(plane_devs)]
+    hops = [rcopy(sq.at[1], sqr.at[8 + z], qs.at[7 + i], qr.at[8 + z], dev) for i, dev in enumerate(column_devs)]
+    for h in rounds:
+        h.start()
+
+    def arrived(slot):
+        return rcopy(sqr.at[slot], sqr.at[slot], qs.at[0], qr.at[slot], cdev)
+
+    rs.finish()
+    late.finish()
+    for zs in (0, 1, 2):
+        zc.sent(zs, 3, 1)
+    for zs in (0, 1):
+        zc.sent(zs, 2, 1)
+    zc.sent(3, 2, -1)
+    zc.sent(0, 1, 1)
+    zc.sent(3, 1, -1)
+    zc.sent(2, 1, -1)
+    for zs in (1, 2, 3):
+        zc.sent(zs, 0, -1)
+    for pair in range(H // 2):
+        swap(pair).wait_send()
     q, sh = shard_start(d)
     base = q - FRONT
 
@@ -1637,9 +1560,17 @@
         at, wide = tile_start(w0 + t)
         flatten(total, t, at - base, wide)
 
-    rounds[0].wait_recv()
-    sq[1] = sq[0] + sqr[0]
-    rounds[1].start()
+    for i in range(8):
+        @pl.when(place_in != i)
+        def _():
+            arrived(i).wait_recv()
+    layer = sqr[0]
+    for i in range(1, 8):
+        layer = layer + sqr[i]
+    sq[1] = layer
+    sqr[8 + z] = layer
+    for h in hops:
+        h.start()
     @pl.when(d > 0)
     def _():
         to_next.wait_recv()
@@ -1658,16 +1589,11 @@
             at, wide = tile_start(w0 + mine + t)
             flatten(ebuf.at[1], t, at - base, wide)
 
-    rounds[1].wait_recv()
-    sq[2] = sq[1] + sqr[1]
-    rounds[2].start()
-    rounds[2].wait_recv()
-    sq[3] = sq[2] + sqr[2]
-    for h in hops:
-        h.start()
-    for h in hops:
-        h.wait_recv()
-    summed = (sq[3] + sqr[4]) + (sqr[3] + sqr[5])
+    for i in range(4):
+        @pl.when(z != i)
+        def _():
+            arrived(8 + i).wait_recv()
+    summed = (sqr[8] + sqr[9]) + (sqr[10] + sqr[11])
 
     @pl.when(d == 0)
     def _():
@@ -1716,20 +1642,6 @@
     def _():
         to_prev.wait_send()
 
-    rs.finish()
-    late.finish()
-    for zs in (0, 1, 2):
-        zc.sent(zs, 3, 1)
-    for zs in (0, 1):
-        zc.sent(zs, 2, 1)
-    zc.sent(3, 2, -1)
-    zc.sent(0, 1, 1)
-    zc.sent(3, 1, -1)
-    zc.sent(2, 1, -1)
-    for zs in (1, 2, 3):
-        zc.sent(zs, 0, -1)
-    for pair in range(H // 2):
-        swap(pair).wait_send()
     shown.wait()
     for copy in results:
         copy.wait()
@@ -1759,8 +1671,8 @@
             V((3, rows, D), bf), V((2, 8, D), f32),
             w, w, w, V((rows, D), bf), V((rows, D), f32), V((rows, LF), bf), V((16, 8, D), bf), w, w, w, V((4, 8, D), bf),
             sem((12,)), sem((24,)), sem((7,)),
-            V((37,) + tile, f32), V((2, EDGE) + tile, f32), V((4, 8, 128), f32), V((6, 8, 128), f32),
-            V((WIN2, 128), f32), line, line, line, sem((3,)), sem((2,)), sem((2,)), sem((6,)), sem((6,)),
+            V((37,) + tile, f32), V((2, EDGE) + tile, f32), V((2, 8, 128), f32), V((12, 8, 128), f32),
+            V((WIN2, 128), f32), line, line, line, sem((3,)), sem((2,)), sem((2,)), sem((10,)), sem((12,)),
         ] + reducer_scratch() + chain_scratch(),
         input_output_aliases={10: 1},
         compiler_params=pltpu.CompilerParams(collective_id=5, has_side_effects=True, vmem_limit_bytes=63 << 20),

time: 240 us -> 231 us (0.963)
  Pallas kernels: 226 us -> 218 us
    pallas_call x1, Pallas kernels: 110 us -> 98.9 us  [backward_and_step(): pl.pallas_call(backward_kernel, out_shape=[S((rows, D), f32), S(grads.sha...]
    pallas_call x1, Pallas kernels: 81.6 us -> 84.8 us  [gather_and_attend(): pl.pallas_call(forward_kernel, out_shape=[S((16, CHIP, 8, D), bf), S((row...]
where the time goes in v5:
time: 231 us; the launch traced here: 230 us
  Pallas kernels  218 us (94%)
  local copies, waits for them, and re-layouts  10.6 us (5%)
    pallas_call x1, Pallas kernels, backward_and_step(): pl.pallas_call(backward_kernel, out_shape=[S((rows, D), f32), S(grads.sha...  98.9 us
    pallas_call x1, Pallas kernels, gather_and_attend(): pl.pallas_call(forward_kernel, out_shape=[S((16, CHIP, 8, D), bf), S((row...  84.8 us
    pallas_call x1, Pallas kernels, middle(): pl.pallas_call(middle_kernel, out_shape=[S((rows, D), bf), S((rows, D), f...  33.9 us
    unnamed x17, local copies, waits for them, and re-layouts  5.74 us

profile of v5, /device:TPU:0, one launch (start us, length us, event | category | flops | bytes accessed | tf_op | source)
XLA Modules:
  0.0 230.3 jit_solution(5878539931927530228)
XLA Ops:
  0.6 0.0 copy-start.5
  0.6 2.2 pad_bitcast_fusion.2.x_ref.m_ref
  2.8 0.7 convert_element_type.20
  3.5 0.5 fusion
  4.1 0.8 copy.16.feats.feats_in
  4.8 0.0 copy-done.5
  4.8 0.6 broadcast_in_dim.16.pad
  5.5 84.8 %gather_and_attend.1 = (bf16[16,74,8,768]{3,2,1,0:T(8,128)(2,1)}, f32[512,768]{1,0:T(8,128)}, bf16[512,768]{1,0:T(8,128)(2,1)}, bf16[512,768]{1,0:T(8,128)(2,1)}...) custom-call(f32[1760,128]{1,0:T(8,128)} %pad_bitcast_fusion.2.x_ref., ...), custom_call_target="tpu_custom_call" | custom-call | tf_op jit(solution)/shard_map/gather_and_attend/pallas_call | solution.py:981
  90.3 0.0 copy-start
  90.3 0.0 copy-start.1
  90.3 33.9 %middle.1 = (bf16[512,768]{1,0:T(8,128)(2,1)}, f32[512,768]{1,0:T(8,128)}, bf16[512,768]{1,0:T(8,128)(2,1)}, bf16[1184,8,768]{2,1,0:T(8,128)(2,1)}) custom-call(bf16[1184,8,768]{2,1,0:T(8,128)(2,1)} %bitcast.25, bf16[512,768]{1,0:T(8,128)(2,1)} %get-tuple-element.23.ctx, f32[512,768]{1,0:T(8,128)} %get-tuple-element.24.hidden, bf16[512,768]{1,0:T(8,128)(2,1)} %bitcast.32), custom_call_target="tpu_custom_call" | custom-call | tf_op jit(solution)/shard_map/middle/pallas_call | solution.py:348
  124.2 0.0 copy-done
  124.2 0.0 copy-done.1
  124.3 1.3 pad_bitcast_fusion
  125.6 98.9 %backward_and_step.1 = (f32[512,768]{1,0:T(8,128)}, bf16[1184,8,768]{2,1,0:T(8,128)(2,1)}, f32[1760,128]{1,0:T(8,128)}, f32[1760,128]{1,0:T(8,128)}, f32[1760,12...) custom-call(bf16[1184,8,768]{2,1,0:T(8,128)(2,1)} %bitcast.26, ...), custom_call_target="tpu_custom_call", output_to_operand_aliasing={{1}: (10, {})} | custom-call | tf_op jit(solution)/shard_map/backward_and_step/pallas_call | solution.py:1661
  224.5 0.0 copy-start.4
  224.5 0.0 copy-start.3
  224.5 2.8 %copy.26 = f32[1,512,768]{2,1,0:T(8,128)} copy(f32[1,512,768]{2,1,0:T(8,128)} %bitcast.28) | data formatting | bytes 3145728
  227.3 0.0 copy-done.4
  227.3 1.0 copy.27
  228.3 0.0 copy-done.3
  228.3 1.0 copy.28
  229.3 0.0 copy-done.2
  229.3 1.0 copy.29
  (4 shorter events, 0.0 us)
Async XLA Ops:
  0.6 4.2 %copy-start.5 = (s32[1,512]{1,0:T(1,128)S(1)}, s32[1,512]{1,0:T(1,128)}, u32[]{:S(2)}) copy-start(s32[1,512]{1,0:T(1,128)} %param.13) | copy-start | bytes 6148
  90.3 34.0 %copy-start = (f32[224580]{0:T(1024)S(1)}, f32[224580]{0:T(1024)}, u32[]{:S(2)}) copy-start(f32[224580]{0:T(1024)} %param.17) | copy-start | bytes 2694964
  90.3 34.0 %copy-start.1 = (f32[224580]{0:T(1024)S(1)}, f32[224580]{0:T(1024)}, u32[]{:S(2)}) copy-start(f32[224580]{0:T(1024)} %param.16) | copy-start | bytes 2694964
  224.5 2.8 %copy-start.4 = (f32[1760,128]{1,0:T(8,128)S(1)}, f32[1760,128]{1,0:T(8,128)}, u32[]{:S(2)}) copy-start(f32[1760,128]{1,0:T(8,128)} %get-tuple-element.36) | copy-start | bytes 2703364
  224.5 3.8 %copy-start.3 = (f32[1760,128]{1,0:T(8,128)S(1)}, f32[1760,128]{1,0:T(8,128)}, u32[]{:S(2)}) copy-start(f32[1760,128]{1,0:T(8,128)} %get-tuple-element.37) | copy-start | bytes 2703364
  227.3 2.0 copy-start.2

commit v6 on v5

--- a/solution.py
+++ b/solution.py
@@ -1,4 +1,5 @@
 import functools
+import math
 
 import jax
 import jax.numpy as jnp
@@ -229,7 +230,7 @@
                   wo, wup, wdn, vecs, vf, act, slope, low1, hat1, inv1, hat2, inv2, a, sums, dwo, dwup, dwdn, vgrads, lsem, ssem):
     f32, bf = jnp.float32, jnp.bfloat16
     rows = ctx.shape[0]
-    R = 64
+    R = 128
     steps = rows // R
     loads_o = pieces(tiles, wo, 304, 96, lsem, 0)
     loads_u = pieces(tiles, wup, 400, 384, lsem, 4)
@@ -731,8 +732,22 @@
 )
 
 
-def forward_kernel(x_ref, tokens, feats, pad, buckets, lengths,
-                   g_ref, hidden, low, query, keys, values, ctx, soft, code_out,
+def fill_features(out, boxes):
+    rows = out.shape[0]
+    f32 = jnp.float32
+    cols = jnp.concatenate([boxes[i].astype(f32) for i in range(4)] + [jnp.zeros((4, rows), f32)]).T
+    lane = lax.broadcasted_iota(jnp.int32, (rows, LF), 1)
+    rate = jnp.exp((lane % FREQ).astype(f32) * (-math.log(10000.0) / FREQ))
+    coordinate = lane // (2 * FREQ)
+    at = cols[:, 3:4]
+    for i in range(3):
+        at = jnp.where(coordinate == i, cols[:, i : i + 1], at)
+    angle = at * rate
+    out[...] = jnp.where(lane // FREQ % 2 == 0, jnp.sin(angle), jnp.cos(angle)).astype(jnp.bfloat16)
+
+
+def forward_kernel(x_ref, tokens, boxes, pad, buckets, lengths,
+                   g_ref, hidden, low, query, keys, values, ctx, soft, code_out, feats,
                    xv, tail, head, win, chunk, lsem, hsend, hrecv, own,
                    ssem, rsem, cr,
                    pads, hidden_v, low_v, query_v, keys_v, values_v, ctx_v, code, buckets_v, tokens_v, feats_v, p_v, s_scr, tab,
@@ -741,10 +756,10 @@
     rows = tokens.shape[0]
     k, c, z, y, x = place()
     d = 2 * k + c
-    inputs = [pltpu.make_async_copy(r, v, isem.at[i]) for i, (r, v) in enumerate(((buckets, buckets_v), (tokens, tokens_v), (feats, feats_v)))]
+    inputs = [pltpu.make_async_copy(r, v, isem.at[i]) for i, (r, v) in enumerate(((buckets, buckets_v), (tokens, tokens_v)))]
     for copy in inputs:
         copy.start()
-    pads[pl.ds(c, 1)] = pad[...].reshape(1, 8, rows)
+    pads[pl.ds(c, 1)] = jnp.broadcast_to(pad[...], (8, rows)).reshape(1, 8, rows)
     greet(k, c, z, y, x)
     load = pltpu.make_async_copy(x_ref, xv, lsem)
     load.start()
@@ -863,8 +878,10 @@
         copy.wait()
     pair_pads.wait()
     fill_codes(code, buckets_v, pads, lengths)
-    outs = [pltpu.make_async_copy(code, code_out, osem.at[0])]
-    outs[0].start()
+    fill_features(feats_v, boxes)
+    outs = [pltpu.make_async_copy(code, code_out, osem.at[0]), pltpu.make_async_copy(feats_v, feats, osem.at[7])]
+    for copy in outs:
+        copy.start()
     for zz in range(4):
         @pl.when(z == zz)
         def _():
@@ -900,7 +917,7 @@
     query_v[...] = ((jnp.dot(low_v[...], matrix(wq[...]), preferred_element_type=f32) + vf[1, 0:1, :]) * 0.125).astype(bf)
     share(keys_v, 0).wait()
     outs += [pltpu.make_async_copy(v, r, osem.at[1 + i]) for i, (v, r) in enumerate(((hidden_v, hidden), (low_v, low), (query_v, query), (keys_v, keys)))]
-    for copy in outs[1:]:
+    for copy in outs[2:]:
         copy.start()
 
     def make_values():
@@ -970,7 +987,7 @@
         copy.wait()
 
 
-def gather_and_attend(master, tokens, feats, pad, buckets, page_lengths):
+def gather_and_attend(master, tokens, boxes, pad, buckets, page_lengths):
     x = jnp.pad(master, (0, ROWS * 128 - SHARD)).reshape(ROWS, 128)
     sem = pltpu.SemaphoreType.DMA
     any_, vm = pl.BlockSpec(memory_space=pl.ANY), pl.BlockSpec(memory_space=pltpu.VMEM)
@@ -982,10 +999,10 @@
         forward_kernel,
         out_shape=[
             S((16, CHIP, 8, D), bf), S((rows, D), f32), S((rows, D), bf), S((rows, D), bf), S((key_rows, D), bf), S((key_rows, D), bf),
-            S((rows, D), bf), S((H, key_rows, rows), bf), S((key_rows, rows), jnp.int32),
+            S((rows, D), bf), S((H, key_rows, rows), bf), S((key_rows, rows), jnp.int32), S((rows, LF), bf),
         ],
-        in_specs=[any_, any_, any_, vm, any_, pl.BlockSpec(memory_space=pltpu.SMEM)],
-        out_specs=[any_] * 9,
+        in_specs=[any_, any_, vm, vm, any_, pl.BlockSpec(memory_space=pltpu.SMEM)],
+        out_specs=[any_] * 10,
         scratch_shapes=[
             V((ROWS, 128), f32), V((TAIL, 128), f32), V((HEAD, 128), f32), V((WIN, 128), f32), V((SLOTS, 8, D), bf),
             sem, sem((2,)), sem((2,)), sem((2,)),
@@ -994,11 +1011,11 @@
             V((rows, D), bf), V((key_rows, rows), jnp.int32), V((rows, key_rows), jnp.int32), V((rows, D), bf), V((rows, LF), bf),
             V((H, key_rows, rows), bf), V((key_rows, rows), f32), V((16, 128), f32),
             V((16, 8, D), bf), w, w, w, V((3, 8, D), bf), V((3, 8, D), f32),
-            sem((3,)), sem((3,)), sem((20,)), sem((3,)), sem((7,)), sem((H // 2,)),
+            sem((3,)), sem((3,)), sem((20,)), sem((3,)), sem((8,)), sem((H // 2,)),
         ],
         compiler_params=pltpu.CompilerParams(collective_id=0, has_side_effects=True, vmem_limit_bytes=60 << 20),
         name="gather_and_attend",
-    )(x, tokens, feats, pad, buckets, page_lengths)
+    )(x, tokens, boxes, pad, buckets, page_lengths)
 
 
 def guarded(cond, f):
@@ -1238,7 +1255,7 @@
     pl.semaphore_wait(bar, 10 + jnp.where(far_next | far_prev, 1, 0))
     corners = ((1, 1), (1, 0), (0, 1), (0, 0))
     for oy, ox in corners:
-        rs.begin(2, oy, ox)
+        rs.begin(3, oy, ox)
     code_copy = pltpu.make_async_copy(code_hbm, code_ref, csem.at[0])
     inputs = [pltpu.make_async_copy(r, v, isem.at[i]) for i, (r, v) in enumerate(((low_in, low), (gfi_in, gfi), (feats_in, feats)))]
     loads = pieces(tiles, wq, 16, 96, wsem, 8) + pieces(tiles, wv, 208, 96, wsem, 4) + pieces(tiles, wk, 112, 96, wsem, 0)
@@ -1264,15 +1281,12 @@
         return pltpu.make_async_copy(dsv.at[hh], spread.at[:, 2 * pair + hh], dssem.at[hh])
 
     plan = {
-        0: [(rs.first, 2, 0, 0), (rs.first, 2, 0, 1), (rs.first, 2, 1, 0), (rs.first, 3, 1, 1), (rs.begin, 1, 1, 1), (rs.begin, 1, 1, 0), (rs.begin, 1, 0, 1), (rs.begin, 1, 0, 0)],
-        1: [(rs.first, 3, 1, 0), (rs.first, 3, 0, 0), (rs.second, 2), (rs.first, 1, 1, 1), (rs.first, 3, 0, 1)],
-        5: [(rs.second, 3)],
+        0: [(rs.first, 3, 1, 0), (rs.begin, 2, 1, 1), (rs.begin, 2, 1, 0), (rs.begin, 2, 0, 1), (rs.begin, 2, 0, 0), (rs.first, 3, 0, 1)],
+        1: [(rs.begin, 1, 1, 1), (rs.begin, 1, 1, 0), (rs.begin, 1, 0, 1), (rs.begin, 1, 0, 0), (rs.first, 2, 1, 1), (rs.first, 2, 0, 1), (rs.second, 3)],
+        2: [(rs.first, 2, 1, 0)],
+        4: [(rs.first, 2, 0, 0), (rs.second, 2), (rs.first, 3, 0, 0), (rs.first, 1, 1, 1)],
     }
-    rs.begin(3, 1, 1)
-    rs.begin(3, 1, 0)
-    rs.begin(3, 0, 1)
-    rs.begin(3, 0, 0)
-    rs.first(2, 1, 1)
+    rs.first(3, 1, 1)
 
     def pair_of_heads(pair, _):
         slot = pair % 2
@@ -1412,48 +1426,48 @@
             counts[...] = lax.fori_loop(0, GROUPS, count, counts[...], unroll=8)
 
     early_one, late_one = rs.want(1, y, x), late.want(1, y, x)
-    count_some(0, 1)
+    rs.third(3)
+    zc.move(0, 3, 1, take=False)
     late.first(0, 1, 1)
     late.first(1, 1, 1)
+    zc.move(1, 3, 1)
     late.first(0, 1, 0)
     late.first(1, 1, 0)
-    rs.third(3)
-    zc.move(0, 3, 1, take=False)
+    count_some(0, 1)
     late.first(0, 0, 1)
     late.first(1, 0, 1)
     rs.third(2)
     count_some(1, 1)
-    zc.move(1, 3, 1)
     count_some(2, 1)
+    late.first(0, 0, 0)
+    late.first(1, 0, 0)
+    zc.move(0, 2, 1, take=False)
+    zc.move(2, 3, 1)
     zc.move(3, 2, -1, take=False)
     count_some(3, 1)
     late.second(0)
     late.second(1)
-    rs.first(1, 0, 0)
+    rs.first(1, 0, 1)
     count_some(4, 1)
     rs.first(1, 1, 0)
-    rs.first(1, 0, 1)
+    count_some(5, 1)
+    zc.move(1, 2, 1)
     rs.second(1)
-    late.first(0, 0, 0)
-    late.first(1, 0, 0)
-    count_some(5, 1)
-    zc.move(0, 2, 1, take=False)
     count_some(6, 1)
-    zc.move(1, 2, 1)
-    zc.move(2, 3, 1)
     late.third(0)
-    zc.move(1, 0, -1)
-    zc.move(2, 0, -1)
     zc.move(3, 0, -1, take=False)
     late.third(1)
     zc.move(0, 1, 1, take=False, also=late_one)
     zc.move(3, 1, -1, take=False, also=late_one)
+    zc.move(2, 0, -1)
     zc.move(2, 1, -1, also=late_one)
+    zc.move(1, 0, -1)
+    count_some(7, 1)
+    rs.first(1, 0, 0)
     rs.third(1)
+    zc.move(2, 1, -1, also=early_one)
+    zc.move(3, 1, -1, take=False, also=early_one)
     zc.move(0, 1, 1, take=False, also=early_one)
-    zc.move(3, 1, -1, take=False, also=early_one)
-    count_some(7, 1)
-    zc.move(2, 1, -1, also=early_one)
     table = table_row(counts[...], (8, D))
 
     total[...] = acc[k].astype(f32)
@@ -1730,16 +1744,15 @@
     custom, tokens, cotangent, page_boxes, page_lengths, padding, buckets, master, first_moment, second_moment
 ):
     rows = tokens.shape[1]
-    feats = layout_features(page_boxes.reshape(4, rows)).astype(jnp.bfloat16)
-    pad = jnp.broadcast_to(padding, (8, rows))
     if custom:
-        tiles, hidden, low, query, keys, values, ctx, soft, code = gather_and_attend(
-            master, tokens[0], feats, pad, buckets[0], page_lengths
+        tiles, hidden, low, query, keys, values, ctx, soft, code, feats = gather_and_attend(
+            master, tokens[0], page_boxes, padding, buckets[0], page_lengths
         )
         tiles = tiles.reshape(16 * CHIP, 8, D)
     else:
+        feats = layout_features(page_boxes.reshape(4, rows)).astype(jnp.bfloat16)
         tiles = to_tiles(unpack(lax.all_gather(master.astype(jnp.bfloat16), ("dp", "seq"), axis=0, tiled=True)))
-        hidden, low, query, keys, values, pads = enter(tiles, tokens[0], feats, pad)
+        hidden, low, query, keys, values, pads = enter(tiles, tokens[0], feats, jnp.broadcast_to(padding, (8, rows)))
         ctx, soft, code = attend(query, keys, values, buckets[0], page_lengths, pads, tiles[vector_at(0)])
     activations, grad_first_in, grad_context, grads = middle(tiles, ctx, hidden, cotangent[0])
     if custom:

time: 231 us -> 226 us (0.978)
    unnamed x17 -> x14, local copies, waits for them, and re-layouts: 5.74 us -> 5.73 us
where the time goes in v6:
time: 226 us
  Pallas kernels  216 us (96%)
  local copies, waits for them, and re-layouts  9.21 us (4%)
    pallas_call x1, Pallas kernels, backward_and_step(): pl.pallas_call(backward_kernel, out_shape=[S((rows, D), f32), S(grads.sha...  97.9 us
    pallas_call x1, Pallas kernels, gather_and_attend(): pl.pallas_call(forward_kernel, out_shape=[S((16, CHIP, 8, D), bf), S((row...  84.8 us
    pallas_call x1, Pallas kernels, middle(): pl.pallas_call(middle_kernel, out_shape=[S((rows, D), bf), S((rows, D), f...  33 us
    unnamed x14, local copies, waits for them, and re-layouts  5.73 us

profile of v6, /device:TPU:0, one launch (start us, length us, event | category | flops | bytes accessed | tf_op | source)
XLA Modules:
  0.0 225.7 jit_solution(8507093420623725986)
XLA Ops:
  0.6 2.1 pad_bitcast_fusion.2.x_ref.m_ref
  2.8 84.8 %gather_and_attend.1 = (bf16[16,74,8,768]{3,2,1,0:T(8,128)(2,1)}, f32[512,768]{1,0:T(8,128)}, bf16[512,768]{1,0:T(8,128)(2,1)}, bf16[512,768]{1,0:T(8,128)(2,1)}...) custom-call(f32[1760,128]{1,0:T(8,128)} %pad_bitcast_fusion.2.x_ref., ...), custom_call_target="tpu_custom_call" | custom-call | tf_op jit(solution)/shard_map/gather_and_attend/pallas_call | solution.py:998
  87.6 0.0 copy-start
  87.6 0.0 copy-start.1
  87.6 33.0 %middle.1 = (bf16[512,768]{1,0:T(8,128)(2,1)}, f32[512,768]{1,0:T(8,128)}, bf16[512,768]{1,0:T(8,128)(2,1)}, bf16[1184,8,768]{2,1,0:T(8,128)(2,1)}) custom-call(bf16[1184,8,768]{2,1,0:T(8,128)(2,1)} %bitcast.18, bf16[512,768]{1,0:T(8,128)(2,1)} %get-tuple-element.24.ctx, f32[512,768]{1,0:T(8,128)} %get-tuple-element.25.hidden, bf16[512,768]{1,0:T(8,128)(2,1)} %bitcast.25), custom_call_target="tpu_custom_call" | custom-call | tf_op jit(solution)/shard_map/middle/pallas_call | solution.py:349
  120.7 0.0 copy-done
  120.7 0.0 copy-done.1
  120.7 1.3 pad_bitcast_fusion
  122.0 97.9 %backward_and_step.1 = (f32[512,768]{1,0:T(8,128)}, bf16[1184,8,768]{2,1,0:T(8,128)(2,1)}, f32[1760,128]{1,0:T(8,128)}, f32[1760,128]{1,0:T(8,128)}, f32[1760,12...) custom-call(bf16[1184,8,768]{2,1,0:T(8,128)(2,1)} %bitcast.19, ...), custom_call_target="tpu_custom_call", output_to_operand_aliasing={{1}: (10, {})} | custom-call | tf_op jit(solution)/shard_map/backward_and_step/pallas_call | solution.py:1675
  219.9 0.0 copy-start.4
  219.9 0.0 copy-start.3
  219.9 2.8 %copy.20 = f32[1,512,768]{2,1,0:T(8,128)} copy(f32[1,512,768]{2,1,0:T(8,128)} %bitcast.21) | data formatting | bytes 3145728
  222.7 0.0 copy-done.4
  222.7 0.0 copy-start.2
  222.7 1.0 copy.21
  223.7 0.0 copy-done.3
  223.7 1.0 copy.22
  224.7 0.0 copy-done.2
  224.7 1.0 copy.23
Async XLA Ops:
  87.6 33.1 %copy-start = (f32[224580]{0:T(1024)S(1)}, f32[224580]{0:T(1024)}, u32[]{:S(2)}) copy-start(f32[224580]{0:T(1024)} %param.17) | copy-start | bytes 2694964
  87.6 33.1 %copy-start.1 = (f32[224580]{0:T(1024)S(1)}, f32[224580]{0:T(1024)}, u32[]{:S(2)}) copy-start(f32[224580]{0:T(1024)} %param.16) | copy-start | bytes 2694964
  219.9 2.8 %copy-start.4 = (f32[1760,128]{1,0:T(8,128)S(1)}, f32[1760,128]{1,0:T(8,128)}, u32[]{:S(2)}) copy-start(f32[1760,128]{1,0:T(8,128)} %get-tuple-element.38) | copy-start | bytes 2703364
  219.9 3.8 %copy-start.3 = (f32[1760,128]{1,0:T(8,128)S(1)}, f32[1760,128]{1,0:T(8,128)}, u32[]{:S(2)}) copy-start(f32[1760,128]{1,0:T(8,128)} %get-tuple-element.39) | copy-start | bytes 2703364
  222.7 2.0 copy-start.2

commit v7 on v6

--- a/solution.py
+++ b/solution.py
@@ -226,8 +226,8 @@
 ROOT_TAU = 0.3989422804014327
 
 
-def middle_kernel(tiles, ctx, hidden, cot, act_out, gfi_out, gctx_out, grads,
-                  wo, wup, wdn, vecs, vf, act, slope, low1, hat1, inv1, hat2, inv2, a, sums, dwo, dwup, dwdn, vgrads, lsem, ssem):
+def middle_kernel(tiles, ctx_in, hidden_in, cot_in, act_hbm, gfi_hbm, gctx_hbm, grads,
+                  ctx, hidden, cot, act_out, gfi_out, gctx_out, iosem, wo, wup, wdn, vecs, vf, act, slope, low1, hat1, inv1, hat2, inv2, a, sums, dwo, dwup, dwdn, vgrads, lsem, ssem):
     f32, bf = jnp.float32, jnp.bfloat16
     rows = ctx.shape[0]
     R = 128
@@ -236,7 +236,9 @@
     loads_u = pieces(tiles, wup, 400, 384, lsem, 4)
     loads_d = pieces(tiles, wdn, 784, 384, lsem, 12)
     loads_v = [pltpu.make_async_copy(tiles.at[vector_at(c)], vecs.at[i], lsem.at[20 + i]) for i, c in enumerate((5, 10, 15))]
-    for c in loads_v + loads_o + loads_u + loads_d:
+    ins = [pltpu.make_async_copy(r, v, iosem.at[i]) for i, (r, v) in enumerate(((ctx_in, ctx), (hidden_in, hidden), (cot_in, cot)))]
+    outs = [pltpu.make_async_copy(v, r, iosem.at[3 + i]) for i, (v, r) in enumerate(((act_out, act_hbm), (gfi_out, gfi_hbm), (gctx_out, gctx_hbm)))]
+    for c in ins[:1] + loads_v + loads_o + ins[1:2] + loads_u + loads_d + ins[2:]:
         c.start()
     up4 = wup.reshape(96, 4, 8, D)
     dup4 = dwup.reshape(96, 4, 8, D)
@@ -249,7 +251,7 @@
         def _(i):
             f(pl.ds(pl.multiple_of(i * R, R), R))
 
-    for c in loads_v + loads_o:
+    for c in ins[:2] + loads_v + loads_o:
         c.wait()
     vf[...] = vecs[...].astype(f32)
     a[...] = jnp.dot(ctx[...], matrix(wo[...]), preferred_element_type=f32)
@@ -263,7 +265,7 @@
         low1[sl, :] = out.astype(bf)
 
     each(first)
-    for c in loads_u + loads_d:
+    for c in loads_u:
         c.wait()
 
     def up(j, _):
@@ -276,6 +278,8 @@
         return 0
 
     lax.fori_loop(0, 4, up, 0)
+    for c in loads_d:
+        c.wait()
 
     def down(j, _):
         a[...] += jnp.dot(act[j], matrix(wdn[pl.ds(96 * j, 96)]), preferred_element_type=f32)
@@ -295,7 +299,9 @@
         a[sl, :] = back
         hat2[sl, :] = back.astype(bf)
 
+    ins[2].wait()
     each(second)
+    outs[0].start()
     down_back = hat2
 
     def back(j, _):
@@ -325,7 +331,9 @@
         hat2[sl, :] = back.astype(bf)
 
     each(third)
+    outs[1].start()
     gctx_out[...] = lax.dot_general(hat2[...], matrix(wo[...]), NT, preferred_element_type=f32).astype(bf)
+    outs[2].start()
     dwo[...] = lax.dot_general(ctx[...], hat2[...], TN, preferred_element_type=f32).astype(bf).reshape(96, 8, D)
     for i, held in enumerate(((2, 3, 4), (8, 9, 10, 11), (5, 6, 7))):
         lines = [jnp.sum(sums[s], axis=0, keepdims=True) for s in held]
@@ -337,7 +345,7 @@
     last += [pltpu.make_async_copy(vgrads.at[min(i, 3)], grads.at[vector_at(ch)], ssem.at[20 + i]) for i, ch in enumerate([5, 10, 15] + quiet)]
     for c in last:
         c.start()
-    for c in stores + last:
+    for c in stores + last + outs:
         c.wait()
 
 
@@ -349,9 +357,11 @@
     return pl.pallas_call(
         middle_kernel,
         out_shape=[S((rows, D), bf), S((rows, D), f32), S((rows, D), bf), S((16 * CHIP, 8, D), bf)],
-        in_specs=[any_, vm, vm, vm],
-        out_specs=[vm, vm, vm, any_],
+        in_specs=[any_] * 4,
+        out_specs=[any_] * 4,
         scratch_shapes=[
+            pltpu.VMEM((rows, D), bf), pltpu.VMEM((rows, D), f32), pltpu.VMEM((rows, D), bf),
+            pltpu.VMEM((rows, D), bf), pltpu.VMEM((rows, D), f32), pltpu.VMEM((rows, D), bf), pltpu.SemaphoreType.DMA((6,)),
             pltpu.VMEM((96, 8, D), bf), pltpu.VMEM((384, 8, D), bf), pltpu.VMEM((384, 8, D), bf), pltpu.VMEM((3, 8, D), bf), pltpu.VMEM((3, 8, D), f32),
             pltpu.VMEM((4, rows, D), bf), pltpu.VMEM((4, rows, D), f32), pltpu.VMEM((rows, D), bf),
             pltpu.VMEM((rows, D), f32), pltpu.VMEM((rows, 1), f32), pltpu.VMEM((rows, D), bf), pltpu.VMEM((rows, D), bf),

time: 226 us -> 225 us (level)
  no operation moved by 1% of the time
where the time goes in v7:
time: 225 us
  Pallas kernels  215 us (96%)
  local copies, waits for them, and re-layouts  9.21 us (4%)
    pallas_call x1, Pallas kernels, backward_and_step(): pl.pallas_call(backward_kernel, out_shape=[S((rows, D), f32), S(grads.sha...  97.9 us
    pallas_call x1, Pallas kernels, gather_and_attend(): pl.pallas_call(forward_kernel, out_shape=[S((16, CHIP, 8, D), bf), S((row...  84.8 us
    pallas_call x1, Pallas kernels, middle(): pl.pallas_call(middle_kernel, out_shape=[S((rows, D), bf), S((rows, D), f...  32.1 us
    unnamed x14, local copies, waits for them, and re-layouts  5.73 us

profile of v7, /device:TPU:0, one launch (start us, length us, event | category | flops | bytes accessed | tf_op | source)
XLA Modules:
  0.0 224.7 jit_solution(10904428818550510342)
XLA Ops:
  0.6 2.1 pad_bitcast_fusion.2.x_ref.m_ref
  2.8 84.8 %gather_and_attend.1 = (bf16[16,74,8,768]{3,2,1,0:T(8,128)(2,1)}, f32[512,768]{1,0:T(8,128)}, bf16[512,768]{1,0:T(8,128)(2,1)}, bf16[512,768]{1,0:T(8,128)(2,1)}...) custom-call(f32[1760,128]{1,0:T(8,128)} %pad_bitcast_fusion.2.x_ref., ...), custom_call_target="tpu_custom_call" | custom-call | tf_op jit(solution)/shard_map/gather_and_attend/pallas_call | solution.py:1008
  87.6 0.0 copy-start
  87.6 0.0 copy-start.1
  87.6 32.1 %middle.1 = (bf16[512,768]{1,0:T(8,128)(2,1)}, f32[512,768]{1,0:T(8,128)}, bf16[512,768]{1,0:T(8,128)(2,1)}, bf16[1184,8,768]{2,1,0:T(8,128)(2,1)}) custom-call(bf16[1184,8,768]{2,1,0:T(8,128)(2,1)} %bitcast.18, bf16[512,768]{1,0:T(8,128)(2,1)} %get-tuple-element.24.ctx_in, f32[512,768]{1,0:T(8,128)} %get-tuple-element.25.hidden_in, bf16[512,768]{1,0:T(8,128)(2,1)} %bitcast.25), custom_call_target="tpu_custom_call" | custom-call | tf_op jit(solution)/shard_map/middle/pallas_call | solution.py:357
  119.7 0.0 copy-done
  119.7 0.0 copy-done.1
  119.7 1.3 pad_bitcast_fusion
  121.1 97.9 %backward_and_step.1 = (f32[512,768]{1,0:T(8,128)}, bf16[1184,8,768]{2,1,0:T(8,128)(2,1)}, f32[1760,128]{1,0:T(8,128)}, f32[1760,128]{1,0:T(8,128)}, f32[1760,12...) custom-call(bf16[1184,8,768]{2,1,0:T(8,128)(2,1)} %bitcast.19, ...), custom_call_target="tpu_custom_call", output_to_operand_aliasing={{1}: (10, {})} | custom-call | tf_op jit(solution)/shard_map/backward_and_step/pallas_call | solution.py:1685
  219.0 0.0 copy-start.4
  219.0 0.0 copy-start.3
  219.0 2.8 %copy.20 = f32[1,512,768]{2,1,0:T(8,128)} copy(f32[1,512,768]{2,1,0:T(8,128)} %bitcast.21) | data formatting | bytes 3145728
  221.8 0.0 copy-done.4
  221.8 0.0 copy-start.2
  221.8 1.0 copy.21
  222.8 0.0 copy-done.3
  222.8 1.0 copy.22
  223.7 0.0 copy-done.2
  223.8 1.0 copy.23
Async XLA Ops:
  87.6 32.1 %copy-start = (f32[224580]{0:T(1024)S(1)}, f32[224580]{0:T(1024)}, u32[]{:S(2)}) copy-start(f32[224580]{0:T(1024)} %param.17) | copy-start | bytes 2694964
  87.6 32.1 %copy-start.1 = (f32[224580]{0:T(1024)S(1)}, f32[224580]{0:T(1024)}, u32[]{:S(2)}) copy-start(f32[224580]{0:T(1024)} %param.16) | copy-start | bytes 2694964
  219.0 2.8 %copy-start.4 = (f32[1760,128]{1,0:T(8,128)S(1)}, f32[1760,128]{1,0:T(8,128)}, u32[]{:S(2)}) copy-start(f32[1760,128]{1,0:T(8,128)} %get-tuple-element.38) | copy-start | bytes 2703364
  219.0 3.8 %copy-start.3 = (f32[1760,128]{1,0:T(8,128)S(1)}, f32[1760,128]{1,0:T(8,128)}, u32[]{:S(2)}) copy-start(f32[1760,128]{1,0:T(8,128)} %get-tuple-element.39) | copy-start | bytes 2703364
  221.8 2.0 copy-start.2

commit v8 on v7

--- a/solution.py
+++ b/solution.py
@@ -436,9 +436,8 @@
     s_scr[...] = s
     top = jnp.max(jnp.max(s.reshape(keys // 8, 8, rows), axis=0), axis=0, keepdims=True)
     e = jnp.exp(s_scr[...] - top)
-    s_scr[...] = e
     inverse = 1.0 / jnp.sum(jnp.sum(e.reshape(keys // 8, 8, rows), axis=0), axis=0, keepdims=True)
-    p_ref[...] = (s_scr[...] * inverse).astype(bf)
+    p_ref[...] = (jnp.exp(s_scr[...] - top) * inverse).astype(bf)
 
 
 def context_pair(v, p_ref):

time: 225 us -> 225 us (level)
  no operation moved by 1% of the time
where the time goes in v8:
time: 225 us
  Pallas kernels  215 us (96%)
  local copies, waits for them, and re-layouts  9.21 us (4%)
    pallas_call x1, Pallas kernels, backward_and_step(): pl.pallas_call(backward_kernel, out_shape=[S((rows, D), f32), S(grads.sha...  97.9 us
    pallas_call x1, Pallas kernels, gather_and_attend(): pl.pallas_call(forward_kernel, out_shape=[S((16, CHIP, 8, D), bf), S((row...  84.8 us
    pallas_call x1, Pallas kernels, middle(): pl.pallas_call(middle_kernel, out_shape=[S((rows, D), bf), S((rows, D), f...  32.1 us
    unnamed x14, local copies, waits for them, and re-layouts  5.73 us

profile of v8, /device:TPU:0, one launch (start us, length us, event | category | flops | bytes accessed | tf_op | source)
XLA Modules:
  0.0 224.7 jit_solution(10904428818550510342)
XLA Ops:
  0.6 2.1 pad_bitcast_fusion.2.x_ref.m_ref
  2.8 84.8 %gather_and_attend.1 = (bf16[16,74,8,768]{3,2,1,0:T(8,128)(2,1)}, f32[512,768]{1,0:T(8,128)}, bf16[512,768]{1,0:T(8,128)(2,1)}, bf16[512,768]{1,0:T(8,128)(2,1)}...) custom-call(f32[1760,128]{1,0:T(8,128)} %pad_bitcast_fusion.2.x_ref., ...), custom_call_target="tpu_custom_call" | custom-call | tf_op jit(solution)/shard_map/gather_and_attend/pallas_call | solution.py:1007
  87.6 0.0 copy-start
  87.6 0.0 copy-start.1
  87.6 32.1 %middle.1 = (bf16[512,768]{1,0:T(8,128)(2,1)}, f32[512,768]{1,0:T(8,128)}, bf16[512,768]{1,0:T(8,128)(2,1)}, bf16[1184,8,768]{2,1,0:T(8,128)(2,1)}) custom-call(bf16[1184,8,768]{2,1,0:T(8,128)(2,1)} %bitcast.18, bf16[512,768]{1,0:T(8,128)(2,1)} %get-tuple-element.24.ctx_in, f32[512,768]{1,0:T(8,128)} %get-tuple-element.25.hidden_in, bf16[512,768]{1,0:T(8,128)(2,1)} %bitcast.25), custom_call_target="tpu_custom_call" | custom-call | tf_op jit(solution)/shard_map/middle/pallas_call | solution.py:357
  119.7 0.0 copy-done
  119.7 0.0 copy-done.1
  119.7 1.3 pad_bitcast_fusion
  121.1 97.9 %backward_and_step.1 = (f32[512,768]{1,0:T(8,128)}, bf16[1184,8,768]{2,1,0:T(8,128)(2,1)}, f32[1760,128]{1,0:T(8,128)}, f32[1760,128]{1,0:T(8,128)}, f32[1760,12...) custom-call(bf16[1184,8,768]{2,1,0:T(8,128)(2,1)} %bitcast.19, ...), custom_call_target="tpu_custom_call", output_to_operand_aliasing={{1}: (10, {})} | custom-call | tf_op jit(solution)/shard_map/backward_and_step/pallas_call | solution.py:1684
  219.0 0.0 copy-start.4
  219.0 0.0 copy-start.3
  219.0 2.8 %copy.20 = f32[1,512,768]{2,1,0:T(8,128)} copy(f32[1,512,768]{2,1,0:T(8,128)} %bitcast.21) | data formatting | bytes 3145728
  221.8 0.0 copy-done.4
  221.8 0.0 copy-start.2
  221.8 1.0 copy.21
  222.8 0.0 copy-done.3
  222.8 1.0 copy.22
  223.7 0.0 copy-done.2
  223.8 1.0 copy.23
Async XLA Ops:
  87.6 32.1 %copy-start = (f32[224580]{0:T(1024)S(1)}, f32[224580]{0:T(1024)}, u32[]{:S(2)}) copy-start(f32[224580]{0:T(1024)} %param.17) | copy-start | bytes 2694964
  87.6 32.1 %copy-start.1 = (f32[224580]{0:T(1024)S(1)}, f32[224580]{0:T(1024)}, u32[]{:S(2)}) copy-start(f32[224580]{0:T(1024)} %param.16) | copy-start | bytes 2694964
  219.0 2.8 %copy-start.4 = (f32[1760,128]{1,0:T(8,128)S(1)}, f32[1760,128]{1,0:T(8,128)}, u32[]{:S(2)}) copy-start(f32[1760,128]{1,0:T(8,128)} %get-tuple-element.38) | copy-start | bytes 2703364
  219.0 3.8 %copy-start.3 = (f32[1760,128]{1,0:T(8,128)S(1)}, f32[1760,128]{1,0:T(8,128)}, u32[]{:S(2)}) copy-start(f32[1760,128]{1,0:T(8,128)} %get-tuple-element.39) | copy-start | bytes 2703364
  221.8 2.0 copy-start.2
